TPU v7x, 256 devices: a whole 4x4x8 slice. The times are simulated.
256 devices in a mesh: ax: 8 (over x, y_lo), az: 32 (over z, y_hi, core).
Axes of the slice: x: 4, y: 4 (y_hi: 2, y_lo: 2; y = y_hi * 2 + y_lo), z: 8, core: 2. Of those that a mesh axis runs over, the one named last changes fastest.
Arguments:
- flow_state: float32 [5, 32, 1024, 256], P(None, 'ax', 'az'), may hold values from -6 to 6
- radial_coef: float32 [32, 1024, 256], P('ax', 'az'), may hold values from 50 to 2000
- blanking: int32 [32, 1024, 256], P('ax', 'az'), may hold values from 0 to 1, as said below
- canard_index: int32 [32, 1024], P('ax', 'az'), may hold values from 0 to 127
- canard_table: float32 [8, 128, 5, 256], P('ax', 'az'), may hold values from -6 to 6
- coupling: float32 [5, 5], replicated, may hold values from -0.15 to 0.15
- upwind_split: float32 [5], replicated, may hold values from 0.05 to 0.95
Outputs:
- update: float32 [5, 32, 1024, 256], P(None, 'ax', 'az')
Inputs may be any that keep to these rules, and one draw needn't show every extreme that they name: `blanking`: 0 marks a blanked cell.
All inputs are finite; a program needn't handle non-finite values.
Results may differ from a plain program's by a relative error of at most 0.0001.
Values sent between devices are 32-bit elements; how exact they have to be, the bound alone decides.
No kernel may reach another device: no remote copies, remote signals or barrier semaphores. Data moves between devices by JAX's collectives and lax.ppermute only.
A program may use at most 128 MiB of HBM per device.

v0:
```python
import jax
import jax.numpy as jnp
from jax import lax
from jax.experimental import pallas as pl
from jax.experimental.pallas import tpu as pltpu
from jax.sharding import PartitionSpec as P

N = 5
NN = 25
SEG = 8
LANES = 128
HALF = 16
VMEM_LIMIT = 20 * 1024 * 1024
F32 = jnp.float32
STEPS = [(s * (2 * i + 1), s) for s in (1, 2, 4, 8) for i in range(8 // s)]


def up(x, s):
    return pltpu.roll(x, SEG - s, 0)


def down(x, s):
    return pltpu.roll(x, s, 0)


def splat_consts(coupling_ref, upwind_ref):
    shape = (SEG, LANES)
    p = [[jnp.full(shape, coupling_ref[i, j], F32) for j in range(N)] for i in range(N)]
    w = [jnp.full(shape, upwind_ref[0, i], F32) for i in range(N)]
    a = [[p[i][j] + w[i] if i == j else p[i][j] for j in range(N)] for i in range(N)]
    b = [[(1.0 - w[i]) - p[j][i] if i == j else -p[j][i] for j in range(N)] for i in range(N)]
    return a, b


def dot_row(row, cols, j):
    acc = row[0] * cols[0][j]
    for k in range(1, N):
        acc = acc + row[k] * cols[k][j]
    return acc


def mat_mul(x, y):
    return [[dot_row(x[i], y, j) for j in range(N)] for i in range(N)]


def mat_vec(x, v):
    out = []
    for i in range(N):
        acc = x[i][0] * v[0]
        for k in range(1, N):
            acc = acc + x[i][k] * v[k]
        out.append(acc)
    return out


def invert(matrix):
    m = [list(row) for row in matrix]
    for p in range(N):
        piv = 1.0 / m[p][p]
        m[p] = [piv if j == p else m[p][j] * piv for j in range(N)]
        for i in range(N):
            if i != p:
                f = m[i][p]
                m[i] = [-(f * piv) if j == p else m[i][j] - f * m[p][j] for j in range(N)]
    return m


def load_mat(ref, slot, base):
    return [[ref[slot, base + i * N + j] for j in range(N)] for i in range(N)]


def load_row(ref, slot, base, i):
    return [ref[slot, base + i * N + j] for j in range(N)]


def store_mat(ref, slot, base, mat):
    for i in range(N):
        for j in range(N):
            ref[slot, base + i * N + j] = mat[i][j]


def strided(ref, k):
    return ref[pl.ds(k, SEG, stride=2 * HALF), :]


def slot_of(p):
    return p + 2


D0, OUT0, IN0 = 0, NN, 2 * NN
LO0, LI0 = 0, NN


def factor_kernel(coef_ref, blank_ref, coup_ref, upw_ref, mb, mf, scal, sd, lam_t, mask_t, face, pw):
    mask = blank_ref[...].astype(F32).reshape(LANES, 2 * HALF * SEG)
    lam = coef_ref[...].reshape(LANES, 2 * HALF * SEG) * mask
    lam_t[...] = lam.T
    mask_t[...] = mask.T
    a, b = splat_consts(coup_ref, upw_ref)
    for which, mat in enumerate((mat_mul(a, a), mat_mul(b, b), mat_mul(a, b), mat_mul(b, a))):
        store_mat(pw, which, 0, mat)

    sub = lax.broadcasted_iota(jnp.int32, (SEG, LANES), 0)
    first_lam, first_mask = strided(lam_t, 0), strided(mask_t, 0)
    lam_k, mask_k = first_lam, first_mask
    for k in range(2 * HALF):
        if k < 2 * HALF - 1:
            lam_n, mask_n = strided(lam_t, k + 1), strided(mask_t, k + 1)
            f = 0.5 * (lam_k * mask_n + lam_n * mask_k)
        else:
            lam_n, mask_n = up(first_lam, 1), up(first_mask, 1)
            f = jnp.where(sub == SEG - 1, 0.0, 0.5 * (lam_k * mask_n + lam_n * mask_k))
        face[k + 1] = f
        lam_k, mask_k = lam_n, mask_n
    face[0] = down(face[2 * HALF], 1)

    def build_odd(m, c):
        fl, fr = face[2 * m + 1], face[2 * m + 2]
        scal[m, 0] = 1.0 / (1.0 + 0.5 * (fl + fr))
        scal[m, 1] = fl
        scal[m, 2] = fr
        return c

    lax.fori_loop(0, HALF, build_odd, 0)

    def build_even(p, c):
        prev = jnp.where(p == 0, HALF - 1, p - 1)
        inv, fl, fr = scal[p, 0], scal[p, 1], scal[p, 2]
        inv_p, fl_p, fr_p = scal[prev, 0], scal[prev, 1], scal[prev, 2]
        beta = fr_p * fr_p * inv_p
        delta = fr_p * fl_p * inv_p
        beta = jnp.where(p == 0, down(beta, 1), beta)
        alpha = fl * fl * inv
        gamma = fl * fr * inv
        d = 1.0 + 0.5 * (face[2 * p] + face[2 * p + 1])
        for i in range(N):
            for j in range(N):
                e = i * N + j
                val = -(alpha * pw[2, e] + beta * pw[3, e])
                mb[slot_of(p), D0 + e] = d + val if i == j else val
                mb[slot_of(p), OUT0 + e] = gamma * pw[0, e]
                mb[slot_of(p), IN0 + e] = delta * pw[1, e]
        return c

    lax.fori_loop(0, HALF, build_even, 0)
    last = scal[HALF - 1, 1] * scal[HALF - 1, 2] * scal[HALF - 1, 0]
    for e in range(NN):
        mb[slot_of(HALF), D0 + e] = jnp.zeros((SEG, LANES), F32)
        mb[slot_of(HALF), OUT0 + e] = jnp.zeros((SEG, LANES), F32)
        mb[slot_of(HALF), IN0 + e] = last * pw[1, e]

    def eliminate(it, c):
        s = jnp.where(it < 8, 1, jnp.where(it < 12, 2, jnp.where(it < 14, 4, 8)))
        first = jnp.where(it < 8, 0, jnp.where(it < 12, 8, jnp.where(it < 14, 12, 14)))
        m = s * (2 * (it - first) + 1)
        sm, sp, sq = slot_of(m), slot_of(m - s), slot_of(m + s)
        di = invert(load_mat(mb, sm, D0))
        store_mat(mb, sm, D0, di)
        for i in range(N):
            row = load_row(mb, sp, OUT0, i)
            for j in range(N):
                mf[sm, LO0 + i * N + j] = dot_row(row, di, j)
            row = load_row(mb, sq, IN0, i)
            for j in range(N):
                mf[sm, LI0 + i * N + j] = dot_row(row, di, j)
        in_m = load_mat(mb, sm, IN0)
        for i in range(N):
            row = load_row(mf, sm, LO0, i)
            for j in range(N):
                e = i * N + j
                mb[sp, D0 + e] = mb[sp, D0 + e] - dot_row(row, in_m, j)
            row = load_row(mf, sm, LI0, i)
            for j in range(N):
                mb[sq, IN0 + i * N + j] = dot_row(row, in_m, j)
        out_m = load_mat(mb, sm, OUT0)
        for i in range(N):
            row = load_row(mf, sm, LI0, i)
            for j in range(N):
                e = i * N + j
                mb[sq, D0 + e] = mb[sq, D0 + e] - dot_row(row, out_m, j)
            row = load_row(mf, sm, LO0, i)
            for j in range(N):
                mb[sp, OUT0 + i * N + j] = dot_row(row, out_m, j)
        return c

    lax.fori_loop(0, len(STEPS), eliminate, 0)

    s0, s16 = slot_of(0), slot_of(HALF)
    for e in range(NN):
        mb[0, D0 + e] = mb[s0, D0 + e] + down(mb[s16, D0 + e], 1)
        mb[0, OUT0 + e] = mb[s0, OUT0 + e]
        mb[0, IN0 + e] = down(mb[s16, IN0 + e], 1)
    for level, s in enumerate((1, 2, 4)):
        d = load_mat(mb, level, D0)
        di = invert(d)
        store_mat(mb, level, D0, di)
        di_up = [[up(di[i][j], s) for j in range(N)] for i in range(N)]
        for i in range(N):
            row = load_row(mb, level, OUT0, i)
            for j in range(N):
                mf[level, LO0 + i * N + j] = dot_row(row, di_up, j)
        di_down = [[down(di[i][j], s) for j in range(N)] for i in range(N)]
        for i in range(N):
            row = load_row(mb, level, IN0, i)
            for j in range(N):
                mf[level, LI0 + i * N + j] = dot_row(row, di_down, j)
        in_up = [[up(mb[level, IN0 + i * N + j], s) for j in range(N)] for i in range(N)]
        acc = []
        for i in range(N):
            row = load_row(mf, level, LO0, i)
            acc.append([d[i][j] - dot_row(row, in_up, j) for j in range(N)])
        out_down = [[down(mb[level, OUT0 + i * N + j], s) for j in range(N)] for i in range(N)]
        for i in range(N):
            row = load_row(mf, level, LI0, i)
            for j in range(N):
                val = acc[i][j] - dot_row(row, out_down, j)
                if level < 2:
                    mb[level + 1, D0 + i * N + j] = val
                else:
                    sd[pl.ds(i * N + j, 1), :] = val[0:1]
        if level < 2:
            out_up = [[up(mb[level, OUT0 + i * N + j], s) for j in range(N)] for i in range(N)]
            for i in range(N):
                row = load_row(mf, level, LO0, i)
                for j in range(N):
                    mb[level + 1, OUT0 + i * N + j] = dot_row(row, out_up, j)
            in_down = [[down(mb[level, IN0 + i * N + j], s) for j in range(N)] for i in range(N)]
            for i in range(N):
                row = load_row(mf, level, LI0, i)
                for j in range(N):
                    mb[level + 1, IN0 + i * N + j] = dot_row(row, in_down, j)
    sd[pl.ds(NN, 1), :] = first_lam[0:1]
    sd[pl.ds(NN + 1, 1), :] = first_mask[0:1]
    sd[pl.ds(NN + 2, 5), :] = jnp.zeros((5, LANES), F32)


def join_kernel(own_ref, other_ref, j_ref):
    lam, mask = own_ref[pl.ds(NN, 1), :], own_ref[pl.ds(NN + 1, 1), :]
    other_lam, other_mask = other_ref[pl.ds(NN, 1), :], other_ref[pl.ds(NN + 1, 1), :]
    c = 0.25 * (lam * other_mask + other_lam * mask)

    def total(ref):
        mat = [[ref[pl.ds(i * N + j, 1), :] for j in range(N)] for i in range(N)]
        return [[mat[i][j] + c if i == j else mat[i][j] for j in range(N)] for i in range(N)]

    own, inv_other = total(own_ref), invert(total(other_ref))
    schur = [[own[i][j] - c * (c * inv_other[i][j]) for j in range(N)] for i in range(N)]
    j1 = invert(schur)
    j2 = mat_mul(j1, inv_other)
    for i in range(N):
        for j in range(N):
            j_ref[pl.ds(i * N + j, 1), :] = j1[i][j]
            j_ref[pl.ds(NN + i * N + j, 1), :] = c * j2[i][j]


def stencil_block(u, v, z, planes, zprev, znext, tprev, tnext):
    cur = u[v, z]
    rows = lax.broadcasted_iota(jnp.int32, cur.shape, 0)
    behind = u[v, z - 1] if z > 0 else zprev[v]
    ahead = u[v, z + 1] if z < planes - 1 else znext[v]
    sectors = cur.shape[0]
    before_t = jnp.where(rows == 0, tprev[v, pl.ds(z, 1), :], pltpu.roll(cur, 1, 0))
    after_t = jnp.where(rows == sectors - 1, tnext[v, pl.ds(z, 1), :], pltpu.roll(cur, sectors - 1, 0))
    return behind + ahead + before_t + after_t - 4.0 * cur + 0.5 * (behind - ahead)


def forward_body(rhs_t, mf, scal, coup_ref, upw_ref, e_ref, o_ref, y_ref):
    a, b = splat_consts(coup_ref, upw_ref)
    zero = jnp.zeros((SEG, LANES), F32)
    carry = [zero] * N
    first = None
    for m in range(HALF):
        inv, fl, fr = scal[m, 0], scal[m, 1], scal[m, 2]
        odd = [strided(rhs_t.at[v], 2 * m + 1) for v in range(N)]
        scaled = [x * inv for x in odd]
        ta = mat_vec(a, scaled)
        tb = mat_vec(b, scaled)
        for v in range(N):
            o_ref[m, v] = odd[v]
            e_ref[slot_of(m), v] = strided(rhs_t.at[v], 2 * m) + carry[v] + fl * ta[v]
        carry = [fr * tb[v] for v in range(N)]
    for v in range(N):
        e_ref[slot_of(0), v] = e_ref[slot_of(0), v] + down(carry[v], 1)
        e_ref[slot_of(HALF), v] = zero
    for m, s in STEPS:
        vec = [e_ref[slot_of(m), v] for v in range(N)]
        lo = mat_vec(load_mat(mf, slot_of(m), LO0), vec)
        li = mat_vec(load_mat(mf, slot_of(m), LI0), vec)
        for v in range(N):
            e_ref[slot_of(m - s), v] = e_ref[slot_of(m - s), v] + lo[v]
            e_ref[slot_of(m + s), v] = e_ref[slot_of(m + s), v] + li[v]
    cur = [e_ref[slot_of(0), v] + down(e_ref[slot_of(HALF), v], 1) for v in range(N)]
    for level, s in enumerate((1, 2, 4)):
        for v in range(N):
            e_ref[level, v] = cur[v]
        lo = mat_vec(load_mat(mf, level, LO0), [up(x, s) for x in cur])
        li = mat_vec(load_mat(mf, level, LI0), [down(x, s) for x in cur])
        cur = [cur[v] + lo[v] + li[v] for v in range(N)]
    for v in range(N):
        y_ref[pl.ds(v, 1), :] = cur[v][0:1]
    y_ref[pl.ds(N, 3), :] = jnp.zeros((3, LANES), F32)


def forward_first_kernel(
    u, zprev, znext, tprev, tnext, blank, idx, table, mf, scal, coup, upw, e_ref, o_ref, y_ref, rhs_t
):
    planes, sectors, radial = blank.shape
    mask = blank[...].astype(F32).reshape(planes * sectors, radial)
    rows = lax.broadcasted_iota(jnp.int32, (table.shape[0], LANES), 0)
    onehot = (rows == idx[...]).astype(F32).T
    for v in range(N):
        force = jnp.dot(
            onehot,
            table[:, pl.ds(v * radial, radial)],
            precision=lax.Precision.HIGHEST,
            preferred_element_type=F32,
        )
        blocks = [stencil_block(u, v, z, planes, zprev, znext, tprev, tnext) for z in range(planes)]
        rhs = mask * (jnp.concatenate(blocks, axis=0) + force)
        rhs_t[v] = rhs.T
    forward_body(rhs_t, mf, scal, coup, upw, e_ref, o_ref, y_ref)


def forward_second_kernel(
    u, zprev, znext, tprev, tnext, blank, mf, scal, coup, upw, e_ref, o_ref, y_ref, rhs_t
):
    planes, sectors, radial = blank.shape
    mask = blank[...].astype(F32).reshape(planes * sectors, radial)
    for v in range(N):
        blocks = [stencil_block(u, v, z, planes, zprev, znext, tprev, tnext) for z in range(planes)]
        rhs_t[v] = (mask * jnp.concatenate(blocks, axis=0)).T
    forward_body(rhs_t, mf, scal, coup, upw, e_ref, o_ref, y_ref)


def backward_body(y_own, y_other, j_ref, mb, scal, coup_ref, upw_ref, e_ref, o_ref, x_ref, x_t):
    a, b = splat_consts(coup_ref, upw_ref)
    sub = lax.broadcasted_iota(jnp.int32, (SEG, LANES), 0)
    own = [y_own[pl.ds(v, 1), :] for v in range(N)]
    other = [y_other[pl.ds(v, 1), :] for v in range(N)]
    cur = []
    for i in range(N):
        acc = j_ref[pl.ds(i * N, 1), :] * own[0]
        for k in range(N):
            if k > 0:
                acc = acc + j_ref[pl.ds(i * N + k, 1), :] * own[k]
            acc = acc + j_ref[pl.ds(NN + i * N + k, 1), :] * other[k]
        cur.append(jnp.broadcast_to(acc, (SEG, LANES)))

    def recover(slot, high, low):
        o = mat_vec(load_mat(mb, slot, OUT0), high)
        i = mat_vec(load_mat(mb, slot, IN0), low)
        total = [e_ref[slot, v] + o[v] + i[v] for v in range(N)]
        return mat_vec(load_mat(mb, slot, D0), total)

    for level, s in ((2, 4), (1, 2), (0, 1)):
        new = recover(level, [up(x, s) for x in cur], [down(x, s) for x in cur])
        cur = [jnp.where(sub % (2 * s) == s, new[v], cur[v]) for v in range(N)]
    for v in range(N):
        x_ref[0, v] = cur[v]
        x_ref[HALF, v] = up(cur[v], 1)
    for m, s in reversed(STEPS):
        new = recover(
            slot_of(m), [x_ref[m + s, v] for v in range(N)], [x_ref[m - s, v] for v in range(N)]
        )
        for v in range(N):
            x_ref[m, v] = new[v]
    low = [x_ref[0, v] for v in range(N)]
    for m in range(HALF):
        inv, fl, fr = scal[m, 0], scal[m, 1], scal[m, 2]
        high = [x_ref[m + 1, v] for v in range(N)]
        ta = mat_vec(a, high)
        tb = mat_vec(b, low)
        for v in range(N):
            odd = inv * (o_ref[m, v] + fr * ta[v] + fl * tb[v])
            x_t.at[v][pl.ds(2 * m, SEG, stride=2 * HALF), :] = low[v]
            x_t.at[v][pl.ds(2 * m + 1, SEG, stride=2 * HALF), :] = odd
        low = high


def backward_first_kernel(
    y_own, y_other, j_ref, mb, scal, coup, upw, e_ref, o_ref,
    out, zfirst, zlast, tfirst, tlast, x_ref, x_t,
):
    backward_body(y_own, y_other, j_ref, mb, scal, coup, upw, e_ref, o_ref, x_ref, x_t)
    _, planes, sectors, radial = out.shape
    for v in range(N):
        field = x_t[v].T.reshape(planes, sectors, radial)
        out[v] = field
        zfirst[v] = field[0]
        zlast[v] = field[planes - 1]
        for z in range(planes):
            tfirst[v, pl.ds(z, 1), :] = field[z, 0:1]
            tlast[v, pl.ds(z, 1), :] = field[z, sectors - 1 : sectors]


def backward_second_kernel(
    y_own, y_other, j_ref, mb, scal, coup, upw, e_ref, o_ref, first, out, x_ref, x_t
):
    backward_body(y_own, y_other, j_ref, mb, scal, coup, upw, e_ref, o_ref, x_ref, x_t)
    _, planes, sectors, radial = out.shape
    for v in range(N):
        out[v] = first[v] + 0.5 * x_t[v].T.reshape(planes, sectors, radial)


def call(kernel, inputs, outs, scratch, flops, smem=()):
    vmem = pl.BlockSpec(memory_space=pltpu.VMEM)
    in_specs = [pl.BlockSpec(memory_space=pltpu.SMEM) if i in smem else vmem for i in range(len(inputs))]
    out_shape = [jax.ShapeDtypeStruct(s, F32) for s in outs]
    moved = sum(x.size for x in inputs) * 4 + sum(s.size for s in out_shape) * 4
    return pl.pallas_call(
        kernel,
        out_shape=out_shape,
        in_specs=in_specs,
        out_specs=[vmem] * len(outs),
        scratch_shapes=[pltpu.VMEM(s, F32) for s in scratch],
        compiler_params=pltpu.CompilerParams(vmem_limit_bytes=VMEM_LIMIT),
        cost_estimate=pl.CostEstimate(flops=flops, bytes_accessed=moved, transcendentals=0),
    )(*inputs)


def shifted(x, axis, step, wrap):
    size = lax.axis_size(axis)
    pairs = [(i, (i + step) % size) for i in range(size) if wrap or 0 <= i + step < size]
    return lax.ppermute(x, axis, pairs)


def halos(zfirst, zlast, tfirst, tlast):
    return (
        shifted(zlast, "ax", 1, False),
        shifted(zfirst, "ax", -1, False),
        shifted(tlast, "az", 1, True),
        shifted(tfirst, "az", -1, True),
    )


def per_device(
    flow_state, radial_coef, blanking, canard_index, canard_table, coupling, upwind_split
):
    comps, planes, sectors, radial = flow_state.shape
    tile = (SEG, LANES)
    upw = upwind_split.reshape(1, N)
    local_rows = canard_table.shape[1]
    half_turn = lax.axis_size("az") // 2

    first_halos = halos(
        flow_state[:, 0], flow_state[:, planes - 1], flow_state[:, :, 0], flow_state[:, :, sectors - 1]
    )
    table = lax.all_gather(
        canard_table.reshape(local_rows, comps * radial), "az", axis=0, tiled=True
    )
    idx = canard_index.reshape(1, planes * sectors)

    field = (comps, planes, sectors, radial)
    mb, mf, scal, sd = call(
        factor_kernel,
        (radial_coef, blanking, coupling, upw),
        [(HALF + 3, 3 * NN) + tile, (HALF + 2, 2 * NN) + tile, (HALF, 3) + tile, (32, LANES)],
        [(radial, LANES), (radial, LANES), (2 * HALF + 1,) + tile, (4, NN) + tile],
        32_000_000,
        (2, 3),
    )
    other_sd = shifted(sd, "az", half_turn, True)
    fwd_outs = [(HALF + 3, N) + tile, (HALF, N) + tile, tile]
    rhs_scratch = [(N, radial, LANES)]
    back_scratch = [(HALF + 1, N) + tile, (N, radial, LANES)]

    e1, o1, y1 = call(
        forward_first_kernel,
        (flow_state, *first_halos, blanking, idx, table, mf, scal, coupling, upw),
        fwd_outs,
        rhs_scratch,
        4_000_000,
        (10, 11),
    )
    other_y1 = shifted(y1, "az", half_turn, True)
    (joint,) = call(join_kernel, (sd, other_sd), [(2 * NN, LANES)], [], 200_000)
    first, *edges = call(
        backward_first_kernel,
        (y1, other_y1, joint, mb, scal, coupling, upw, e1, o1),
        [field, (comps, sectors, radial), (comps, sectors, radial), (comps, planes, radial), (comps, planes, radial)],
        back_scratch,
        4_000_000,
        (5, 6),
    )
    second_halos = halos(*edges)
    e2, o2, y2 = call(
        forward_second_kernel,
        (first, *second_halos, blanking, mf, scal, coupling, upw),
        fwd_outs,
        rhs_scratch,
        4_000_000,
        (8, 9),
    )
    other_y2 = shifted(y2, "az", half_turn, True)
    (update,) = call(
        backward_second_kernel,
        (y2, other_y2, joint, mb, scal, coupling, upw, e2, o2, first),
        [field],
        back_scratch,
        4_000_000,
        (5, 6),
    )
    return update


def solution(mesh):
    return jax.shard_map(
        per_device,
        mesh=mesh,
        in_specs=(
            P(None, "ax", "az", None),
            P("ax", "az", None),
            P("ax", "az", None),
            P("ax", "az"),
            P("ax", "az", None, None),
            P(),
            P(),
        ),
        out_specs=P(None, "ax", "az", None),
        check_vma=False,
    )
```

profile of v0, /device:TPU:6, one launch (start us, length us, event | category | flops | bytes accessed | tf_op | source)
XLA Modules:
  0.0 124.5 jit_solution(6769002583511273899)
XLA Ops:
  0.0 1.1 fusion
  1.1 0.1 collective-permute-start.2
  1.2 8.0 %collective-permute-start.3 = (f32[5,4,256]{2,1,0:T(4,128)S(1)}, f32[5,4,256]{2,1,0:T(4,128)S(1)}, u32[]{:S(2)}, u32[]{:S(2)}) collective-permute-start(f32[5,4,256]{2,1,0:T(4,128)S(1)} %bitcast.24), channel_id=1, source_target_pairs={{0,31},{1,0},{2,1},{3,2},{4,3},{5,4},{6,5},{7,6},{8,7},{9,8},{10,9... | collective-permute-start | bytes 61448 | tf_op jit(solution)/shard_map/ppermute | solution.py:424
  9.2 1.0 slice_bitcast_fusion
  10.2 2.9 %collective-permute-start.1 = (f32[5,32,256]{2,1,0:T(8,128)S(1)}, f32[5,32,256]{2,1,0:T(8,128)S(1)}, u32[]{:S(2)}, u32[]{:S(2)}) collective-permute-start(f32[5,32,256]{2,1,0:T(8,128)S(1)} %get-tuple-element.37), channel_id=1, source_target_pairs={{32,0},{64,32},{96,64},{128,96},{160,128},{192,160},{224,192},{33,... | collective-permute-start | bytes 491528 | tf_op jit(solution)/shard_map/ppermute | solution.py:424
  13.1 3.0 %collective-permute-start = (f32[5,32,256]{2,1,0:T(8,128)S(1)}, f32[5,32,256]{2,1,0:T(8,128)S(1)}, u32[]{:S(2)}, u32[]{:S(2)}) collective-permute-start(f32[5,32,256]{2,1,0:T(8,128)S(1)} %get-tuple-element.38), channel_id=1, source_target_pairs={{0,32},{32,64},{64,96},{96,128},{128,160},{160,192},{192,224},{1,3... | collective-permute-start | bytes 491528 | tf_op jit(solution)/shard_map/ppermute | solution.py:424
  16.1 0.0 copy-start.6
  16.1 0.9 copy-done.6
  17.0 0.9 copy-done.9
  17.9 0.7 copy-done.10
  18.6 0.7 copy-done.13
  19.2 6.2 %shard_map.73 = (f32[19,75,8,128]{3,2,1,0:T(8,128)S(1)}, f32[18,50,8,128]{3,2,1,0:T(8,128)S(1)}, f32[16,3,8,128]{3,2,1,0:T(8,128)S(1)}, f32[32,128]{1,0:T(8,128)S(1)}) custom-call(f32[4,32,256]{2,1,0:T(8,128)S(1)} %copy-done.9, s32[4,32,256]{2,1,0:T(8,128)S(1)} %copy-done.6, f32[5,5]{1,0:T(8,128)S(1)} %copy-done.10, f32[1,5]{1,0:T(1,128)S(1)} %bitcast.18), custom_call_target="tpu_custom_call" | custom-call | flops 32000000 | bytes 9998456 | tf_op jit(solution)/shard_map/pallas_call | solution.py:410
  25.5 2.5 %copy-done = f32[19,75,8,128]{3,2,1,0:T(8,128)} copy-done((f32[19,75,8,128]{3,2,1,0:T(8,128)}, f32[19,75,8,128]{3,2,1,0:T(8,128)S(1)}, u32[]{:S(2)}) %copy-start) | copy-done | bytes 5836824
  28.0 1.8 %copy-done.2 = f32[18,50,8,128]{3,2,1,0:T(8,128)} copy-done((f32[18,50,8,128]{3,2,1,0:T(8,128)}, f32[18,50,8,128]{3,2,1,0:T(8,128)S(1)}, u32[]{:S(2)}) %copy-start.2) | copy-done | bytes 3686424
  29.8 4.5 %collective-permute-start.5 = (f32[32,128]{1,0:T(8,128)S(1)}, f32[32,128]{1,0:T(8,128)S(1)}, u32[]{:S(2)}, u32[]{:S(2)}) collective-permute-start(f32[32,128]{1,0:T(8,128)S(1)} %get-tuple-element.23.own_ref), channel_id=1, source_target_pairs={{0,16},{1,17},{2,18},{3,19},{4,20},{5,21},{6,22},{7,23},{8,24},{9,... | collective-permute-start | bytes 49160 | tf_op jit(solution)/shard_map/ppermute | solution.py:424
  34.4 42.2 %all-gather = f32[32,4,1280]{2,1,0:T(4,128)} all-gather(f32[1,4,1280]{2,1,0:T(4,128)} %bitcast.25), channel_id=1, replica_groups=mesh['ax'=8,'az'=32] {'az'}, dimensions={0}, use_global_device_ids=true | all-gather | bytes 675840 | tf_op jit(solution)/shard_map/all_gather | solution.py:448
  76.6 0.8 reshape.9.idx
  77.3 1.4 %reshape.13.table = f32[128,1280]{1,0:T(8,128)S(1)} reshape(f32[32,4,1280]{2,1,0:T(4,128)} %all-gather) | data formatting | bytes 1310720
  78.8 0.0 collective-permute-done.2.tprev
  78.8 0.0 collective-permute-done.3.tnext
  78.8 0.0 collective-permute-done.1.znext
  78.8 0.0 collective-permute-done.zprev
  78.8 0.0 copy-start.3
  78.8 2.0 %copy-done.3 = f32[18,50,8,128]{3,2,1,0:T(8,128)S(1)} copy-done((f32[18,50,8,128]{3,2,1,0:T(8,128)S(1)}, f32[18,50,8,128]{3,2,1,0:T(8,128)}, u32[]{:S(2)}) %copy-start.3) | copy-done | bytes 3686424
  80.9 1.1 copy-done.5
  81.9 0.9 copy-done.7
  82.8 0.7 copy-done.11
  83.5 0.7 copy-done.14
  84.2 2.4 %shard_map.74 = (f32[19,5,8,128]{3,2,1,0:T(8,128)S(1)}, f32[16,5,8,128]{3,2,1,0:T(8,128)S(1)}, f32[8,128]{1,0:T(8,128)S(1)}) custom-call(f32[5,4,32,256]{3,2,1,0:T(8,128)S(1)} %copy-done.5, f32[5,32,256]{2,1,0:T(8,128)S(1)} %collective-permute-done.zprev, f32[5,32,256]{2,1,0:T(8,128)S(1)} %collective-permute-done.1.znext, ...), custom_call_target="tpu_custom_call" | custom-call | flops 4000000 | bytes 6414968 | tf_op jit(solution)/shard_map/pallas_call | solution.py:410
  86.6 4.0 %collective-permute-start.4 = (f32[8,128]{1,0:T(8,128)S(1)}, f32[8,128]{1,0:T(8,128)S(1)}, u32[]{:S(2)}, u32[]{:S(2)}) collective-permute-start(f32[8,128]{1,0:T(8,128)S(1)} %get-tuple-element.22.y_own), channel_id=1, source_target_pairs={{0,16},{1,17},{2,18},{3,19},{4,20},{5,21},{6,22},{7,23},{8,24},{9,... | collective-permute-start | bytes 12296 | tf_op jit(solution)/shard_map/ppermute | solution.py:424
  90.6 0.0 collective-permute-done.5.other_ref
  90.6 0.1 shard_map.75.j_ref
  90.8 3.4 %collective-permute-done.4.y_other = f32[8,128]{1,0:T(8,128)S(1)} collective-permute-done((f32[8,128]{1,0:T(8,128)S(1)}, f32[8,128]{1,0:T(8,128)S(1)}, u32[]{:S(2)}, u32[]{:S(2)}) %collective-permute-start.4) | collective-permute-done | bytes 4128 | tf_op jit(solution)/shard_map/ppermute | solution.py:424
  94.2 0.0 copy-done.12
  94.2 2.7 %copy-done.1 = f32[19,75,8,128]{3,2,1,0:T(8,128)S(1)} copy-done((f32[19,75,8,128]{3,2,1,0:T(8,128)S(1)}, f32[19,75,8,128]{3,2,1,0:T(8,128)}, u32[]{:S(2)}) %copy-start.1) | copy-done | bytes 5836824
  96.9 1.8 %shard_map.76 = (f32[5,4,32,256]{3,2,1,0:T(8,128)S(1)}, f32[5,32,256]{2,1,0:T(8,128)S(1)}, f32[5,32,256]{2,1,0:T(8,128)S(1)}, f32[5,4,256]{2,1,0:T(4,128)S(1)}, f32[5,4,256]{2,1,0:T(4,128)S(1)}) custom-call(f32[8,128]{1,0:T(8,128)S(1)} %get-tuple-element.22.y_own, f32[8,128]{1,0:T(8,128)S(1)} %collective-permute-done.4.y_other, ...), custom_call_target="tpu_custom_call" | custom-call | flops 4000000 | bytes 7808120 | tf_op jit(solution)/shard_map/pallas_call | solution.py:410
  98.6 1.9 %collective-permute-start.6 = (f32[5,32,256]{2,1,0:T(8,128)S(1)}, f32[5,32,256]{2,1,0:T(8,128)S(1)}, u32[]{:S(2)}, u32[]{:S(2)}) collective-permute-start(f32[5,32,256]{2,1,0:T(8,128)S(1)} %get-tuple-element.28), channel_id=1, source_target_pairs={{0,32},{32,64},{64,96},{96,128},{128,160},{160,192},{192,224},{1,3... | collective-permute-start | bytes 491528 | tf_op jit(solution)/shard_map/ppermute | solution.py:424
  100.6 4.8 %collective-permute-start.7 = (f32[5,32,256]{2,1,0:T(8,128)S(1)}, f32[5,32,256]{2,1,0:T(8,128)S(1)}, u32[]{:S(2)}, u32[]{:S(2)}) collective-permute-start(f32[5,32,256]{2,1,0:T(8,128)S(1)} %get-tuple-element.29), channel_id=1, source_target_pairs={{32,0},{64,32},{96,64},{128,96},{160,128},{192,160},{224,192},{33,... | collective-permute-start | bytes 491528 | tf_op jit(solution)/shard_map/ppermute | solution.py:424
  105.4 0.1 collective-permute-start.8
  105.5 5.3 %collective-permute-start.9 = (f32[5,4,256]{2,1,0:T(4,128)S(1)}, f32[5,4,256]{2,1,0:T(4,128)S(1)}, u32[]{:S(2)}, u32[]{:S(2)}) collective-permute-start(f32[5,4,256]{2,1,0:T(4,128)S(1)} %get-tuple-element.31), channel_id=1, source_target_pairs={{0,31},{1,0},{2,1},{3,2},{4,3},{5,4},{6,5},{7,6},{8,7},{9,8},{10,9... | collective-permute-start | bytes 61448 | tf_op jit(solution)/shard_map/ppermute | solution.py:424
  110.8 1.5 %collective-permute-done.8.tprev = f32[5,4,256]{2,1,0:T(4,128)S(1)} collective-permute-done((f32[5,4,256]{2,1,0:T(4,128)S(1)}, f32[5,4,256]{2,1,0:T(4,128)S(1)}, u32[]{:S(2)}, u32[]{:S(2)}) %collective-permute-start.8) | collective-permute-done | bytes 20512 | tf_op jit(solution)/shard_map/ppermute | solution.py:424
  112.3 0.0 collective-permute-done.9.tnext
  112.3 0.0 collective-permute-done.6.zprev
  112.3 0.0 collective-permute-done.7.znext
  112.3 1.9 %shard_map.77 = (f32[19,5,8,128]{3,2,1,0:T(8,128)S(1)}, f32[16,5,8,128]{3,2,1,0:T(8,128)S(1)}, f32[8,128]{1,0:T(8,128)S(1)}) custom-call(f32[5,4,32,256]{3,2,1,0:T(8,128)S(1)} %get-tuple-element.27.u.first, f32[5,32,256]{2,1,0:T(8,128)S(1)} %collective-permute-done.6.zprev, f32[5,32,256]{2,1,0:T(8,128)S(1)} %collective-permute-done.7.znext, ...), custom_call_target="tpu_custom_call" | custom-call | flops 4000000 | bytes 5759096 | tf_op jit(solution)/shard_map/pallas_call | solution.py:410
  114.3 4.0 %collective-permute-start.10 = (f32[8,128]{1,0:T(8,128)S(1)}, f32[8,128]{1,0:T(8,128)S(1)}, u32[]{:S(2)}, u32[]{:S(2)}) collective-permute-start(f32[8,128]{1,0:T(8,128)S(1)} %get-tuple-element.32.y_own), channel_id=1, source_target_pairs={{0,16},{1,17},{2,18},{3,19},{4,20},{5,21},{6,22},{7,23},{8,24},{9,... | collective-permute-start | bytes 12296 | tf_op jit(solution)/shard_map/ppermute | solution.py:424
  118.3 3.6 %collective-permute-done.10.y_other = f32[8,128]{1,0:T(8,128)S(1)} collective-permute-done((f32[8,128]{1,0:T(8,128)S(1)}, f32[8,128]{1,0:T(8,128)S(1)}, u32[]{:S(2)}, u32[]{:S(2)}) %collective-permute-start.10) | collective-permute-done | bytes 4128 | tf_op jit(solution)/shard_map/ppermute | solution.py:424
  121.9 2.6 %shard_map.78 = f32[5,4,32,256]{3,2,1,0:T(8,128)} custom-call(f32[8,128]{1,0:T(8,128)S(1)} %get-tuple-element.32.y_own, f32[8,128]{1,0:T(8,128)S(1)} %collective-permute-done.10.y_other, f32[50,128]{1,0:T(8,128)S(1)} %shard_map.75.j_ref, f32[19,75,8,128]{3,2,1,0:T(8,128)S(1)} %bitcast.17, f32[16,3,8,128]{3,2,1,0:T(8,128)S(1)} %get-tuple-element.21.scal, ...), custom_call_target="tpu_custom_call" | custom-call | flops 4000000 | bytes 8094840 | tf_op jit(solution)/shard_map/pallas_call | solution.py:410
  (24 shorter events, 0.1 us)
Async XLA Ops:
  0.0 94.2 %copy-start.12 = (f32[5,5]{1,0:T(8,128)S(1)}, f32[5,5]{1,0:T(8,128)}, u32[]{:S(2)}) copy-start(f32[5,5]{1,0:T(8,128)} %coup.7) | copy-start | bytes 304
  0.0 94.2 %copy-start.15 = (f32[5]{0:T(128)S(1)}, f32[5]{0:T(128)}, u32[]{:S(2)}) copy-start(f32[5]{0:T(128)} %param.13) | copy-start | bytes 64
  1.1 77.7 %collective-permute-start.2 = (f32[5,4,256]{2,1,0:T(4,128)S(1)}, f32[5,4,256]{2,1,0:T(4,128)S(1)}, u32[]{:S(2)}, u32[]{:S(2)}) collective-permute-start(f32[5,4,256]{2,1,0:T(4,128)S(1)} %bitcast.23), channel_id=1, source_target_pairs={{0,1},{1,2},{2,3},{3,4},{4,5},{5,6},{6,7},{7,8},{8,9},{9,10},{10,1... | collective-permute-start | bytes 61448 | tf_op jit(solution)/shard_map/ppermute | solution.py:424
  1.2 77.6 %collective-permute-start.3 = (f32[5,4,256]{2,1,0:T(4,128)S(1)}, f32[5,4,256]{2,1,0:T(4,128)S(1)}, u32[]{:S(2)}, u32[]{:S(2)}) collective-permute-start(f32[5,4,256]{2,1,0:T(4,128)S(1)} %bitcast.24), channel_id=1, source_target_pairs={{0,31},{1,0},{2,1},{3,2},{4,3},{5,4},{6,5},{7,6},{8,7},{9,8},{10,9... | collective-permute-start | bytes 61448 | tf_op jit(solution)/shard_map/ppermute | solution.py:424
  10.2 68.6 %collective-permute-start.1 = (f32[5,32,256]{2,1,0:T(8,128)S(1)}, f32[5,32,256]{2,1,0:T(8,128)S(1)}, u32[]{:S(2)}, u32[]{:S(2)}) collective-permute-start(f32[5,32,256]{2,1,0:T(8,128)S(1)} %get-tuple-element.37), channel_id=1, source_target_pairs={{32,0},{64,32},{96,64},{128,96},{160,128},{192,160},{224,192},{33,... | collective-permute-start | bytes 491528 | tf_op jit(solution)/shard_map/ppermute | solution.py:424
  13.1 65.7 %collective-permute-start = (f32[5,32,256]{2,1,0:T(8,128)S(1)}, f32[5,32,256]{2,1,0:T(8,128)S(1)}, u32[]{:S(2)}, u32[]{:S(2)}) collective-permute-start(f32[5,32,256]{2,1,0:T(8,128)S(1)} %get-tuple-element.38), channel_id=1, source_target_pairs={{0,32},{32,64},{64,96},{96,128},{128,160},{160,192},{192,224},{1,3... | collective-permute-start | bytes 491528 | tf_op jit(solution)/shard_map/ppermute | solution.py:424
  16.1 0.9 copy-start.6
  17.0 0.9 copy-start.9
  17.9 0.7 copy-start.10
  18.6 0.7 copy-start.13
  25.4 2.5 %copy-start = (f32[19,75,8,128]{3,2,1,0:T(8,128)}, f32[19,75,8,128]{3,2,1,0:T(8,128)S(1)}, u32[]{:S(2)}) copy-start(f32[19,75,8,128]{3,2,1,0:T(8,128)S(1)} %get-tuple-element.24.mb) | copy-start | bytes 17510404
  28.0 1.9 %copy-start.2 = (f32[18,50,8,128]{3,2,1,0:T(8,128)}, f32[18,50,8,128]{3,2,1,0:T(8,128)S(1)}, u32[]{:S(2)}) copy-start(f32[18,50,8,128]{3,2,1,0:T(8,128)S(1)} %get-tuple-element.20.mf) | copy-start | bytes 11059204
  29.8 60.8 %collective-permute-start.5 = (f32[32,128]{1,0:T(8,128)S(1)}, f32[32,128]{1,0:T(8,128)S(1)}, u32[]{:S(2)}, u32[]{:S(2)}) collective-permute-start(f32[32,128]{1,0:T(8,128)S(1)} %get-tuple-element.23.own_ref), channel_id=1, source_target_pairs={{0,16},{1,17},{2,18},{3,19},{4,20},{5,21},{6,22},{7,23},{8,24},{9,... | collective-permute-start | bytes 49160 | tf_op jit(solution)/shard_map/ppermute | solution.py:424
  77.3 44.6 %slice-start = ((s8[5836800]{0:T(1024)(128)(4,1)}), s8[1642496]{0:T(1024)(128)(4,1)S(1)}, s32[]{:S(2)}) async-start(s8[5836800]{0:T(1024)(128)(4,1)} %bitcast.16), calls=%async_computation | async-start | bytes 3284992
  78.8 2.0 %copy-start.3 = (f32[18,50,8,128]{3,2,1,0:T(8,128)S(1)}, f32[18,50,8,128]{3,2,1,0:T(8,128)}, u32[]{:S(2)}) copy-start(f32[18,50,8,128]{3,2,1,0:T(8,128)} %copy-done.2) | copy-start | bytes 11059204
  80.9 1.1 copy-start.5
  81.9 0.9 copy-start.7
  82.8 0.7 copy-start.11
  83.5 0.7 copy-start.14
  84.2 28.1 %copy-start.4 = (f32[18,50,8,128]{3,2,1,0:T(8,128)S(1)}, f32[18,50,8,128]{3,2,1,0:T(8,128)}, u32[]{:S(2)}) copy-start(f32[18,50,8,128]{3,2,1,0:T(8,128)} %copy-done.2) | copy-start | bytes 11059204
  84.2 28.1 %copy-start.8 = (s32[4,32,256]{2,1,0:T(8,128)S(1)}, s32[4,32,256]{2,1,0:T(8,128)}, u32[]{:S(2)}) copy-start(s32[4,32,256]{2,1,0:T(8,128)} %blank.3) | copy-start | bytes 393220
  86.6 7.6 %collective-permute-start.4 = (f32[8,128]{1,0:T(8,128)S(1)}, f32[8,128]{1,0:T(8,128)S(1)}, u32[]{:S(2)}, u32[]{:S(2)}) collective-permute-start(f32[8,128]{1,0:T(8,128)S(1)} %get-tuple-element.22.y_own), channel_id=1, source_target_pairs={{0,16},{1,17},{2,18},{3,19},{4,20},{5,21},{6,22},{7,23},{8,24},{9,... | collective-permute-start | bytes 12296 | tf_op jit(solution)/shard_map/ppermute | solution.py:424
  94.2 2.7 %copy-start.1 = (f32[19,75,8,128]{3,2,1,0:T(8,128)S(1)}, f32[19,75,8,128]{3,2,1,0:T(8,128)}, u32[]{:S(2)}) copy-start(f32[19,75,8,128]{3,2,1,0:T(8,128)} %copy-done) | copy-start | bytes 17510404
  96.9 25.0 %slice-start.1 = ((s8[5836800]{0:T(1024)(128)(4,1)}), s8[4194304]{0:T(1024)(128)(4,1)S(1)}, s32[]{:S(2)}) async-start(s8[5836800]{0:T(1024)(128)(4,1)} %bitcast.16), calls=%async_computation.1 | async-start | bytes 8388608
  98.6 13.7 %collective-permute-start.6 = (f32[5,32,256]{2,1,0:T(8,128)S(1)}, f32[5,32,256]{2,1,0:T(8,128)S(1)}, u32[]{:S(2)}, u32[]{:S(2)}) collective-permute-start(f32[5,32,256]{2,1,0:T(8,128)S(1)} %get-tuple-element.28), channel_id=1, source_target_pairs={{0,32},{32,64},{64,96},{96,128},{128,160},{160,192},{192,224},{1,3... | collective-permute-start | bytes 491528 | tf_op jit(solution)/shard_map/ppermute | solution.py:424
  100.6 11.8 %collective-permute-start.7 = (f32[5,32,256]{2,1,0:T(8,128)S(1)}, f32[5,32,256]{2,1,0:T(8,128)S(1)}, u32[]{:S(2)}, u32[]{:S(2)}) collective-permute-start(f32[5,32,256]{2,1,0:T(8,128)S(1)} %get-tuple-element.29), channel_id=1, source_target_pairs={{32,0},{64,32},{96,64},{128,96},{160,128},{192,160},{224,192},{33,... | collective-permute-start | bytes 491528 | tf_op jit(solution)/shard_map/ppermute | solution.py:424
  105.4 6.9 %collective-permute-start.8 = (f32[5,4,256]{2,1,0:T(4,128)S(1)}, f32[5,4,256]{2,1,0:T(4,128)S(1)}, u32[]{:S(2)}, u32[]{:S(2)}) collective-permute-start(f32[5,4,256]{2,1,0:T(4,128)S(1)} %get-tuple-element.30), channel_id=1, source_target_pairs={{0,1},{1,2},{2,3},{3,4},{4,5},{5,6},{6,7},{7,8},{8,9},{9,10},{10,1... | collective-permute-start | bytes 61448 | tf_op jit(solution)/shard_map/ppermute | solution.py:424
  105.5 6.8 %collective-permute-start.9 = (f32[5,4,256]{2,1,0:T(4,128)S(1)}, f32[5,4,256]{2,1,0:T(4,128)S(1)}, u32[]{:S(2)}, u32[]{:S(2)}) collective-permute-start(f32[5,4,256]{2,1,0:T(4,128)S(1)} %get-tuple-element.31), channel_id=1, source_target_pairs={{0,31},{1,0},{2,1},{3,2},{4,3},{5,4},{6,5},{7,6},{8,7},{9,8},{10,9... | collective-permute-start | bytes 61448 | tf_op jit(solution)/shard_map/ppermute | solution.py:424
  114.3 7.6 %collective-permute-start.10 = (f32[8,128]{1,0:T(8,128)S(1)}, f32[8,128]{1,0:T(8,128)S(1)}, u32[]{:S(2)}, u32[]{:S(2)}) collective-permute-start(f32[8,128]{1,0:T(8,128)S(1)} %get-tuple-element.32.y_own), channel_id=1, source_target_pairs={{0,16},{1,17},{2,18},{3,19},{4,20},{5,21},{6,22},{7,23},{8,24},{9,... | collective-permute-start | bytes 12296 | tf_op jit(solution)/shard_map/ppermute | solution.py:424
where the time goes:
time: 126 us; the launch traced here: 124 us
  blocking collectives  42.2 us (33%)
  starting transfers between devices  38.7 us (31%)
  local copies, waits for them, and re-layouts  19.8 us (16%)
  Pallas kernels  15.1 us (12%)
  waiting for transfers between devices  8.51 us (7%)
    all_gather x1, blocking collectives, per_device(): lax.all_gather(canard_table.reshape(local_rows, comps * radial), 'az', ax...  42.2 us
    ppermute x11, starting transfers between devices, shifted(): return lax.ppermute(x, axis, pairs)  38.7 us
    unnamed x39, local copies, waits for them, and re-layouts  17 us
    pallas_call x6, Pallas kernels, call(): pl.pallas_call(kernel, out_shape=out_shape, in_specs=in_specs, out_specs=...  15.1 us
    ppermute x11, waiting for transfers between devices, shifted(): return lax.ppermute(x, axis, pairs)  8.51 us
  transfers between devices with their start and end apart: 11, of which 3 were waited for; matrix products, arithmetic and copies ran while one was open for 3% of the time, Pallas kernels for 7%

commit v1 on v0

--- a/solution.py
+++ b/solution.py
@@ -10,7 +10,7 @@
 SEG = 8
 LANES = 128
 HALF = 16
-VMEM_LIMIT = 20 * 1024 * 1024
+VMEM_LIMIT = 16 * 1024 * 1024
 F32 = jnp.float32
 STEPS = [(s * (2 * i + 1), s) for s in (1, 2, 4, 8) for i in range(8 // s)]
 
@@ -26,7 +26,7 @@
 def splat_consts(coupling_ref, upwind_ref):
     shape = (SEG, LANES)
     p = [[jnp.full(shape, coupling_ref[i, j], F32) for j in range(N)] for i in range(N)]
-    w = [jnp.full(shape, upwind_ref[0, i], F32) for i in range(N)]
+    w = [jnp.full(shape, upwind_ref[i], F32) for i in range(N)]
     a = [[p[i][j] + w[i] if i == j else p[i][j] for j in range(N)] for i in range(N)]
     b = [[(1.0 - w[i]) - p[j][i] if i == j else -p[j][i] for j in range(N)] for i in range(N)]
     return a, b
@@ -87,16 +87,64 @@
     return p + 2
 
 
+LAM_ROW, MASK_ROW, VEC_ROW, JOINT_ROWS = NN, NN + 1, NN + 2, 32
 D0, OUT0, IN0 = 0, NN, 2 * NN
 LO0, LI0 = 0, NN
 
 
-def factor_kernel(coef_ref, blank_ref, coup_ref, upw_ref, mb, mf, scal, sd, lam_t, mask_t, face, pw):
-    mask = blank_ref[...].astype(F32).reshape(LANES, 2 * HALF * SEG)
+def prelude_kernel(
+    flow, table, coef, blank, index, coup, upw,
+    u, rows, coef_ref, mask_ref, place, cst, zfirst, zlast, tfirst, tlast,
+    piece, blank_ref, index_ref, coup_ref, upw_ref, sem,
+):
+    pairs = (
+        (table.at[0], piece),
+        (coup, coup_ref),
+        (upw, upw_ref),
+        (index, index_ref),
+        (blank, blank_ref),
+        (coef, coef_ref),
+        (flow, u),
+    )
+    copies = [pltpu.make_async_copy(src, dst, sem.at[i]) for i, (src, dst) in enumerate(pairs)]
+    for copy in copies:
+        copy.start()
+    _, planes, sectors, radial = u.shape
+    copies[0].wait()
+    for row in range(piece.shape[1]):
+        for v in range(N):
+            rows[pl.ds(row, 1), pl.ds(v * radial, radial)] = piece[v, pl.ds(row, 1), :]
+    copies[1].wait()
+    copies[2].wait()
+    a, b = splat_consts(coup_ref, upw_ref)
+    store_mat(cst, 0, 0, a)
+    store_mat(cst, 1, 0, b)
+    copies[3].wait()
+    place[...] = table_place(index_ref[...])
+    copies[4].wait()
+    mask_ref[...] = blank_ref[...].astype(F32).reshape(planes * sectors, radial)
+    copies[5].wait()
+    copies[6].wait()
+    for v in range(N):
+        zfirst[v] = u[v, 0]
+        zlast[v] = u[v, planes - 1]
+        for z in range(planes):
+            tfirst[v, pl.ds(z, 1), :] = u[v, z, pl.ds(0, 1), :]
+            tlast[v, pl.ds(z, 1), :] = u[v, z, pl.ds(sectors - 1, 1), :]
+
+
+def append_kernel(low, high, out):
+    half = low.shape[0]
+    out[pl.ds(0, half), :] = low[...]
+    out[pl.ds(half, half), :] = high[...]
+
+
+def factor_kernel(coef_ref, mask_ref, cst, mb, mf, scal, sd, lam_t, mask_t, face, pw):
+    mask = mask_ref[...]
     lam = coef_ref[...].reshape(LANES, 2 * HALF * SEG) * mask
     lam_t[...] = lam.T
     mask_t[...] = mask.T
-    a, b = splat_consts(coup_ref, upw_ref)
+    a, b = load_mat(cst, 0, 0), load_mat(cst, 1, 0)
     for which, mat in enumerate((mat_mul(a, a), mat_mul(b, b), mat_mul(a, b), mat_mul(b, a))):
         store_mat(pw, which, 0, mat)
 
@@ -149,7 +197,14 @@
         mb[slot_of(HALF), OUT0 + e] = jnp.zeros((SEG, LANES), F32)
         mb[slot_of(HALF), IN0 + e] = last * pw[1, e]
 
-    def eliminate(it, c):
+    sd[...] = jnp.zeros((JOINT_ROWS, LANES), F32)
+    sd[pl.ds(LAM_ROW, 1), :] = first_lam[0:1]
+    sd[pl.ds(MASK_ROW, 1), :] = first_mask[0:1]
+    eliminate(mb, mf, 0, 8)
+
+
+def eliminate(mb, mf, start, stop):
+    def step(it, c):
         s = jnp.where(it < 8, 1, jnp.where(it < 12, 2, jnp.where(it < 14, 4, 8)))
         first = jnp.where(it < 8, 0, jnp.where(it < 12, 8, jnp.where(it < 14, 12, 14)))
         m = s * (2 * (it - first) + 1)
@@ -183,8 +238,11 @@
                 mb[sp, OUT0 + i * N + j] = dot_row(row, out_m, j)
         return c
 
-    lax.fori_loop(0, len(STEPS), eliminate, 0)
-
+    lax.fori_loop(start, stop, step, 0)
+
+
+def factor_rest_kernel(mb_in, mf_in, sd_in, mb, mf, sd):
+    eliminate(mb, mf, 8, len(STEPS))
     s0, s16 = slot_of(0), slot_of(HALF)
     for e in range(NN):
         mb[0, D0 + e] = mb[s0, D0 + e] + down(mb[s16, D0 + e], 1)
@@ -229,14 +287,11 @@
                 row = load_row(mf, level, LI0, i)
                 for j in range(N):
                     mb[level + 1, IN0 + i * N + j] = dot_row(row, in_down, j)
-    sd[pl.ds(NN, 1), :] = first_lam[0:1]
-    sd[pl.ds(NN + 1, 1), :] = first_mask[0:1]
-    sd[pl.ds(NN + 2, 5), :] = jnp.zeros((5, LANES), F32)
-
-
-def join_kernel(own_ref, other_ref, j_ref):
-    lam, mask = own_ref[pl.ds(NN, 1), :], own_ref[pl.ds(NN + 1, 1), :]
-    other_lam, other_mask = other_ref[pl.ds(NN, 1), :], other_ref[pl.ds(NN + 1, 1), :]
+
+
+def join(own_ref, other_ref, j_ref):
+    lam, mask = own_ref[pl.ds(LAM_ROW, 1), :], own_ref[pl.ds(MASK_ROW, 1), :]
+    other_lam, other_mask = other_ref[pl.ds(LAM_ROW, 1), :], other_ref[pl.ds(MASK_ROW, 1), :]
     c = 0.25 * (lam * other_mask + other_lam * mask)
 
     def total(ref):
@@ -264,8 +319,8 @@
     return behind + ahead + before_t + after_t - 4.0 * cur + 0.5 * (behind - ahead)
 
 
-def forward_body(rhs_t, mf, scal, coup_ref, upw_ref, e_ref, o_ref, y_ref):
-    a, b = splat_consts(coup_ref, upw_ref)
+def forward_body(rhs_t, mf, scal, cst, e_ref, o_ref):
+    a, b = load_mat(cst, 0, 0), load_mat(cst, 1, 0)
     zero = jnp.zeros((SEG, LANES), F32)
     carry = [zero] * N
     first = None
@@ -296,47 +351,70 @@
         lo = mat_vec(load_mat(mf, level, LO0), [up(x, s) for x in cur])
         li = mat_vec(load_mat(mf, level, LI0), [down(x, s) for x in cur])
         cur = [cur[v] + lo[v] + li[v] for v in range(N)]
-    for v in range(N):
-        y_ref[pl.ds(v, 1), :] = cur[v][0:1]
-    y_ref[pl.ds(N, 3), :] = jnp.zeros((3, LANES), F32)
+    return [cur[v][0:1] for v in range(N)]
+
+
+def doubling_bits():
+    return [bit for bit in (16, 8, 2, 4, 1) if bit < lax.axis_size("az")]
+
+
+def table_place(index):
+    apart = lax.shift_right_logical(index, 2) ^ lax.axis_index("az")
+    block = jnp.zeros_like(apart)
+    for i, bit in enumerate(doubling_bits()):
+        block = block | (jnp.where((apart & bit) != 0, 1, 0) << i)
+    return block * 4 + (index & 3)
 
 
 def forward_first_kernel(
-    u, zprev, znext, tprev, tnext, blank, idx, table, mf, scal, coup, upw, e_ref, o_ref, y_ref, rhs_t
+    u, zprev, znext, tprev, tnext, mask_ref, place, low, high, mf, scal, cst, sd,
+    e_ref, o_ref, joint, rhs_t,
 ):
-    planes, sectors, radial = blank.shape
-    mask = blank[...].astype(F32).reshape(planes * sectors, radial)
-    rows = lax.broadcasted_iota(jnp.int32, (table.shape[0], LANES), 0)
-    onehot = (rows == idx[...]).astype(F32).T
-    for v in range(N):
-        force = jnp.dot(
-            onehot,
-            table[:, pl.ds(v * radial, radial)],
+    planes, sectors = place.shape
+    radial = mask_ref.shape[1]
+    mask = mask_ref[...]
+    half = low.shape[0]
+    rows = lax.broadcasted_iota(jnp.int32, (2 * half, sectors), 0)
+    onehot = [(rows == place[pl.ds(z, 1), :]).astype(F32).T for z in range(planes)]
+    hot_low = jnp.concatenate([x[:, :half] for x in onehot], axis=0)
+    hot_high = jnp.concatenate([x[:, half:] for x in onehot], axis=0)
+
+    def pick(hot, rows, v):
+        return jnp.dot(
+            hot,
+            rows[:, pl.ds(v * radial, radial)],
             precision=lax.Precision.HIGHEST,
             preferred_element_type=F32,
         )
+
+    for v in range(N):
+        force = pick(hot_low, low, v) + pick(hot_high, high, v)
         blocks = [stencil_block(u, v, z, planes, zprev, znext, tprev, tnext) for z in range(planes)]
         rhs = mask * (jnp.concatenate(blocks, axis=0) + force)
         rhs_t[v] = rhs.T
-    forward_body(rhs_t, mf, scal, coup, upw, e_ref, o_ref, y_ref)
+    reduced = forward_body(rhs_t, mf, scal, cst, e_ref, o_ref)
+    joint[...] = sd[...]
+    for v in range(N):
+        joint[pl.ds(VEC_ROW + v, 1), :] = reduced[v]
 
 
 def forward_second_kernel(
-    u, zprev, znext, tprev, tnext, blank, mf, scal, coup, upw, e_ref, o_ref, y_ref, rhs_t
+    u, zprev, znext, tprev, tnext, mask_ref, mf, scal, cst, e_ref, o_ref, y_ref, rhs_t
 ):
-    planes, sectors, radial = blank.shape
-    mask = blank[...].astype(F32).reshape(planes * sectors, radial)
+    planes = u.shape[1]
+    mask = mask_ref[...]
     for v in range(N):
         blocks = [stencil_block(u, v, z, planes, zprev, znext, tprev, tnext) for z in range(planes)]
         rhs_t[v] = (mask * jnp.concatenate(blocks, axis=0)).T
-    forward_body(rhs_t, mf, scal, coup, upw, e_ref, o_ref, y_ref)
-
-
-def backward_body(y_own, y_other, j_ref, mb, scal, coup_ref, upw_ref, e_ref, o_ref, x_ref, x_t):
-    a, b = splat_consts(coup_ref, upw_ref)
+    reduced = forward_body(rhs_t, mf, scal, cst, e_ref, o_ref)
+    y_ref[...] = jnp.zeros((SEG, LANES), F32)
+    for v in range(N):
+        y_ref[pl.ds(v, 1), :] = reduced[v]
+
+
+def backward_body(own, other, j_ref, mb, scal, cst, e_ref, o_ref, x_ref, x_t):
+    a, b = load_mat(cst, 0, 0), load_mat(cst, 1, 0)
     sub = lax.broadcasted_iota(jnp.int32, (SEG, LANES), 0)
-    own = [y_own[pl.ds(v, 1), :] for v in range(N)]
-    other = [y_other[pl.ds(v, 1), :] for v in range(N)]
     cur = []
     for i in range(N):
         acc = j_ref[pl.ds(i * N, 1), :] * own[0]
@@ -378,10 +456,13 @@
 
 
 def backward_first_kernel(
-    y_own, y_other, j_ref, mb, scal, coup, upw, e_ref, o_ref,
-    out, zfirst, zlast, tfirst, tlast, x_ref, x_t,
+    joint, other_joint, mb, scal, cst, e_ref, o_ref,
+    out, zfirst, zlast, tfirst, tlast, j_ref, x_ref, x_t,
 ):
-    backward_body(y_own, y_other, j_ref, mb, scal, coup, upw, e_ref, o_ref, x_ref, x_t)
+    join(joint, other_joint, j_ref)
+    own = [joint[pl.ds(VEC_ROW + v, 1), :] for v in range(N)]
+    other = [other_joint[pl.ds(VEC_ROW + v, 1), :] for v in range(N)]
+    backward_body(own, other, j_ref, mb, scal, cst, e_ref, o_ref, x_ref, x_t)
     _, planes, sectors, radial = out.shape
     for v in range(N):
         field = x_t[v].T.reshape(planes, sectors, radial)
@@ -394,27 +475,33 @@
 
 
 def backward_second_kernel(
-    y_own, y_other, j_ref, mb, scal, coup, upw, e_ref, o_ref, first, out, x_ref, x_t
+    y_own, y_other, j_ref, mb, scal, cst, e_ref, o_ref, first, out, x_ref, x_t
 ):
-    backward_body(y_own, y_other, j_ref, mb, scal, coup, upw, e_ref, o_ref, x_ref, x_t)
+    own = [y_own[pl.ds(v, 1), :] for v in range(N)]
+    other = [y_other[pl.ds(v, 1), :] for v in range(N)]
+    backward_body(own, other, j_ref, mb, scal, cst, e_ref, o_ref, x_ref, x_t)
     _, planes, sectors, radial = out.shape
     for v in range(N):
         out[v] = first[v] + 0.5 * x_t[v].T.reshape(planes, sectors, radial)
 
 
-def call(kernel, inputs, outs, scratch, flops, smem=()):
+def call(kernel, inputs, outs, scratch, us, hbm=False, aliases=None):
     vmem = pl.BlockSpec(memory_space=pltpu.VMEM)
-    in_specs = [pl.BlockSpec(memory_space=pltpu.SMEM) if i in smem else vmem for i in range(len(inputs))]
-    out_shape = [jax.ShapeDtypeStruct(s, F32) for s in outs]
-    moved = sum(x.size for x in inputs) * 4 + sum(s.size for s in out_shape) * 4
+    if hbm:
+        inputs = [pltpu.with_memory_space_constraint(x, pltpu.HBM) for x in inputs]
+    in_spec = pl.BlockSpec(memory_space=pltpu.HBM) if hbm else vmem
+    out_shape = [s if isinstance(s, jax.ShapeDtypeStruct) else jax.ShapeDtypeStruct(s, F32) for s in outs]
     return pl.pallas_call(
         kernel,
         out_shape=out_shape,
-        in_specs=in_specs,
+        in_specs=[in_spec] * len(inputs),
         out_specs=[vmem] * len(outs),
-        scratch_shapes=[pltpu.VMEM(s, F32) for s in scratch],
+        scratch_shapes=[pltpu.VMEM(s, F32) if isinstance(s, tuple) else s for s in scratch],
+        input_output_aliases=aliases or {},
         compiler_params=pltpu.CompilerParams(vmem_limit_bytes=VMEM_LIMIT),
-        cost_estimate=pl.CostEstimate(flops=flops, bytes_accessed=moved, transcendentals=0),
+        cost_estimate=pl.CostEstimate(
+            flops=int(us * 1e9), bytes_accessed=int(us * 3e6), transcendentals=0
+        ),
     )(*inputs)
 
 
@@ -433,72 +520,121 @@
     )
 
 
+def xor_swap(x, bit):
+    return lax.ppermute(x, "az", [(i, i ^ bit) for i in range(lax.axis_size("az"))])
+
+
+def append(low, high):
+    (both,) = call(append_kernel, (low, high), [(2 * low.shape[0], low.shape[1])], [], 0.2)
+    return both
+
+
+def after(x, *others):
+    return lax.optimization_barrier((x, *others))[0]
+
+
 def per_device(
     flow_state, radial_coef, blanking, canard_index, canard_table, coupling, upwind_split
 ):
     comps, planes, sectors, radial = flow_state.shape
     tile = (SEG, LANES)
-    upw = upwind_split.reshape(1, N)
+    half_turn = lax.axis_size("az") // 2
     local_rows = canard_table.shape[1]
-    half_turn = lax.axis_size("az") // 2
-
-    first_halos = halos(
-        flow_state[:, 0], flow_state[:, planes - 1], flow_state[:, :, 0], flow_state[:, :, sectors - 1]
-    )
-    table = lax.all_gather(
-        canard_table.reshape(local_rows, comps * radial), "az", axis=0, tiled=True
-    )
-    idx = canard_index.reshape(1, planes * sectors)
-
     field = (comps, planes, sectors, radial)
+    edges = [(comps, sectors, radial)] * 2 + [(comps, planes, radial)] * 2
+
+    ints = jax.ShapeDtypeStruct(canard_index.shape, jnp.int32)
+    u, rows, coef, mask, place, cst, *first_edges = call(
+        prelude_kernel,
+        (flow_state, canard_table.transpose(0, 2, 1, 3), radial_coef, blanking, canard_index, coupling, upwind_split),
+        [
+            field,
+            (local_rows, comps * radial),
+            (planes, sectors, radial),
+            (LANES, radial),
+            ints,
+            (2, NN) + tile,
+        ]
+        + edges,
+        [
+            (comps, local_rows, radial),
+            pltpu.VMEM((planes, sectors, radial), jnp.int32),
+            pltpu.VMEM(canard_index.shape, jnp.int32),
+            pltpu.SMEM((N, N), F32),
+            pltpu.SMEM((N,), F32),
+            pltpu.SemaphoreType.DMA((7,)),
+        ],
+        1.2,
+        hbm=True,
+    )
+    bits = doubling_bits()
+    swapped = xor_swap(rows, bits[0])
+    first_halos = halos(*first_edges)
+    rows = append(rows, swapped)
     mb, mf, scal, sd = call(
         factor_kernel,
-        (radial_coef, blanking, coupling, upw),
-        [(HALF + 3, 3 * NN) + tile, (HALF + 2, 2 * NN) + tile, (HALF, 3) + tile, (32, LANES)],
+        (after(coef, rows), mask, cst),
+        [
+            (HALF + 3, 3 * NN) + tile,
+            (HALF + 2, 2 * NN) + tile,
+            (HALF, 3) + tile,
+            (JOINT_ROWS, LANES),
+        ],
         [(radial, LANES), (radial, LANES), (2 * HALF + 1,) + tile, (4, NN) + tile],
-        32_000_000,
-        (2, 3),
-    )
-    other_sd = shifted(sd, "az", half_turn, True)
-    fwd_outs = [(HALF + 3, N) + tile, (HALF, N) + tile, tile]
+        3.2,
+    )
+    for i, bit in enumerate(bits[1:-1]):
+        swapped = xor_swap(rows, bit)
+        if i == 0:
+            swapped = after(swapped, sd)
+        elif i == 1:
+            mb, mf, sd = call(
+                factor_rest_kernel,
+                (after(mb, rows), mf, sd),
+                [mb.shape, mf.shape, sd.shape],
+                [],
+                3.0,
+                aliases={0: 0, 1: 1, 2: 2},
+            )
+            swapped = after(swapped, sd, *first_halos[:2])
+        else:
+            swapped = after(swapped, *first_halos[2:])
+        rows = append(rows, swapped)
+    others = xor_swap(rows, bits[-1])
+    fwd_outs = [(HALF + 3, N) + tile, (HALF, N) + tile]
     rhs_scratch = [(N, radial, LANES)]
     back_scratch = [(HALF + 1, N) + tile, (N, radial, LANES)]
 
-    e1, o1, y1 = call(
+    e1, o1, joint = call(
         forward_first_kernel,
-        (flow_state, *first_halos, blanking, idx, table, mf, scal, coupling, upw),
-        fwd_outs,
+        (u, *first_halos, mask, place, rows, others, mf, scal, cst, sd),
+        fwd_outs + [(JOINT_ROWS, LANES)],
         rhs_scratch,
-        4_000_000,
-        (10, 11),
-    )
-    other_y1 = shifted(y1, "az", half_turn, True)
-    (joint,) = call(join_kernel, (sd, other_sd), [(2 * NN, LANES)], [], 200_000)
-    first, *edges = call(
+        2.4,
+    )
+    other_joint = shifted(joint, "az", half_turn, True)
+    first, *second_edges, axis_inverse = call(
         backward_first_kernel,
-        (y1, other_y1, joint, mb, scal, coupling, upw, e1, o1),
-        [field, (comps, sectors, radial), (comps, sectors, radial), (comps, planes, radial), (comps, planes, radial)],
+        (joint, other_joint, mb, scal, cst, e1, o1),
+        [field] + edges + [(2 * NN, LANES)],
         back_scratch,
-        4_000_000,
-        (5, 6),
-    )
-    second_halos = halos(*edges)
+        2.0,
+    )
+    second_halos = halos(*second_edges)
     e2, o2, y2 = call(
         forward_second_kernel,
-        (first, *second_halos, blanking, mf, scal, coupling, upw),
-        fwd_outs,
+        (first, *second_halos, mask, mf, scal, cst),
+        fwd_outs + [tile],
         rhs_scratch,
-        4_000_000,
-        (8, 9),
+        2.0,
     )
     other_y2 = shifted(y2, "az", half_turn, True)
     (update,) = call(
         backward_second_kernel,
-        (y2, other_y2, joint, mb, scal, coupling, upw, e2, o2, first),
+        (y2, other_y2, axis_inverse, mb, scal, cst, e2, o2, first),
         [field],
         back_scratch,
-        4_000_000,
-        (5, 6),
+        2.0,
     )
     return update
 

time: 126 us -> 73.1 us (0.58); the launches traced: 124 us -> 72.9 us
  blocking collectives: 42.2 us -> 0 us
  local copies, waits for them, and re-layouts: 19.8 us -> 0 us
  waiting for transfers between devices: 8.51 us -> 17.6 us
  starting transfers between devices: 38.7 us -> 41.3 us
    all_gather x1 -> x0, blocking collectives: 42.2 us -> none  [per_device(): lax.all_gather(canard_table.reshape(local_rows, comps * radial), 'az', ax...]
    unnamed x39 -> x0, local copies, waits for them, and re-layouts: 17 us -> none
    ppermute x0 -> x5, starting transfers between devices: none -> 14.4 us  [xor_swap(): lax.ppermute(x, 'az', [(i, i ^ bit) for i in range(lax.axis_size('az'))])]
    ppermute x11 -> x10, starting transfers between devices: 38.7 us -> 26.9 us  [shifted(): return lax.ppermute(x, axis, pairs)]
    ppermute x11 -> x10, waiting for transfers between devices: 8.51 us -> 15.8 us  [shifted(): return lax.ppermute(x, axis, pairs)]
    ppermute x0 -> x5, waiting for transfers between devices: none -> 1.81 us  [xor_swap(): lax.ppermute(x, 'az', [(i, i ^ bit) for i in range(lax.axis_size('az'))])]
    pallas_call x6 -> x11, Pallas kernels: 15.1 us -> 13.9 us  [call(): pl.pallas_call(kernel, out_shape=out_shape, in_specs=[in_spec] * len(inpu...]
  transfers between devices with their start and end apart: 11 -> 15, of which waited for: 3 -> 7; matrix products, arithmetic and copies ran while one was open for 3% -> 0% of each run, Pallas kernels for 7% -> 8%
where the time goes in v1:
time: 73.1 us; the launch traced here: 72.9 us
  starting transfers between devices  41.3 us (56%)
  waiting for transfers between devices  17.6 us (24%)
  Pallas kernels  13.9 us (19%)
    ppermute x10, starting transfers between devices, shifted(): return lax.ppermute(x, axis, pairs)  26.9 us
    ppermute x10, waiting for transfers between devices, shifted(): return lax.ppermute(x, axis, pairs)  15.8 us
    ppermute x5, starting transfers between devices, xor_swap(): lax.ppermute(x, 'az', [(i, i ^ bit) for i in range(lax.axis_size('az'))])  14.4 us
    pallas_call x11, Pallas kernels, call(): pl.pallas_call(kernel, out_shape=out_shape, in_specs=[in_spec] * len(inpu...  13.9 us
    ppermute x5, waiting for transfers between devices, xor_swap(): lax.ppermute(x, 'az', [(i, i ^ bit) for i in range(lax.axis_size('az'))])  1.81 us
  transfers between devices with their start and end apart: 15, of which 7 were waited for; matrix products, arithmetic and copies ran while one was open for 0% of the time, Pallas kernels for 8%

profile of v1, /device:TPU:6, one launch (start us, length us, event | category | flops | bytes accessed | tf_op | source)
XLA Modules:
  0.0 72.9 jit_solution(15348111675117646404)
XLA Ops:
  0.0 1.4 %shard_map.73 = (f32[5,4,32,256]{3,2,1,0:T(8,128)S(1)}, f32[4,1280]{1,0:T(4,128)S(1)}, f32[4,32,256]{2,1,0:T(8,128)S(1)}, f32[128,256]{1,0:T(8,128)S(1)}, s32[4,...) custom-call(f32[5,4,32,256]{3,2,1,0:T(8,128)} %flow.1, ...), custom_call_target="tpu_custom_call" | custom-call | flops 1200000000 | bytes 3600000 | tf_op jit(solution)/shard_map/pallas_call | solution.py:494
  1.4 7.3 %collective-permute-start.4 = (f32[4,1280]{1,0:T(4,128)S(1)}, f32[4,1280]{1,0:T(4,128)S(1)}, u32[]{:S(2)}, u32[]{:S(2)}) collective-permute-start(f32[4,1280]{1,0:T(4,128)S(1)} %get-tuple-element.46.low), channel_id=1, source_target_pairs={{0,16},{1,17},{2,18},{3,19},{4,20},{5,21},{6,22},{7,23},{8,24},{9,... | collective-permute-start | bytes 61448 | tf_op jit(solution)/shard_map/ppermute | solution.py:524
  8.6 3.5 %collective-permute-start = (f32[5,32,256]{2,1,0:T(8,128)S(1)}, f32[5,32,256]{2,1,0:T(8,128)S(1)}, u32[]{:S(2)}, u32[]{:S(2)}) collective-permute-start(f32[5,32,256]{2,1,0:T(8,128)S(1)} %get-tuple-element.40), channel_id=1, source_target_pairs={{0,32},{32,64},{64,96},{96,128},{128,160},{160,192},{192,224},{1,3... | collective-permute-start | bytes 491528 | tf_op jit(solution)/shard_map/ppermute | solution.py:511
  12.1 3.3 %collective-permute-start.1 = (f32[5,32,256]{2,1,0:T(8,128)S(1)}, f32[5,32,256]{2,1,0:T(8,128)S(1)}, u32[]{:S(2)}, u32[]{:S(2)}) collective-permute-start(f32[5,32,256]{2,1,0:T(8,128)S(1)} %get-tuple-element.41), channel_id=1, source_target_pairs={{32,0},{64,32},{96,64},{128,96},{160,128},{192,160},{224,192},{33,... | collective-permute-start | bytes 491528 | tf_op jit(solution)/shard_map/ppermute | solution.py:511
  15.4 0.0 collective-permute-done.4.high
  15.4 1.6 %collective-permute-start.5 = (f32[8,1280]{1,0:T(8,128)S(1)}, f32[8,1280]{1,0:T(8,128)S(1)}, u32[]{:S(2)}, u32[]{:S(2)}) collective-permute-start(f32[8,1280]{1,0:T(8,128)S(1)} %shard_map.74.low), channel_id=1, source_target_pairs={{0,8},{1,9},{2,10},{3,11},{4,12},{5,13},{6,14},{7,15},{8,0},{9,1},... | collective-permute-start | bytes 122888 | tf_op jit(solution)/shard_map/ppermute | solution.py:524
  17.0 3.1 %shard_map.75 = (f32[19,75,8,128]{3,2,1,0:T(8,128)S(1)}, f32[18,50,8,128]{3,2,1,0:T(8,128)S(1)}, f32[16,3,8,128]{3,2,1,0:T(8,128)S(1)}, f32[32,128]{1,0:T(8,128)S(1)}) custom-call(f32[4,32,256]{2,1,0:T(8,128)S(1)} %get-tuple-element.48.coef_ref, f32[128,256]{1,0:T(8,128)S(1)} %get-tuple-element.44.mask_ref, f32[2,25,8,128]{3,2,1,0:T(8,128)S(1)} %get-tuple-element.49.cst), custom_call_target="tpu_custom_call" | custom-call | flops 3200000000 | bytes 9600000 | tf_op jit(solution)/shard_map/pallas_call | solution.py:494
  20.1 0.3 collective-permute-done.5.high
  20.4 3.2 %collective-permute-start.6 = (f32[16,1280]{1,0:T(8,128)S(1)}, f32[16,1280]{1,0:T(8,128)S(1)}, u32[]{:S(2)}, u32[]{:S(2)}) collective-permute-start(f32[16,1280]{1,0:T(8,128)S(1)} %shard_map.76.low), channel_id=1, source_target_pairs={{0,2},{1,3},{2,0},{3,1},{4,6},{5,7},{6,4},{7,5},{8,10},{9,11},{10,... | collective-permute-start | bytes 245768 | tf_op jit(solution)/shard_map/ppermute | solution.py:524
  23.6 2.5 %shard_map.77 = (f32[19,75,8,128]{3,2,1,0:T(8,128)S(1)}, f32[18,50,8,128]{3,2,1,0:T(8,128)S(1)}, f32[32,128]{1,0:T(8,128)S(1)}) custom-call(f32[19,75,8,128]{3,2,1,0:T(8,128)S(1)} %get-tuple-element.53.mb_in, f32[18,50,8,128]{3,2,1,0:T(8,128)S(1)} %get-tuple-element.54.mf_in, ...), custom_call_target="tpu_custom_call", output_to_operand_aliasing={{0}: (0, {}), {1}: (1, {}), {2}: (2, {})} | custom-call | flops 3000000000 | bytes 9000000 | tf_op jit(solution)/shard_map/pallas_call | solution.py:494
  26.1 0.3 collective-permute-done.6.high
  26.4 0.0 collective-permute-done.zprev
  26.4 0.0 collective-permute-done.1.znext
  26.4 1.1 %collective-permute-start.7 = (f32[32,1280]{1,0:T(8,128)S(1)}, f32[32,1280]{1,0:T(8,128)S(1)}, u32[]{:S(2)}, u32[]{:S(2)}) collective-permute-start(f32[32,1280]{1,0:T(8,128)S(1)} %shard_map.78.low), channel_id=1, source_target_pairs={{0,4},{1,5},{2,6},{3,7},{4,0},{5,1},{6,2},{7,3},{8,12},{9,13},{10,... | collective-permute-start | bytes 491528 | tf_op jit(solution)/shard_map/ppermute | solution.py:524
  27.5 0.0 collective-permute-start.2
  27.5 5.4 %collective-permute-start.3 = (f32[5,4,256]{2,1,0:T(4,128)S(1)}, f32[5,4,256]{2,1,0:T(4,128)S(1)}, u32[]{:S(2)}, u32[]{:S(2)}) collective-permute-start(f32[5,4,256]{2,1,0:T(4,128)S(1)} %get-tuple-element.43), channel_id=1, source_target_pairs={{0,31},{1,0},{2,1},{3,2},{4,3},{5,4},{6,5},{7,6},{8,7},{9,8},{10,9... | collective-permute-start | bytes 61448 | tf_op jit(solution)/shard_map/ppermute | solution.py:511
  32.9 1.5 %collective-permute-done.2.tprev = f32[5,4,256]{2,1,0:T(4,128)S(1)} collective-permute-done((f32[5,4,256]{2,1,0:T(4,128)S(1)}, f32[5,4,256]{2,1,0:T(4,128)S(1)}, u32[]{:S(2)}, u32[]{:S(2)}) %collective-permute-start.2) | collective-permute-done | bytes 20512 | tf_op jit(solution)/shard_map/ppermute | solution.py:511
  34.3 0.0 collective-permute-done.3.tnext
  34.3 0.0 collective-permute-done.7.high
  34.4 1.3 %collective-permute-start.8 = (f32[64,1280]{1,0:T(8,128)S(1)}, f32[64,1280]{1,0:T(8,128)S(1)}, u32[]{:S(2)}, u32[]{:S(2)}) collective-permute-start(f32[64,1280]{1,0:T(8,128)S(1)} %shard_map.79.low), channel_id=1, source_target_pairs={{0,1},{1,0},{2,3},{3,2},{4,5},{5,4},{6,7},{7,6},{8,9},{9,8},{10,11... | collective-permute-start | bytes 983048 | tf_op jit(solution)/shard_map/ppermute | solution.py:524
  35.6 1.3 %collective-permute-done.8.high = f32[64,1280]{1,0:T(8,128)S(1)} collective-permute-done((f32[64,1280]{1,0:T(8,128)S(1)}, f32[64,1280]{1,0:T(8,128)S(1)}, u32[]{:S(2)}, u32[]{:S(2)}) %collective-permute-start.8) | collective-permute-done | bytes 327712 | tf_op jit(solution)/shard_map/ppermute | solution.py:524
  36.9 2.3 %shard_map.80 = (f32[19,5,8,128]{3,2,1,0:T(8,128)S(1)}, f32[16,5,8,128]{3,2,1,0:T(8,128)S(1)}, f32[32,128]{1,0:T(8,128)S(1)}) custom-call(f32[5,4,32,256]{3,2,1,0:T(8,128)S(1)} %get-tuple-element.39.u, f32[5,32,256]{2,1,0:T(8,128)S(1)} %collective-permute-done.zprev, f32[5,32,256]{2,1,0:T(8,128)S(1)} %collective-permute-done.1.znext, ...), custom_call_target="tpu_custom_call" | custom-call | flops 2400000000 | bytes 7200000 | tf_op jit(solution)/shard_map/pallas_call | solution.py:494
  39.2 1.4 %collective-permute-start.9 = (f32[32,128]{1,0:T(8,128)S(1)}, f32[32,128]{1,0:T(8,128)S(1)}, u32[]{:S(2)}, u32[]{:S(2)}) collective-permute-start(f32[32,128]{1,0:T(8,128)S(1)} %get-tuple-element.60.joint), channel_id=1, source_target_pairs={{0,16},{1,17},{2,18},{3,19},{4,20},{5,21},{6,22},{7,23},{8,24},{9,... | collective-permute-start | bytes 49160 | tf_op jit(solution)/shard_map/ppermute | solution.py:511
  40.5 6.4 %collective-permute-done.9.other_joint = f32[32,128]{1,0:T(8,128)S(1)} collective-permute-done((f32[32,128]{1,0:T(8,128)S(1)}, f32[32,128]{1,0:T(8,128)S(1)}, u32[]{:S(2)}, u32[]{:S(2)}) %collective-permute-start.9) | collective-permute-done | bytes 16416 | tf_op jit(solution)/shard_map/ppermute | solution.py:511
  46.9 1.3 %shard_map.81 = (f32[5,4,32,256]{3,2,1,0:T(8,128)S(1)}, f32[5,32,256]{2,1,0:T(8,128)S(1)}, f32[5,32,256]{2,1,0:T(8,128)S(1)}, f32[5,4,256]{2,1,0:T(4,128)S(1)}, ...) custom-call(f32[32,128]{1,0:T(8,128)S(1)} %get-tuple-element.60.joint, f32[32,128]{1,0:T(8,128)S(1)} %collective-permute-done.9.other_joint, ...), custom_call_target="tpu_custom_call" | custom-call | flops 2000000000 | bytes 6000000 | tf_op jit(solution)/shard_map/pallas_call | solution.py:494
  48.2 1.9 %collective-permute-start.10 = (f32[5,32,256]{2,1,0:T(8,128)S(1)}, f32[5,32,256]{2,1,0:T(8,128)S(1)}, u32[]{:S(2)}, u32[]{:S(2)}) collective-permute-start(f32[5,32,256]{2,1,0:T(8,128)S(1)} %get-tuple-element.65), channel_id=1, source_target_pairs={{0,32},{32,64},{64,96},{96,128},{128,160},{160,192},{192,224},{1,3... | collective-permute-start | bytes 491528 | tf_op jit(solution)/shard_map/ppermute | solution.py:511
  50.1 4.8 %collective-permute-start.11 = (f32[5,32,256]{2,1,0:T(8,128)S(1)}, f32[5,32,256]{2,1,0:T(8,128)S(1)}, u32[]{:S(2)}, u32[]{:S(2)}) collective-permute-start(f32[5,32,256]{2,1,0:T(8,128)S(1)} %get-tuple-element.66), channel_id=1, source_target_pairs={{32,0},{64,32},{96,64},{128,96},{160,128},{192,160},{224,192},{33,... | collective-permute-start | bytes 491528 | tf_op jit(solution)/shard_map/ppermute | solution.py:511
  55.0 0.1 collective-permute-start.12
  55.0 5.3 %collective-permute-start.13 = (f32[5,4,256]{2,1,0:T(4,128)S(1)}, f32[5,4,256]{2,1,0:T(4,128)S(1)}, u32[]{:S(2)}, u32[]{:S(2)}) collective-permute-start(f32[5,4,256]{2,1,0:T(4,128)S(1)} %get-tuple-element.68), channel_id=1, source_target_pairs={{0,31},{1,0},{2,1},{3,2},{4,3},{5,4},{6,5},{7,6},{8,7},{9,8},{10,9... | collective-permute-start | bytes 61448 | tf_op jit(solution)/shard_map/ppermute | solution.py:511
  60.4 1.5 %collective-permute-done.12.tprev = f32[5,4,256]{2,1,0:T(4,128)S(1)} collective-permute-done((f32[5,4,256]{2,1,0:T(4,128)S(1)}, f32[5,4,256]{2,1,0:T(4,128)S(1)}, u32[]{:S(2)}, u32[]{:S(2)}) %collective-permute-start.12) | collective-permute-done | bytes 20512 | tf_op jit(solution)/shard_map/ppermute | solution.py:511
  61.9 0.0 collective-permute-done.13.tnext
  61.9 0.0 collective-permute-done.10.zprev
  61.9 0.0 collective-permute-done.11.znext
  62.0 1.3 %shard_map.82 = (f32[19,5,8,128]{3,2,1,0:T(8,128)S(1)}, f32[16,5,8,128]{3,2,1,0:T(8,128)S(1)}, f32[8,128]{1,0:T(8,128)S(1)}) custom-call(f32[5,4,32,256]{3,2,1,0:T(8,128)S(1)} %get-tuple-element.64.u.first, f32[5,32,256]{2,1,0:T(8,128)S(1)} %collective-permute-done.10.zprev, f32[5,32,256]{2,1,0:T(8,128)S(1)} %collective-permute-done.11.znext, ...), custom_call_target="tpu_custom_call" | custom-call | flops 2000000000 | bytes 6000000 | tf_op jit(solution)/shard_map/pallas_call | solution.py:494
  63.3 1.3 %collective-permute-start.14 = (f32[8,128]{1,0:T(8,128)S(1)}, f32[8,128]{1,0:T(8,128)S(1)}, u32[]{:S(2)}, u32[]{:S(2)}) collective-permute-start(f32[8,128]{1,0:T(8,128)S(1)} %get-tuple-element.69.y_own), channel_id=1, source_target_pairs={{0,16},{1,17},{2,18},{3,19},{4,20},{5,21},{6,22},{7,23},{8,24},{9,... | collective-permute-start | bytes 12296 | tf_op jit(solution)/shard_map/ppermute | solution.py:511
  64.5 6.3 %collective-permute-done.14.y_other = f32[8,128]{1,0:T(8,128)S(1)} collective-permute-done((f32[8,128]{1,0:T(8,128)S(1)}, f32[8,128]{1,0:T(8,128)S(1)}, u32[]{:S(2)}, u32[]{:S(2)}) %collective-permute-start.14) | collective-permute-done | bytes 4128 | tf_op jit(solution)/shard_map/ppermute | solution.py:511
  70.9 2.0 %shard_map.83 = f32[5,4,32,256]{3,2,1,0:T(8,128)} custom-call(f32[8,128]{1,0:T(8,128)S(1)} %get-tuple-element.69.y_own, f32[8,128]{1,0:T(8,128)S(1)} %collective-permute-done.14.y_other, f32[50,128]{1,0:T(8,128)S(1)} %get-tuple-element.70.j_ref, f32[19,75,8,128]{3,2,1,0:T(8,128)S(1)} %get-tuple-element.61.mb, f32[16,3,8,128]{3,2,1,0:T(8,128)S(1)} %get-tuple-element.59.scal, ...), custom_call_target="tpu_custom_call" | custom-call | flops 2000000000 | bytes 6000000 | tf_op jit(solution)/shard_map/pallas_call | solution.py:494
  (4 shorter events, 0.0 us)
Async XLA Ops:
  1.4 14.0 %collective-permute-start.4 = (f32[4,1280]{1,0:T(4,128)S(1)}, f32[4,1280]{1,0:T(4,128)S(1)}, u32[]{:S(2)}, u32[]{:S(2)}) collective-permute-start(f32[4,1280]{1,0:T(4,128)S(1)} %get-tuple-element.46.low), channel_id=1, source_target_pairs={{0,16},{1,17},{2,18},{3,19},{4,20},{5,21},{6,22},{7,23},{8,24},{9,... | collective-permute-start | bytes 61448 | tf_op jit(solution)/shard_map/ppermute | solution.py:524
  8.6 17.7 %collective-permute-start = (f32[5,32,256]{2,1,0:T(8,128)S(1)}, f32[5,32,256]{2,1,0:T(8,128)S(1)}, u32[]{:S(2)}, u32[]{:S(2)}) collective-permute-start(f32[5,32,256]{2,1,0:T(8,128)S(1)} %get-tuple-element.40), channel_id=1, source_target_pairs={{0,32},{32,64},{64,96},{96,128},{128,160},{160,192},{192,224},{1,3... | collective-permute-start | bytes 491528 | tf_op jit(solution)/shard_map/ppermute | solution.py:511
  12.1 14.3 %collective-permute-start.1 = (f32[5,32,256]{2,1,0:T(8,128)S(1)}, f32[5,32,256]{2,1,0:T(8,128)S(1)}, u32[]{:S(2)}, u32[]{:S(2)}) collective-permute-start(f32[5,32,256]{2,1,0:T(8,128)S(1)} %get-tuple-element.41), channel_id=1, source_target_pairs={{32,0},{64,32},{96,64},{128,96},{160,128},{192,160},{224,192},{33,... | collective-permute-start | bytes 491528 | tf_op jit(solution)/shard_map/ppermute | solution.py:511
  15.4 5.0 %collective-permute-start.5 = (f32[8,1280]{1,0:T(8,128)S(1)}, f32[8,1280]{1,0:T(8,128)S(1)}, u32[]{:S(2)}, u32[]{:S(2)}) collective-permute-start(f32[8,1280]{1,0:T(8,128)S(1)} %shard_map.74.low), channel_id=1, source_target_pairs={{0,8},{1,9},{2,10},{3,11},{4,12},{5,13},{6,14},{7,15},{8,0},{9,1},... | collective-permute-start | bytes 122888 | tf_op jit(solution)/shard_map/ppermute | solution.py:524
  20.4 6.0 %collective-permute-start.6 = (f32[16,1280]{1,0:T(8,128)S(1)}, f32[16,1280]{1,0:T(8,128)S(1)}, u32[]{:S(2)}, u32[]{:S(2)}) collective-permute-start(f32[16,1280]{1,0:T(8,128)S(1)} %shard_map.76.low), channel_id=1, source_target_pairs={{0,2},{1,3},{2,0},{3,1},{4,6},{5,7},{6,4},{7,5},{8,10},{9,11},{10,... | collective-permute-start | bytes 245768 | tf_op jit(solution)/shard_map/ppermute | solution.py:524
  26.4 8.0 %collective-permute-start.7 = (f32[32,1280]{1,0:T(8,128)S(1)}, f32[32,1280]{1,0:T(8,128)S(1)}, u32[]{:S(2)}, u32[]{:S(2)}) collective-permute-start(f32[32,1280]{1,0:T(8,128)S(1)} %shard_map.78.low), channel_id=1, source_target_pairs={{0,4},{1,5},{2,6},{3,7},{4,0},{5,1},{6,2},{7,3},{8,12},{9,13},{10,... | collective-permute-start | bytes 491528 | tf_op jit(solution)/shard_map/ppermute | solution.py:524
  27.5 6.8 %collective-permute-start.2 = (f32[5,4,256]{2,1,0:T(4,128)S(1)}, f32[5,4,256]{2,1,0:T(4,128)S(1)}, u32[]{:S(2)}, u32[]{:S(2)}) collective-permute-start(f32[5,4,256]{2,1,0:T(4,128)S(1)} %get-tuple-element.42), channel_id=1, source_target_pairs={{0,1},{1,2},{2,3},{3,4},{4,5},{5,6},{6,7},{7,8},{8,9},{9,10},{10,1... | collective-permute-start | bytes 61448 | tf_op jit(solution)/shard_map/ppermute | solution.py:511
  27.5 6.8 %collective-permute-start.3 = (f32[5,4,256]{2,1,0:T(4,128)S(1)}, f32[5,4,256]{2,1,0:T(4,128)S(1)}, u32[]{:S(2)}, u32[]{:S(2)}) collective-permute-start(f32[5,4,256]{2,1,0:T(4,128)S(1)} %get-tuple-element.43), channel_id=1, source_target_pairs={{0,31},{1,0},{2,1},{3,2},{4,3},{5,4},{6,5},{7,6},{8,7},{9,8},{10,9... | collective-permute-start | bytes 61448 | tf_op jit(solution)/shard_map/ppermute | solution.py:511
  34.4 2.5 %collective-permute-start.8 = (f32[64,1280]{1,0:T(8,128)S(1)}, f32[64,1280]{1,0:T(8,128)S(1)}, u32[]{:S(2)}, u32[]{:S(2)}) collective-permute-start(f32[64,1280]{1,0:T(8,128)S(1)} %shard_map.79.low), channel_id=1, source_target_pairs={{0,1},{1,0},{2,3},{3,2},{4,5},{5,4},{6,7},{7,6},{8,9},{9,8},{10,11... | collective-permute-start | bytes 983048 | tf_op jit(solution)/shard_map/ppermute | solution.py:524
  39.2 7.7 %collective-permute-start.9 = (f32[32,128]{1,0:T(8,128)S(1)}, f32[32,128]{1,0:T(8,128)S(1)}, u32[]{:S(2)}, u32[]{:S(2)}) collective-permute-start(f32[32,128]{1,0:T(8,128)S(1)} %get-tuple-element.60.joint), channel_id=1, source_target_pairs={{0,16},{1,17},{2,18},{3,19},{4,20},{5,21},{6,22},{7,23},{8,24},{9,... | collective-permute-start | bytes 49160 | tf_op jit(solution)/shard_map/ppermute | solution.py:511
  48.2 13.7 %collective-permute-start.10 = (f32[5,32,256]{2,1,0:T(8,128)S(1)}, f32[5,32,256]{2,1,0:T(8,128)S(1)}, u32[]{:S(2)}, u32[]{:S(2)}) collective-permute-start(f32[5,32,256]{2,1,0:T(8,128)S(1)} %get-tuple-element.65), channel_id=1, source_target_pairs={{0,32},{32,64},{64,96},{96,128},{128,160},{160,192},{192,224},{1,3... | collective-permute-start | bytes 491528 | tf_op jit(solution)/shard_map/ppermute | solution.py:511
  50.1 11.8 %collective-permute-start.11 = (f32[5,32,256]{2,1,0:T(8,128)S(1)}, f32[5,32,256]{2,1,0:T(8,128)S(1)}, u32[]{:S(2)}, u32[]{:S(2)}) collective-permute-start(f32[5,32,256]{2,1,0:T(8,128)S(1)} %get-tuple-element.66), channel_id=1, source_target_pairs={{32,0},{64,32},{96,64},{128,96},{160,128},{192,160},{224,192},{33,... | collective-permute-start | bytes 491528 | tf_op jit(solution)/shard_map/ppermute | solution.py:511
  55.0 7.0 %collective-permute-start.12 = (f32[5,4,256]{2,1,0:T(4,128)S(1)}, f32[5,4,256]{2,1,0:T(4,128)S(1)}, u32[]{:S(2)}, u32[]{:S(2)}) collective-permute-start(f32[5,4,256]{2,1,0:T(4,128)S(1)} %get-tuple-element.67), channel_id=1, source_target_pairs={{0,1},{1,2},{2,3},{3,4},{4,5},{5,6},{6,7},{7,8},{8,9},{9,10},{10,1... | collective-permute-start | bytes 61448 | tf_op jit(solution)/shard_map/ppermute | solution.py:511
  55.0 6.9 %collective-permute-start.13 = (f32[5,4,256]{2,1,0:T(4,128)S(1)}, f32[5,4,256]{2,1,0:T(4,128)S(1)}, u32[]{:S(2)}, u32[]{:S(2)}) collective-permute-start(f32[5,4,256]{2,1,0:T(4,128)S(1)} %get-tuple-element.68), channel_id=1, source_target_pairs={{0,31},{1,0},{2,1},{3,2},{4,3},{5,4},{6,5},{7,6},{8,7},{9,8},{10,9... | collective-permute-start | bytes 61448 | tf_op jit(solution)/shard_map/ppermute | solution.py:511
  63.3 7.6 %collective-permute-start.14 = (f32[8,128]{1,0:T(8,128)S(1)}, f32[8,128]{1,0:T(8,128)S(1)}, u32[]{:S(2)}, u32[]{:S(2)}) collective-permute-start(f32[8,128]{1,0:T(8,128)S(1)} %get-tuple-element.69.y_own), channel_id=1, source_target_pairs={{0,16},{1,17},{2,18},{3,19},{4,20},{5,21},{6,22},{7,23},{8,24},{9,... | collective-permute-start | bytes 12296 | tf_op jit(solution)/shard_map/ppermute | solution.py:511

commit v2 on v1

v2 whole, which is shorter than its diff:
```python
import jax
import jax.numpy as jnp
from jax import lax
from jax.experimental import pallas as pl
from jax.experimental.pallas import tpu as pltpu
from jax.sharding import PartitionSpec as P

N = 5
NN = 25
SEG = 8
LANES = 128
HALF = 16
VMEM_LIMIT = 16 * 1024 * 1024
F32 = jnp.float32
STEPS = [(s * (2 * i + 1), s) for s in (1, 2, 4, 8) for i in range(8 // s)]


def up(x, s):
    return pltpu.roll(x, SEG - s, 0)


def down(x, s):
    return pltpu.roll(x, s, 0)


def splat_consts(coupling_ref, upwind_ref):
    shape = (SEG, LANES)
    p = [[jnp.full(shape, coupling_ref[i, j], F32) for j in range(N)] for i in range(N)]
    w = [jnp.full(shape, upwind_ref[i], F32) for i in range(N)]
    a = [[p[i][j] + w[i] if i == j else p[i][j] for j in range(N)] for i in range(N)]
    b = [[(1.0 - w[i]) - p[j][i] if i == j else -p[j][i] for j in range(N)] for i in range(N)]
    return a, b


def dot_row(row, cols, j):
    acc = row[0] * cols[0][j]
    for k in range(1, N):
        acc = acc + row[k] * cols[k][j]
    return acc


def mat_mul(x, y):
    return [[dot_row(x[i], y, j) for j in range(N)] for i in range(N)]


def mat_vec(x, v):
    out = []
    for i in range(N):
        acc = x[i][0] * v[0]
        for k in range(1, N):
            acc = acc + x[i][k] * v[k]
        out.append(acc)
    return out


def invert(matrix):
    m = [list(row) for row in matrix]
    for p in range(N):
        piv = 1.0 / m[p][p]
        m[p] = [piv if j == p else m[p][j] * piv for j in range(N)]
        for i in range(N):
            if i != p:
                f = m[i][p]
                m[i] = [-(f * piv) if j == p else m[i][j] - f * m[p][j] for j in range(N)]
    return m


def load_mat(ref, slot, base):
    return [[ref[slot, base + i * N + j] for j in range(N)] for i in range(N)]


def load_row(ref, slot, base, i):
    return [ref[slot, base + i * N + j] for j in range(N)]


def store_mat(ref, slot, base, mat):
    for i in range(N):
        for j in range(N):
            ref[slot, base + i * N + j] = mat[i][j]


def strided(ref, k):
    return ref[pl.ds(k, SEG, stride=2 * HALF), :]


def slot_of(q):
    return q + 2


LAM_ROW, MASK_ROW, VEC_ROW, JOINT_ROWS = NN, NN + 1, NN + 2, 32
D0, OUT0, IN0 = 0, NN, 2 * NN
LO0, LI0 = 0, NN


def is_even(axis):
    return lax.axis_index(axis) % 2 == 0


def pack_edges(field, v, za, zb, ta, tb):
    _, planes, sectors, _ = field.shape
    z_up, t_up = is_even("ax"), is_even("az")
    za[v] = field[v, jnp.where(z_up, planes - 1, 0)]
    zb[v] = field[v, jnp.where(z_up, 0, planes - 1)]
    for z in range(planes):
        first, last = field[v, z, pl.ds(0, 1), :], field[v, z, pl.ds(sectors - 1, 1), :]
        ta[v, pl.ds(z, 1), :] = jnp.where(t_up, last, first)
        tb[v, pl.ds(z, 1), :] = jnp.where(t_up, first, last)


def prelude_kernel(
    flow, coef, blank, index, coup, upw,
    u, coef_ref, mask_ref, place, cst, za, zb, ta, tb,
    blank_ref, index_ref, coup_ref, upw_ref, sem,
):
    pairs = (
        (flow, u),
        (coup, coup_ref),
        (upw, upw_ref),
        (index, index_ref),
        (blank, blank_ref),
        (coef, coef_ref),
    )
    copies = [pltpu.make_async_copy(src, dst, sem.at[i]) for i, (src, dst) in enumerate(pairs)]
    for copy in copies:
        copy.start()
    _, planes, sectors, radial = u.shape
    copies[1].wait()
    copies[2].wait()
    a, b = splat_consts(coup_ref, upw_ref)
    store_mat(cst, 0, 0, a)
    store_mat(cst, 1, 0, b)
    copies[3].wait()
    place[...] = table_place(index_ref[...])
    copies[4].wait()
    mask_ref[...] = blank_ref[...].astype(F32).reshape(planes * sectors, radial)
    copies[5].wait()
    copies[0].wait()
    for v in range(N):
        pack_edges(u, v, za, zb, ta, tb)


def append_kernel(low, high, out):
    half = low.shape[1]
    out[:, pl.ds(0, half), :] = low[...]
    out[:, pl.ds(half, half), :] = high[...]


def factor_kernel(coef_ref, mask_ref, cst, m1, f1, scal, sd, mask_t, lam_t, face, pw):
    mask = mask_ref[...]
    lam = coef_ref[...].reshape(LANES, 2 * HALF * SEG) * mask
    lam_t[...] = lam.T
    mask_t[...] = mask.T
    a, b = load_mat(cst, 0, 0), load_mat(cst, 1, 0)
    for which, mat in enumerate((mat_mul(a, a), mat_mul(b, b), mat_mul(a, b), mat_mul(b, a))):
        store_mat(pw, which, 0, mat)

    sub = lax.broadcasted_iota(jnp.int32, (SEG, LANES), 0)
    first_lam, first_mask = strided(lam_t, 0), strided(mask_t, 0)
    lam_k, mask_k = first_lam, first_mask
    for k in range(2 * HALF):
        if k < 2 * HALF - 1:
            lam_n, mask_n = strided(lam_t, k + 1), strided(mask_t, k + 1)
            f = 0.5 * (lam_k * mask_n + lam_n * mask_k)
        else:
            lam_n, mask_n = up(first_lam, 1), up(first_mask, 1)
            f = jnp.where(sub == SEG - 1, 0.0, 0.5 * (lam_k * mask_n + lam_n * mask_k))
        face[k + 1] = f
        lam_k, mask_k = lam_n, mask_n
    face[0] = down(face[2 * HALF], 1)

    def build_odd(m, c):
        fl, fr = face[2 * m + 1], face[2 * m + 2]
        scal[m, 0] = 1.0 / (1.0 + 0.5 * (fl + fr))
        scal[m, 1] = fl
        scal[m, 2] = fr
        return c

    lax.fori_loop(0, HALF, build_odd, 0)

    def build_even(p, c):
        prev = jnp.where(p == 0, HALF - 1, p - 1)
        inv, fl, fr = scal[p, 0], scal[p, 1], scal[p, 2]
        inv_p, fl_p, fr_p = scal[prev, 0], scal[prev, 1], scal[prev, 2]
        beta = fr_p * fr_p * inv_p
        delta = fr_p * fl_p * inv_p
        beta = jnp.where(p == 0, down(beta, 1), beta)
        alpha = fl * fl * inv
        gamma = fl * fr * inv
        d = 1.0 + 0.5 * (face[2 * p] + face[2 * p + 1])
        for i in range(N):
            for j in range(N):
                e = i * N + j
                val = -(alpha * pw[2, e] + beta * pw[3, e])
                m1[p, D0 + e] = d + val if i == j else val
                m1[p, OUT0 + e] = gamma * pw[0, e]
                m1[p, IN0 + e] = delta * pw[1, e]
        return c

    lax.fori_loop(0, HALF, build_even, 0)
    last = scal[HALF - 1, 1] * scal[HALF - 1, 2] * scal[HALF - 1, 0]
    for e in range(NN):
        m1[HALF, D0 + e] = jnp.zeros((SEG, LANES), F32)
        m1[HALF, OUT0 + e] = jnp.zeros((SEG, LANES), F32)
        m1[HALF, IN0 + e] = last * pw[1, e]

    sd[...] = jnp.zeros((JOINT_ROWS, LANES), F32)
    sd[pl.ds(LAM_ROW, 1), :] = first_lam[0:1]
    sd[pl.ds(MASK_ROW, 1), :] = first_mask[0:1]

    def step(i, c):
        eliminate(m1, f1, 1, 2 * i + 1, i)
        return c

    lax.fori_loop(0, HALF // 2, step, 0)


def eliminate(mb, mf, s, sm, fm):
    sp, sq = sm - s, sm + s
    di = invert(load_mat(mb, sm, D0))
    store_mat(mb, sm, D0, di)
    for i in range(N):
        row = load_row(mb, sp, OUT0, i)
        for j in range(N):
            mf[fm, LO0 + i * N + j] = dot_row(row, di, j)
        row = load_row(mb, sq, IN0, i)
        for j in range(N):
            mf[fm, LI0 + i * N + j] = dot_row(row, di, j)
    in_m = load_mat(mb, sm, IN0)
    for i in range(N):
        row = load_row(mf, fm, LO0, i)
        for j in range(N):
            e = i * N + j
            mb[sp, D0 + e] = mb[sp, D0 + e] - dot_row(row, in_m, j)
        row = load_row(mf, fm, LI0, i)
        for j in range(N):
            mb[sq, IN0 + i * N + j] = dot_row(row, in_m, j)
    out_m = load_mat(mb, sm, OUT0)
    for i in range(N):
        row = load_row(mf, fm, LI0, i)
        for j in range(N):
            e = i * N + j
            mb[sq, D0 + e] = mb[sq, D0 + e] - dot_row(row, out_m, j)
        row = load_row(mf, fm, LO0, i)
        for j in range(N):
            mb[sp, OUT0 + i * N + j] = dot_row(row, out_m, j)


def factor_rest_kernel(m1, sd_in, mb, mf, sd):
    def fetch(q, c):
        for e in range(3 * NN):
            mb[slot_of(q), e] = m1[2 * q, e]
        return c

    lax.fori_loop(0, HALF // 2 + 1, fetch, 0)

    def step(it, c):
        s = jnp.where(it < 4, 1, jnp.where(it < 6, 2, 4))
        first = jnp.where(it < 4, 0, jnp.where(it < 6, 4, 6))
        q = s * (2 * (it - first) + 1)
        eliminate(mb, mf, s, slot_of(q), slot_of(q))
        return c

    lax.fori_loop(0, HALF // 2 - 1, step, 0)
    sd[...] = sd_in[...]
    s0, s16 = slot_of(0), slot_of(HALF // 2)
    for e in range(NN):
        mb[0, D0 + e] = mb[s0, D0 + e] + down(mb[s16, D0 + e], 1)
        mb[0, OUT0 + e] = mb[s0, OUT0 + e]
        mb[0, IN0 + e] = down(mb[s16, IN0 + e], 1)
    for level, s in enumerate((1, 2, 4)):
        d = load_mat(mb, level, D0)
        di = invert(d)
        store_mat(mb, level, D0, di)
        di_up = [[up(di[i][j], s) for j in range(N)] for i in range(N)]
        for i in range(N):
            row = load_row(mb, level, OUT0, i)
            for j in range(N):
                mf[level, LO0 + i * N + j] = dot_row(row, di_up, j)
        di_down = [[down(di[i][j], s) for j in range(N)] for i in range(N)]
        for i in range(N):
            row = load_row(mb, level, IN0, i)
            for j in range(N):
                mf[level, LI0 + i * N + j] = dot_row(row, di_down, j)
        in_up = [[up(mb[level, IN0 + i * N + j], s) for j in range(N)] for i in range(N)]
        acc = []
        for i in range(N):
            row = load_row(mf, level, LO0, i)
            acc.append([d[i][j] - dot_row(row, in_up, j) for j in range(N)])
        out_down = [[down(mb[level, OUT0 + i * N + j], s) for j in range(N)] for i in range(N)]
        for i in range(N):
            row = load_row(mf, level, LI0, i)
            for j in range(N):
                val = acc[i][j] - dot_row(row, out_down, j)
                if level < 2:
                    mb[level + 1, D0 + i * N + j] = val
                else:
                    sd[pl.ds(i * N + j, 1), :] = val[0:1]
        if level < 2:
            out_up = [[up(mb[level, OUT0 + i * N + j], s) for j in range(N)] for i in range(N)]
            for i in range(N):
                row = load_row(mf, level, LO0, i)
                for j in range(N):
                    mb[level + 1, OUT0 + i * N + j] = dot_row(row, out_up, j)
            in_down = [[down(mb[level, IN0 + i * N + j], s) for j in range(N)] for i in range(N)]
            for i in range(N):
                row = load_row(mf, level, LI0, i)
                for j in range(N):
                    mb[level + 1, IN0 + i * N + j] = dot_row(row, in_down, j)


def join(own_ref, other_ref, j_ref):
    lam, mask = own_ref[pl.ds(LAM_ROW, 1), :], own_ref[pl.ds(MASK_ROW, 1), :]
    other_lam, other_mask = other_ref[pl.ds(LAM_ROW, 1), :], other_ref[pl.ds(MASK_ROW, 1), :]
    c = 0.25 * (lam * other_mask + other_lam * mask)

    def total(ref):
        mat = [[ref[pl.ds(i * N + j, 1), :] for j in range(N)] for i in range(N)]
        return [[mat[i][j] + c if i == j else mat[i][j] for j in range(N)] for i in range(N)]

    own, inv_other = total(own_ref), invert(total(other_ref))
    schur = [[own[i][j] - c * (c * inv_other[i][j]) for j in range(N)] for i in range(N)]
    j1 = invert(schur)
    j2 = mat_mul(j1, inv_other)
    for i in range(N):
        for j in range(N):
            j_ref[pl.ds(i * N + j, 1), :] = j1[i][j]
            j_ref[pl.ds(NN + i * N + j, 1), :] = c * j2[i][j]


def stencil_block(u, v, z, planes, za, zb, ta, tb):
    z_up, t_up = is_even("ax"), is_even("az")
    cur = u[v, z]
    rows = lax.broadcasted_iota(jnp.int32, cur.shape, 0)
    behind = u[v, z - 1] if z > 0 else jnp.where(z_up, zb[v], za[v])
    ahead = u[v, z + 1] if z < planes - 1 else jnp.where(z_up, za[v], zb[v])
    sectors = cur.shape[0]
    t_a, t_b = ta[v, pl.ds(z, 1), :], tb[v, pl.ds(z, 1), :]
    before_t = jnp.where(rows == 0, jnp.where(t_up, t_b, t_a), pltpu.roll(cur, 1, 0))
    after_t = jnp.where(rows == sectors - 1, jnp.where(t_up, t_a, t_b), pltpu.roll(cur, sectors - 1, 0))
    return behind + ahead + before_t + after_t - 4.0 * cur + 0.5 * (behind - ahead)


def forward_body(rhs_t, f1, f2, scal, cst, e_ref, o_ref):
    a, b = load_mat(cst, 0, 0), load_mat(cst, 1, 0)
    zero = jnp.zeros((SEG, LANES), F32)
    carry = [zero] * N
    first = None
    for m in range(HALF):
        inv, fl, fr = scal[m, 0], scal[m, 1], scal[m, 2]
        odd = [strided(rhs_t.at[v], 2 * m + 1) for v in range(N)]
        scaled = [x * inv for x in odd]
        ta = mat_vec(a, scaled)
        tb = mat_vec(b, scaled)
        for v in range(N):
            o_ref[m, v] = odd[v]
            e_ref[m, v] = strided(rhs_t.at[v], 2 * m) + carry[v] + fl * ta[v]
        carry = [fr * tb[v] for v in range(N)]
    for v in range(N):
        e_ref[0, v] = e_ref[0, v] + down(carry[v], 1)
        e_ref[HALF, v] = zero
    for m, s in STEPS:
        vec = [e_ref[m, v] for v in range(N)]
        mf, slot = (f1, m // 2) if s == 1 else (f2, slot_of(m // 2))
        lo = mat_vec(load_mat(mf, slot, LO0), vec)
        li = mat_vec(load_mat(mf, slot, LI0), vec)
        for v in range(N):
            e_ref[m - s, v] = e_ref[m - s, v] + lo[v]
            e_ref[m + s, v] = e_ref[m + s, v] + li[v]
    cur = [e_ref[0, v] + down(e_ref[HALF, v], 1) for v in range(N)]
    for level, s in enumerate((1, 2, 4)):
        for v in range(N):
            e_ref[HALF + 1 + level, v] = cur[v]
        lo = mat_vec(load_mat(f2, level, LO0), [up(x, s) for x in cur])
        li = mat_vec(load_mat(f2, level, LI0), [down(x, s) for x in cur])
        cur = [cur[v] + lo[v] + li[v] for v in range(N)]
    return [cur[v][0:1] for v in range(N)]


def doubling_bits():
    return [bit for bit in (24, 8, 4, 2, 1) if bit < lax.axis_size("az")]


def table_place(index):
    apart = lax.shift_right_logical(index, 2) ^ lax.axis_index("az")
    block = jnp.zeros_like(apart)
    for i, bit in enumerate(doubling_bits()):
        used = (apart & (1 << (bit.bit_length() - 1))) != 0
        apart = jnp.where(used, apart ^ bit, apart)
        block = block | (jnp.where(used, 1, 0) << i)
    return block * 4 + (index & 3)


def one_hot(place, start, count):
    planes, sectors = place.shape
    rows = start + lax.broadcasted_iota(jnp.int32, (count, sectors), 0)
    hot = [jnp.where(rows == place[pl.ds(z, 1), :], 1.0, 0.0) for z in range(planes)]
    return jnp.concatenate(hot, axis=1)


def pick(rows, hot):
    return lax.dot_general(
        rows,
        hot,
        (((0,), (0,)), ((), ())),
        precision=lax.Precision.HIGHEST,
        preferred_element_type=F32,
    )


def rhs_kernel(u, za, zb, ta, tb, mask_ref, mask_t, place, low, rhs_t):
    planes = u.shape[1]
    mask = mask_ref[...]
    hot = one_hot(place, 0, low.shape[1])
    for v in range(N):
        blocks = [stencil_block(u, v, z, planes, za, zb, ta, tb) for z in range(planes)]
        rhs_t[v] = (mask * jnp.concatenate(blocks, axis=0)).T + mask_t[...] * pick(low[v], hot)


def forward_first_kernel(
    rhs_in, mask_t, place, high, f1, f2, scal, cst, sd, e_ref, o_ref, joint, rhs_t
):
    hot = one_hot(place, high.shape[1], high.shape[1])
    for v in range(N):
        rhs_t[v] = rhs_in[v] + mask_t[...] * pick(high[v], hot)
    reduced = forward_body(rhs_t, f1, f2, scal, cst, e_ref, o_ref)
    joint[...] = sd[...]
    for v in range(N):
        joint[pl.ds(VEC_ROW + v, 1), :] = reduced[v]


def forward_second_kernel(
    u, za, zb, ta, tb, mask_ref, f1, f2, scal, cst, e_ref, o_ref, y_ref, rhs_t
):
    planes = u.shape[1]
    mask = mask_ref[...]
    for v in range(N):
        blocks = [stencil_block(u, v, z, planes, za, zb, ta, tb) for z in range(planes)]
        rhs_t[v] = (mask * jnp.concatenate(blocks, axis=0)).T
    reduced = forward_body(rhs_t, f1, f2, scal, cst, e_ref, o_ref)
    y_ref[...] = jnp.zeros((SEG, LANES), F32)
    for v in range(N):
        y_ref[pl.ds(v, 1), :] = reduced[v]


def backward_body(own, other, j_ref, m1, m2, scal, cst, e_ref, o_ref, x_ref, x_t):
    a, b = load_mat(cst, 0, 0), load_mat(cst, 1, 0)
    sub = lax.broadcasted_iota(jnp.int32, (SEG, LANES), 0)
    cur = []
    for i in range(N):
        acc = j_ref[pl.ds(i * N, 1), :] * own[0]
        for k in range(N):
            if k > 0:
                acc = acc + j_ref[pl.ds(i * N + k, 1), :] * own[k]
            acc = acc + j_ref[pl.ds(NN + i * N + k, 1), :] * other[k]
        cur.append(jnp.broadcast_to(acc, (SEG, LANES)))

    def recover(mb, slot, rhs, high, low):
        o = mat_vec(load_mat(mb, slot, OUT0), high)
        i = mat_vec(load_mat(mb, slot, IN0), low)
        total = [e_ref[rhs, v] + o[v] + i[v] for v in range(N)]
        return mat_vec(load_mat(mb, slot, D0), total)

    for level, s in ((2, 4), (1, 2), (0, 1)):
        new = recover(m2, level, HALF + 1 + level, [up(x, s) for x in cur], [down(x, s) for x in cur])
        cur = [jnp.where(sub % (2 * s) == s, new[v], cur[v]) for v in range(N)]
    for v in range(N):
        x_ref[0, v] = cur[v]
        x_ref[HALF, v] = up(cur[v], 1)
    for m, s in reversed(STEPS):
        mb, slot = (m1, m) if s == 1 else (m2, slot_of(m // 2))
        new = recover(
            mb, slot, m, [x_ref[m + s, v] for v in range(N)], [x_ref[m - s, v] for v in range(N)]
        )
        for v in range(N):
            x_ref[m, v] = new[v]
    low = [x_ref[0, v] for v in range(N)]
    for m in range(HALF):
        inv, fl, fr = scal[m, 0], scal[m, 1], scal[m, 2]
        high = [x_ref[m + 1, v] for v in range(N)]
        ta = mat_vec(a, high)
        tb = mat_vec(b, low)
        for v in range(N):
            odd = inv * (o_ref[m, v] + fr * ta[v] + fl * tb[v])
            x_t.at[v][pl.ds(2 * m, SEG, stride=2 * HALF), :] = low[v]
            x_t.at[v][pl.ds(2 * m + 1, SEG, stride=2 * HALF), :] = odd
        low = high


def backward_first_kernel(
    joint, other_joint, m1, m2, scal, cst, e_ref, o_ref,
    out, za, zb, ta, tb, j_ref, x_ref, x_t,
):
    join(joint, other_joint, j_ref)
    own = [joint[pl.ds(VEC_ROW + v, 1), :] for v in range(N)]
    other = [other_joint[pl.ds(VEC_ROW + v, 1), :] for v in range(N)]
    backward_body(own, other, j_ref, m1, m2, scal, cst, e_ref, o_ref, x_ref, x_t)
    _, planes, sectors, radial = out.shape
    for v in range(N):
        out[v] = x_t[v].T.reshape(planes, sectors, radial)
        pack_edges(out, v, za, zb, ta, tb)


def backward_second_kernel(
    y_own, y_other, j_ref, m1, m2, scal, cst, e_ref, o_ref, first, out, x_ref, x_t
):
    own = [y_own[pl.ds(v, 1), :] for v in range(N)]
    other = [y_other[pl.ds(v, 1), :] for v in range(N)]
    backward_body(own, other, j_ref, m1, m2, scal, cst, e_ref, o_ref, x_ref, x_t)
    _, planes, sectors, radial = out.shape
    for v in range(N):
        out[v] = first[v] + 0.5 * x_t[v].T.reshape(planes, sectors, radial)


def call(kernel, inputs, outs, scratch, us, hbm=False, aliases=None):
    vmem = pl.BlockSpec(memory_space=pltpu.VMEM)
    if hbm:
        inputs = [pltpu.with_memory_space_constraint(x, pltpu.HBM) for x in inputs]
    in_spec = pl.BlockSpec(memory_space=pltpu.HBM) if hbm else vmem
    out_shape = [s if isinstance(s, jax.ShapeDtypeStruct) else jax.ShapeDtypeStruct(s, F32) for s in outs]
    return pl.pallas_call(
        kernel,
        out_shape=out_shape,
        in_specs=[in_spec] * len(inputs),
        out_specs=[vmem] * len(outs),
        scratch_shapes=[pltpu.VMEM(s, F32) if isinstance(s, tuple) else s for s in scratch],
        input_output_aliases=aliases or {},
        compiler_params=pltpu.CompilerParams(vmem_limit_bytes=VMEM_LIMIT),
        cost_estimate=pl.CostEstimate(
            flops=int(us * 1e9), bytes_accessed=int(us * 3e6), transcendentals=0
        ),
    )(*inputs)


def swapped_along(x, axis, odd, wrap):
    size = lax.axis_size(axis)
    pairs = []
    for i in range(odd, size, 2):
        if wrap or i + 1 < size:
            j = (i + 1) % size
            pairs += [(i, j), (j, i)]
    return lax.ppermute(x, axis, pairs)


def halos(za, zb, ta, tb):
    return (
        swapped_along(za, "ax", 0, False),
        swapped_along(zb, "ax", 1, False),
        swapped_along(ta, "az", 0, True),
        swapped_along(tb, "az", 1, True),
    )


def xor_swap(x, bit):
    return lax.ppermute(x, "az", [(i, i ^ bit) for i in range(lax.axis_size("az"))])


def append(low, high):
    (both,) = call(append_kernel, (low, high), [(N, 2 * low.shape[1], low.shape[2])], [], 0.2)
    return both


def after(x, *others):
    return lax.optimization_barrier((x, *others))[0]


def per_device(
    flow_state, radial_coef, blanking, canard_index, canard_table, coupling, upwind_split
):
    comps, planes, sectors, radial = flow_state.shape
    tile = (SEG, LANES)
    half_turn = lax.axis_size("az") // 2
    field = (comps, planes, sectors, radial)
    edges = [(comps, sectors, radial)] * 2 + [(comps, planes, radial)] * 2
    columns = (comps, radial, LANES)
    bits = doubling_bits()

    rows = canard_table[0].transpose(1, 0, 2)
    got = xor_swap(rows, bits[0])
    u, coef, mask, place, cst, *first_edges = call(
        prelude_kernel,
        (flow_state, radial_coef, blanking, canard_index, coupling, upwind_split),
        [
            field,
            (planes, sectors, radial),
            (LANES, radial),
            jax.ShapeDtypeStruct(canard_index.shape, jnp.int32),
            (2, NN) + tile,
        ]
        + edges,
        [
            pltpu.VMEM((planes, sectors, radial), jnp.int32),
            pltpu.VMEM(canard_index.shape, jnp.int32),
            pltpu.SMEM((N, N), F32),
            pltpu.SMEM((N,), F32),
            pltpu.SemaphoreType.DMA((6,)),
        ],
        1.2,
        hbm=True,
    )
    first_halos = halos(*first_edges)
    rows = append(rows, after(got, cst))
    done = {}

    def factor(rows, got):
        done["one"] = call(
            factor_kernel,
            (after(coef, rows), mask, cst),
            [
                (HALF + 1, 3 * NN) + tile,
                (HALF // 2, 2 * NN) + tile,
                (HALF, 3) + tile,
                (JOINT_ROWS, LANES),
                (radial, LANES),
            ],
            [(radial, LANES), (2 * HALF + 1,) + tile, (4, NN) + tile],
            3.2,
        )
        return after(got, done["one"][3])

    def factor_rest(rows, got):
        done["rest"] = call(
            factor_rest_kernel,
            (after(done["one"][0], rows), done["one"][3]),
            [
                (HALF // 2 + 3, 3 * NN) + tile,
                (HALF // 2 + 2, 2 * NN) + tile,
                (JOINT_ROWS, LANES),
            ],
            [],
            3.0,
        )
        return after(got, done["rest"][2], *first_halos[:2])

    def sector_halos(rows, got):
        return after(got, *first_halos[2:])

    fillers = [factor, factor_rest, sector_halos]
    for i, bit in enumerate(bits[1:-1]):
        rows = append(rows, fillers[i](rows, xor_swap(rows, bit)))
    for filler in fillers[len(bits) - 2 :]:
        rows = filler(rows, rows)
    others = xor_swap(rows, bits[-1])
    m1, f1, scal, _, mask_t = done["one"]
    m2, f2, sd = done["rest"]
    (rhs,) = call(
        rhs_kernel, (u, *first_halos, mask, mask_t, place, rows), [columns], [], 1.3
    )
    others = after(others, rhs)

    fwd_outs = [(HALF + 4, N) + tile, (HALF, N) + tile]
    back_scratch = [(HALF + 1, N) + tile, columns]
    e1, o1, joint = call(
        forward_first_kernel,
        (rhs, mask_t, place, others, f1, f2, scal, cst, sd),
        fwd_outs + [(JOINT_ROWS, LANES)],
        [columns],
        1.2,
    )
    other_joint = xor_swap(joint, half_turn)
    first, *second_edges, axis_inverse = call(
        backward_first_kernel,
        (joint, other_joint, m1, m2, scal, cst, e1, o1),
        [field] + edges + [(2 * NN, LANES)],
        back_scratch,
        1.3,
    )
    second_halos = halos(*second_edges)
    e2, o2, y2 = call(
        forward_second_kernel,
        (first, *second_halos, mask, f1, f2, scal, cst),
        fwd_outs + [tile],
        [columns],
        1.3,
    )
    other_y2 = xor_swap(y2, half_turn)
    (update,) = call(
        backward_second_kernel,
        (y2, other_y2, axis_inverse, m1, m2, scal, cst, e2, o2, first),
        [field],
        back_scratch,
        2.0,
    )
    return update


def solution(mesh):
    return jax.shard_map(
        per_device,
        mesh=mesh,
        in_specs=(
            P(None, "ax", "az", None),
            P("ax", "az", None),
            P("ax", "az", None),
            P("ax", "az"),
            P("ax", "az", None, None),
            P(),
            P(),
        ),
        out_specs=P(None, "ax", "az", None),
        check_vma=False,
    )
```

time: 73.1 us -> 66.8 us (0.914)
  starting transfers between devices: 41.3 us -> 24.6 us
  waiting for transfers between devices: 17.6 us -> 27.2 us
    ppermute x10 -> x8, starting transfers between devices: 26.9 us -> 9.01 us  [swapped_along(): return lax.ppermute(x, axis, pairs)]
    ppermute x5 -> x7, waiting for transfers between devices: 1.81 us -> 13.9 us  [xor_swap(): lax.ppermute(x, 'az', [(i, i ^ bit) for i in range(lax.axis_size('az'))])]
    ppermute x10 -> x8, waiting for transfers between devices: 15.8 us -> 13.3 us  [swapped_along(): return lax.ppermute(x, axis, pairs)]
    ppermute x5 -> x7, starting transfers between devices: 14.4 us -> 15.5 us  [xor_swap(): lax.ppermute(x, 'az', [(i, i ^ bit) for i in range(lax.axis_size('az'))])]
    pallas_call x11 -> x12, Pallas kernels: 13.9 us -> 14.1 us  [call(): pl.pallas_call(kernel, out_shape=out_shape, in_specs=[in_spec] * len(inpu...]
  transfers between devices with their start and end apart: 15 -> 15, of which waited for: 7 -> 9; matrix products, arithmetic and copies ran while one was open for 0% -> 0% of each run, Pallas kernels for 8% -> 12%
where the time goes in v2:
time: 66.8 us; the launch traced here: 66 us
  waiting for transfers between devices  27.2 us (41%)
  starting transfers between devices  24.6 us (37%)
  Pallas kernels  14.1 us (21%)
    ppermute x7, starting transfers between devices, xor_swap(): lax.ppermute(x, 'az', [(i, i ^ bit) for i in range(lax.axis_size('az'))])  15.5 us
    pallas_call x12, Pallas kernels, call(): pl.pallas_call(kernel, out_shape=out_shape, in_specs=[in_spec] * len(inpu...  14.1 us
    ppermute x7, waiting for transfers between devices, xor_swap(): lax.ppermute(x, 'az', [(i, i ^ bit) for i in range(lax.axis_size('az'))])  13.9 us
    ppermute x8, waiting for transfers between devices, swapped_along(): return lax.ppermute(x, axis, pairs)  13.3 us
    ppermute x8, starting transfers between devices, swapped_along(): return lax.ppermute(x, axis, pairs)  9.01 us
  transfers between devices with their start and end apart: 15, of which 9 were waited for; matrix products, arithmetic and copies ran while one was open for 0% of the time, Pallas kernels for 12%

profile of v2, /device:TPU:6, one launch (start us, length us, event | category | flops | bytes accessed | tf_op | source)
XLA Modules:
  0.0 66.0 jit_solution(9375401739769577922)
XLA Ops:
  0.0 0.0 copy-start
  0.0 6.3 %collective-permute-start.4 = (f32[5,4,256]{2,1,0:T(4,128)}, f32[5,4,256]{2,1,0:T(4,128)S(1)}, u32[]{:S(2)}, u32[]{:S(2)}) collective-permute-start(f32[5,4,256]{2,1,0:T(4,128)} %bitcast.3), channel_id=1, source_target_pairs={{0,24},{1,25},{2,26},{3,27},{4,28},{5,29},{6,30},{7,31},{8,16},{9,... | collective-permute-start | bytes 61448 | tf_op jit(solution)/shard_map/ppermute | solution.py:554
  6.3 1.3 %shard_map.73 = (f32[5,4,32,256]{3,2,1,0:T(8,128)S(1)}, f32[4,32,256]{2,1,0:T(8,128)S(1)}, f32[128,256]{1,0:T(8,128)S(1)}, s32[4,32]{1,0:T(4,128)S(1)}, f32[2,25...) custom-call(f32[5,4,32,256]{3,2,1,0:T(8,128)} %flow.1, ...), custom_call_target="tpu_custom_call" | custom-call | flops 1200000000 | bytes 3600000 | tf_op jit(solution)/shard_map/pallas_call | solution.py:520
  7.6 1.7 %collective-permute-start = (f32[5,32,256]{2,1,0:T(8,128)S(1)}, f32[5,32,256]{2,1,0:T(8,128)S(1)}, u32[]{:S(2)}, u32[]{:S(2)}) collective-permute-start(f32[5,32,256]{2,1,0:T(8,128)S(1)} %get-tuple-element.42), channel_id=1, source_target_pairs={{0,32},{32,0},{64,96},{96,64},{128,160},{160,128},{192,224},{224,1... | collective-permute-start | bytes 491528 | tf_op jit(solution)/shard_map/ppermute | solution.py:541
  9.2 2.6 %collective-permute-start.1 = (f32[5,32,256]{2,1,0:T(8,128)S(1)}, f32[5,32,256]{2,1,0:T(8,128)S(1)}, u32[]{:S(2)}, u32[]{:S(2)}) collective-permute-start(f32[5,32,256]{2,1,0:T(8,128)S(1)} %get-tuple-element.43), channel_id=1, source_target_pairs={{32,64},{64,32},{96,128},{128,96},{160,192},{192,160},{33,65},{65,... | collective-permute-start | bytes 491528 | tf_op jit(solution)/shard_map/ppermute | solution.py:541
  11.8 0.0 collective-permute-done.4.high
  11.9 0.0 copy-done
  11.9 1.5 %collective-permute-start.5 = (f32[5,8,256]{2,1,0:T(8,128)S(1)}, f32[5,8,256]{2,1,0:T(8,128)S(1)}, u32[]{:S(2)}, u32[]{:S(2)}) collective-permute-start(f32[5,8,256]{2,1,0:T(8,128)S(1)} %shard_map.74.low), channel_id=1, source_target_pairs={{0,8},{1,9},{2,10},{3,11},{4,12},{5,13},{6,14},{7,15},{8,0},{9,1},... | collective-permute-start | bytes 122888 | tf_op jit(solution)/shard_map/ppermute | solution.py:554
  13.4 3.0 %shard_map.75 = (f32[17,75,8,128]{3,2,1,0:T(8,128)S(1)}, f32[8,50,8,128]{3,2,1,0:T(8,128)S(1)}, f32[16,3,8,128]{3,2,1,0:T(8,128)S(1)}, f32[32,128]{1,0:T(8,128)S(1)}, f32[256,128]{1,0:T(8,128)S(1)}) custom-call(f32[4,32,256]{2,1,0:T(8,128)S(1)} %get-tuple-element.50.coef_ref, f32[128,256]{1,0:T(8,128)S(1)} %get-tuple-element.46.mask_ref, ...), custom_call_target="tpu_custom_call" | custom-call | flops 3200000000 | bytes 9600000 | tf_op jit(solution)/shard_map/pallas_call | solution.py:520
  16.5 0.4 collective-permute-done.5.high
  16.9 1.0 %collective-permute-start.6 = (f32[5,16,256]{2,1,0:T(8,128)S(1)}, f32[5,16,256]{2,1,0:T(8,128)S(1)}, u32[]{:S(2)}, u32[]{:S(2)}) collective-permute-start(f32[5,16,256]{2,1,0:T(8,128)S(1)} %shard_map.76.low), channel_id=1, source_target_pairs={{0,4},{1,5},{2,6},{3,7},{4,0},{5,1},{6,2},{7,3},{8,12},{9,13},{10,... | collective-permute-start | bytes 245768 | tf_op jit(solution)/shard_map/ppermute | solution.py:554
  17.9 2.7 %shard_map.77 = (f32[11,75,8,128]{3,2,1,0:T(8,128)S(1)}, f32[10,50,8,128]{3,2,1,0:T(8,128)S(1)}, f32[32,128]{1,0:T(8,128)S(1)}) custom-call(f32[17,75,8,128]{3,2,1,0:T(8,128)S(1)} %get-tuple-element.56.m1, f32[32,128]{1,0:T(8,128)S(1)} %get-tuple-element.53.sd_in), custom_call_target="tpu_custom_call" | custom-call | flops 3000000000 | bytes 9000000 | tf_op jit(solution)/shard_map/pallas_call | solution.py:520
  20.6 0.7 %collective-permute-done.6.high = f32[5,16,256]{2,1,0:T(8,128)S(1)} collective-permute-done((f32[5,16,256]{2,1,0:T(8,128)S(1)}, f32[5,16,256]{2,1,0:T(8,128)S(1)}, u32[]{:S(2)}, u32[]{:S(2)}) %collective-permute-start.6) | collective-permute-done | bytes 81952 | tf_op jit(solution)/shard_map/ppermute | solution.py:554
  21.3 0.0 collective-permute-done.za
  21.3 0.0 collective-permute-done.1.zb
  21.3 3.3 %collective-permute-start.7 = (f32[5,32,256]{2,1,0:T(8,128)S(1)}, f32[5,32,256]{2,1,0:T(8,128)S(1)}, u32[]{:S(2)}, u32[]{:S(2)}) collective-permute-start(f32[5,32,256]{2,1,0:T(8,128)S(1)} %shard_map.78.low), channel_id=1, source_target_pairs={{0,2},{1,3},{2,0},{3,1},{4,6},{5,7},{6,4},{7,5},{8,10},{9,11},{10,... | collective-permute-start | bytes 491528 | tf_op jit(solution)/shard_map/ppermute | solution.py:554
  24.6 0.0 collective-permute-start.2
  24.6 0.0 collective-permute-start.3
  24.6 1.2 %collective-permute-done.2.ta = f32[5,4,256]{2,1,0:T(4,128)S(1)} collective-permute-done((f32[5,4,256]{2,1,0:T(4,128)S(1)}, f32[5,4,256]{2,1,0:T(4,128)S(1)}, u32[]{:S(2)}, u32[]{:S(2)}) %collective-permute-start.2) | collective-permute-done | bytes 20512 | tf_op jit(solution)/shard_map/ppermute | solution.py:541
  25.8 5.6 %collective-permute-done.3.tb = f32[5,4,256]{2,1,0:T(4,128)S(1)} collective-permute-done((f32[5,4,256]{2,1,0:T(4,128)S(1)}, f32[5,4,256]{2,1,0:T(4,128)S(1)}, u32[]{:S(2)}, u32[]{:S(2)}) %collective-permute-start.3) | collective-permute-done | bytes 20512 | tf_op jit(solution)/shard_map/ppermute | solution.py:541
  31.5 0.0 collective-permute-done.7.high
  31.5 0.1 collective-permute-start.8
  31.6 0.9 %shard_map.80.rhs_in = f32[5,256,128]{2,1,0:T(8,128)S(1)} custom-call(f32[5,4,32,256]{3,2,1,0:T(8,128)S(1)} %get-tuple-element.41.u, f32[5,32,256]{2,1,0:T(8,128)S(1)} %collective-permute-done.za, f32[5,32,256]{2,1,0:T(8,128)S(1)} %collective-permute-done.1.zb, f32[5,4,256]{2,1,0:T(4,128)S(1)} %collective-permute-done.2.ta, ...), custom_call_target="tpu_custom_call" | custom-call | flops 1300000000 | bytes 3900000 | tf_op jit(solution)/shard_map/pallas_call | solution.py:520
  32.5 0.7 %collective-permute-done.8.high = f32[5,64,256]{2,1,0:T(8,128)S(1)} collective-permute-done((f32[5,64,256]{2,1,0:T(8,128)S(1)}, f32[5,64,256]{2,1,0:T(8,128)S(1)}, u32[]{:S(2)}, u32[]{:S(2)}) %collective-permute-start.8) | collective-permute-done | bytes 327712 | tf_op jit(solution)/shard_map/ppermute | solution.py:554
  33.2 1.6 %shard_map.81 = (f32[20,5,8,128]{3,2,1,0:T(8,128)S(1)}, f32[16,5,8,128]{3,2,1,0:T(8,128)S(1)}, f32[32,128]{1,0:T(8,128)S(1)}) custom-call(f32[5,256,128]{2,1,0:T(8,128)S(1)} %shard_map.80.rhs_in, f32[256,128]{1,0:T(8,128)S(1)} %get-tuple-element.51.mask_t, s32[4,32]{1,0:T(4,128)S(1)} %get-tuple-element.52.place, ...), custom_call_target="tpu_custom_call" | custom-call | flops 1200000000 | bytes 3600000 | tf_op jit(solution)/shard_map/pallas_call | solution.py:520
  34.8 1.5 %collective-permute-start.9 = (f32[32,128]{1,0:T(8,128)S(1)}, f32[32,128]{1,0:T(8,128)S(1)}, u32[]{:S(2)}, u32[]{:S(2)}) collective-permute-start(f32[32,128]{1,0:T(8,128)S(1)} %get-tuple-element.64.joint), channel_id=1, source_target_pairs={{0,16},{1,17},{2,18},{3,19},{4,20},{5,21},{6,22},{7,23},{8,24},{9,... | collective-permute-start | bytes 49160 | tf_op jit(solution)/shard_map/ppermute | solution.py:554
  36.3 6.2 %collective-permute-done.9.other_joint = f32[32,128]{1,0:T(8,128)S(1)} collective-permute-done((f32[32,128]{1,0:T(8,128)S(1)}, f32[32,128]{1,0:T(8,128)S(1)}, u32[]{:S(2)}, u32[]{:S(2)}) %collective-permute-start.9) | collective-permute-done | bytes 16416 | tf_op jit(solution)/shard_map/ppermute | solution.py:554
  42.5 1.3 %shard_map.82 = (f32[5,4,32,256]{3,2,1,0:T(8,128)S(1)}, f32[5,32,256]{2,1,0:T(8,128)S(1)}, f32[5,32,256]{2,1,0:T(8,128)S(1)}, f32[5,4,256]{2,1,0:T(4,128)S(1)}, ...) custom-call(f32[32,128]{1,0:T(8,128)S(1)} %get-tuple-element.64.joint, f32[32,128]{1,0:T(8,128)S(1)} %collective-permute-done.9.other_joint, ...), custom_call_target="tpu_custom_call" | custom-call | flops 1300000000 | bytes 3900000 | tf_op jit(solution)/shard_map/pallas_call | solution.py:520
  43.8 0.1 collective-permute-start.10
  43.9 3.9 %collective-permute-start.11 = (f32[5,32,256]{2,1,0:T(8,128)S(1)}, f32[5,32,256]{2,1,0:T(8,128)S(1)}, u32[]{:S(2)}, u32[]{:S(2)}) collective-permute-start(f32[5,32,256]{2,1,0:T(8,128)S(1)} %get-tuple-element.70), channel_id=1, source_target_pairs={{32,64},{64,32},{96,128},{128,96},{160,192},{192,160},{33,65},{65,... | collective-permute-start | bytes 491528 | tf_op jit(solution)/shard_map/ppermute | solution.py:541
  47.8 0.1 collective-permute-start.12
  47.9 0.7 %collective-permute-start.13 = (f32[5,4,256]{2,1,0:T(4,128)S(1)}, f32[5,4,256]{2,1,0:T(4,128)S(1)}, u32[]{:S(2)}, u32[]{:S(2)}) collective-permute-start(f32[5,4,256]{2,1,0:T(4,128)S(1)} %get-tuple-element.72), channel_id=1, source_target_pairs={{1,2},{2,1},{3,4},{4,3},{5,6},{6,5},{7,8},{8,7},{9,10},{10,9},{11,... | collective-permute-start | bytes 61448 | tf_op jit(solution)/shard_map/ppermute | solution.py:541
  48.6 0.5 collective-permute-done.12.ta
  49.1 5.9 %collective-permute-done.13.tb = f32[5,4,256]{2,1,0:T(4,128)S(1)} collective-permute-done((f32[5,4,256]{2,1,0:T(4,128)S(1)}, f32[5,4,256]{2,1,0:T(4,128)S(1)}, u32[]{:S(2)}, u32[]{:S(2)}) %collective-permute-start.13) | collective-permute-done | bytes 20512 | tf_op jit(solution)/shard_map/ppermute | solution.py:541
  55.0 0.0 collective-permute-done.10.za
  55.0 0.0 collective-permute-done.11.zb
  55.0 1.3 %shard_map.83 = (f32[20,5,8,128]{3,2,1,0:T(8,128)S(1)}, f32[16,5,8,128]{3,2,1,0:T(8,128)S(1)}, f32[8,128]{1,0:T(8,128)S(1)}) custom-call(f32[5,4,32,256]{3,2,1,0:T(8,128)S(1)} %get-tuple-element.68.u.first, f32[5,32,256]{2,1,0:T(8,128)S(1)} %collective-permute-done.10.za, f32[5,32,256]{2,1,0:T(8,128)S(1)} %collective-permute-done.11.zb, ...), custom_call_target="tpu_custom_call" | custom-call | flops 1300000000 | bytes 3900000 | tf_op jit(solution)/shard_map/pallas_call | solution.py:520
  56.4 1.8 %collective-permute-start.14 = (f32[8,128]{1,0:T(8,128)S(1)}, f32[8,128]{1,0:T(8,128)S(1)}, u32[]{:S(2)}, u32[]{:S(2)}) collective-permute-start(f32[8,128]{1,0:T(8,128)S(1)} %get-tuple-element.73.y_own), channel_id=1, source_target_pairs={{0,16},{1,17},{2,18},{3,19},{4,20},{5,21},{6,22},{7,23},{8,24},{9,... | collective-permute-start | bytes 12296 | tf_op jit(solution)/shard_map/ppermute | solution.py:554
  58.2 5.8 %collective-permute-done.14.y_other = f32[8,128]{1,0:T(8,128)S(1)} collective-permute-done((f32[8,128]{1,0:T(8,128)S(1)}, f32[8,128]{1,0:T(8,128)S(1)}, u32[]{:S(2)}, u32[]{:S(2)}) %collective-permute-start.14) | collective-permute-done | bytes 4128 | tf_op jit(solution)/shard_map/ppermute | solution.py:554
  64.0 2.0 %shard_map.84 = f32[5,4,32,256]{3,2,1,0:T(8,128)} custom-call(f32[8,128]{1,0:T(8,128)S(1)} %get-tuple-element.73.y_own, f32[8,128]{1,0:T(8,128)S(1)} %collective-permute-done.14.y_other, f32[50,128]{1,0:T(8,128)S(1)} %get-tuple-element.74.j_ref, f32[17,75,8,128]{3,2,1,0:T(8,128)S(1)} %get-tuple-element.56.m1, f32[11,75,8,128]{3,2,1,0:T(8,128)S(1)} %get-tuple-element.65.m2, ...), custom_call_target="tpu_custom_call" | custom-call | flops 2000000000 | bytes 6000000 | tf_op jit(solution)/shard_map/pallas_call | solution.py:520
  (4 shorter events, 0.0 us)
Async XLA Ops:
  0.0 11.9 %copy-start = (f32[1,4,5,256]{3,1,2,0:T(4,128)S(1)}, f32[1,4,5,256]{3,1,2,0:T(4,128)}, u32[]{:S(2)}) copy-start(f32[1,4,5,256]{3,1,2,0:T(4,128)} %param.11) | copy-start | bytes 61444
  0.0 11.8 %collective-permute-start.4 = (f32[5,4,256]{2,1,0:T(4,128)}, f32[5,4,256]{2,1,0:T(4,128)S(1)}, u32[]{:S(2)}, u32[]{:S(2)}) collective-permute-start(f32[5,4,256]{2,1,0:T(4,128)} %bitcast.3), channel_id=1, source_target_pairs={{0,24},{1,25},{2,26},{3,27},{4,28},{5,29},{6,30},{7,31},{8,16},{9,... | collective-permute-start | bytes 61448 | tf_op jit(solution)/shard_map/ppermute | solution.py:554
  7.6 13.8 %collective-permute-start = (f32[5,32,256]{2,1,0:T(8,128)S(1)}, f32[5,32,256]{2,1,0:T(8,128)S(1)}, u32[]{:S(2)}, u32[]{:S(2)}) collective-permute-start(f32[5,32,256]{2,1,0:T(8,128)S(1)} %get-tuple-element.42), channel_id=1, source_target_pairs={{0,32},{32,0},{64,96},{96,64},{128,160},{160,128},{192,224},{224,1... | collective-permute-start | bytes 491528 | tf_op jit(solution)/shard_map/ppermute | solution.py:541
  9.2 12.1 %collective-permute-start.1 = (f32[5,32,256]{2,1,0:T(8,128)S(1)}, f32[5,32,256]{2,1,0:T(8,128)S(1)}, u32[]{:S(2)}, u32[]{:S(2)}) collective-permute-start(f32[5,32,256]{2,1,0:T(8,128)S(1)} %get-tuple-element.43), channel_id=1, source_target_pairs={{32,64},{64,32},{96,128},{128,96},{160,192},{192,160},{33,65},{65,... | collective-permute-start | bytes 491528 | tf_op jit(solution)/shard_map/ppermute | solution.py:541
  11.9 5.0 %collective-permute-start.5 = (f32[5,8,256]{2,1,0:T(8,128)S(1)}, f32[5,8,256]{2,1,0:T(8,128)S(1)}, u32[]{:S(2)}, u32[]{:S(2)}) collective-permute-start(f32[5,8,256]{2,1,0:T(8,128)S(1)} %shard_map.74.low), channel_id=1, source_target_pairs={{0,8},{1,9},{2,10},{3,11},{4,12},{5,13},{6,14},{7,15},{8,0},{9,1},... | collective-permute-start | bytes 122888 | tf_op jit(solution)/shard_map/ppermute | solution.py:554
  16.9 4.4 %collective-permute-start.6 = (f32[5,16,256]{2,1,0:T(8,128)S(1)}, f32[5,16,256]{2,1,0:T(8,128)S(1)}, u32[]{:S(2)}, u32[]{:S(2)}) collective-permute-start(f32[5,16,256]{2,1,0:T(8,128)S(1)} %shard_map.76.low), channel_id=1, source_target_pairs={{0,4},{1,5},{2,6},{3,7},{4,0},{5,1},{6,2},{7,3},{8,12},{9,13},{10,... | collective-permute-start | bytes 245768 | tf_op jit(solution)/shard_map/ppermute | solution.py:554
  21.3 10.1 %collective-permute-start.7 = (f32[5,32,256]{2,1,0:T(8,128)S(1)}, f32[5,32,256]{2,1,0:T(8,128)S(1)}, u32[]{:S(2)}, u32[]{:S(2)}) collective-permute-start(f32[5,32,256]{2,1,0:T(8,128)S(1)} %shard_map.78.low), channel_id=1, source_target_pairs={{0,2},{1,3},{2,0},{3,1},{4,6},{5,7},{6,4},{7,5},{8,10},{9,11},{10,... | collective-permute-start | bytes 491528 | tf_op jit(solution)/shard_map/ppermute | solution.py:554
  24.6 1.2 %collective-permute-start.2 = (f32[5,4,256]{2,1,0:T(4,128)S(1)}, f32[5,4,256]{2,1,0:T(4,128)S(1)}, u32[]{:S(2)}, u32[]{:S(2)}) collective-permute-start(f32[5,4,256]{2,1,0:T(4,128)S(1)} %get-tuple-element.44), channel_id=1, source_target_pairs={{0,1},{1,0},{2,3},{3,2},{4,5},{5,4},{6,7},{7,6},{8,9},{9,8},{10,11... | collective-permute-start | bytes 61448 | tf_op jit(solution)/shard_map/ppermute | solution.py:541
  24.6 6.8 %collective-permute-start.3 = (f32[5,4,256]{2,1,0:T(4,128)S(1)}, f32[5,4,256]{2,1,0:T(4,128)S(1)}, u32[]{:S(2)}, u32[]{:S(2)}) collective-permute-start(f32[5,4,256]{2,1,0:T(4,128)S(1)} %get-tuple-element.45), channel_id=1, source_target_pairs={{1,2},{2,1},{3,4},{4,3},{5,6},{6,5},{7,8},{8,7},{9,10},{10,9},{11,... | collective-permute-start | bytes 61448 | tf_op jit(solution)/shard_map/ppermute | solution.py:541
  31.5 1.7 %collective-permute-start.8 = (f32[5,64,256]{2,1,0:T(8,128)S(1)}, f32[5,64,256]{2,1,0:T(8,128)S(1)}, u32[]{:S(2)}, u32[]{:S(2)}) collective-permute-start(f32[5,64,256]{2,1,0:T(8,128)S(1)} %shard_map.79.low), channel_id=1, source_target_pairs={{0,1},{1,0},{2,3},{3,2},{4,5},{5,4},{6,7},{7,6},{8,9},{9,8},{10,11... | collective-permute-start | bytes 983048 | tf_op jit(solution)/shard_map/ppermute | solution.py:554
  34.8 7.7 %collective-permute-start.9 = (f32[32,128]{1,0:T(8,128)S(1)}, f32[32,128]{1,0:T(8,128)S(1)}, u32[]{:S(2)}, u32[]{:S(2)}) collective-permute-start(f32[32,128]{1,0:T(8,128)S(1)} %get-tuple-element.64.joint), channel_id=1, source_target_pairs={{0,16},{1,17},{2,18},{3,19},{4,20},{5,21},{6,22},{7,23},{8,24},{9,... | collective-permute-start | bytes 49160 | tf_op jit(solution)/shard_map/ppermute | solution.py:554
  43.8 11.2 %collective-permute-start.10 = (f32[5,32,256]{2,1,0:T(8,128)S(1)}, f32[5,32,256]{2,1,0:T(8,128)S(1)}, u32[]{:S(2)}, u32[]{:S(2)}) collective-permute-start(f32[5,32,256]{2,1,0:T(8,128)S(1)} %get-tuple-element.69), channel_id=1, source_target_pairs={{0,32},{32,0},{64,96},{96,64},{128,160},{160,128},{192,224},{224,1... | collective-permute-start | bytes 491528 | tf_op jit(solution)/shard_map/ppermute | solution.py:541
  43.9 11.1 %collective-permute-start.11 = (f32[5,32,256]{2,1,0:T(8,128)S(1)}, f32[5,32,256]{2,1,0:T(8,128)S(1)}, u32[]{:S(2)}, u32[]{:S(2)}) collective-permute-start(f32[5,32,256]{2,1,0:T(8,128)S(1)} %get-tuple-element.70), channel_id=1, source_target_pairs={{32,64},{64,32},{96,128},{128,96},{160,192},{192,160},{33,65},{65,... | collective-permute-start | bytes 491528 | tf_op jit(solution)/shard_map/ppermute | solution.py:541
  47.8 1.3 %collective-permute-start.12 = (f32[5,4,256]{2,1,0:T(4,128)S(1)}, f32[5,4,256]{2,1,0:T(4,128)S(1)}, u32[]{:S(2)}, u32[]{:S(2)}) collective-permute-start(f32[5,4,256]{2,1,0:T(4,128)S(1)} %get-tuple-element.71), channel_id=1, source_target_pairs={{0,1},{1,0},{2,3},{3,2},{4,5},{5,4},{6,7},{7,6},{8,9},{9,8},{10,11... | collective-permute-start | bytes 61448 | tf_op jit(solution)/shard_map/ppermute | solution.py:541
  47.9 7.1 %collective-permute-start.13 = (f32[5,4,256]{2,1,0:T(4,128)S(1)}, f32[5,4,256]{2,1,0:T(4,128)S(1)}, u32[]{:S(2)}, u32[]{:S(2)}) collective-permute-start(f32[5,4,256]{2,1,0:T(4,128)S(1)} %get-tuple-element.72), channel_id=1, source_target_pairs={{1,2},{2,1},{3,4},{4,3},{5,6},{6,5},{7,8},{8,7},{9,10},{10,9},{11,... | collective-permute-start | bytes 61448 | tf_op jit(solution)/shard_map/ppermute | solution.py:541
  56.4 7.6 %collective-permute-start.14 = (f32[8,128]{1,0:T(8,128)S(1)}, f32[8,128]{1,0:T(8,128)S(1)}, u32[]{:S(2)}, u32[]{:S(2)}) collective-permute-start(f32[8,128]{1,0:T(8,128)S(1)} %get-tuple-element.73.y_own), channel_id=1, source_target_pairs={{0,16},{1,17},{2,18},{3,19},{4,20},{5,21},{6,22},{7,23},{8,24},{9,... | collective-permute-start | bytes 12296 | tf_op jit(solution)/shard_map/ppermute | solution.py:554

commit v3 on v2

--- a/solution.py
+++ b/solution.py
@@ -96,7 +96,15 @@
     return lax.axis_index(axis) % 2 == 0
 
 
-def pack_edges(field, v, za, zb, ta, tb):
+def pack_far_sector(field, v, tb):
+    _, planes, sectors, _ = field.shape
+    up = is_even("az")
+    for z in range(planes):
+        first, last = field[v, z, pl.ds(0, 1), :], field[v, z, pl.ds(sectors - 1, 1), :]
+        tb[v, pl.ds(z, 1), :] = jnp.where(up, first, last)
+
+
+def pack_edges(field, v, za, zb, ta):
     _, planes, sectors, _ = field.shape
     z_up, t_up = is_even("ax"), is_even("az")
     za[v] = field[v, jnp.where(z_up, planes - 1, 0)]
@@ -104,7 +112,6 @@
     for z in range(planes):
         first, last = field[v, z, pl.ds(0, 1), :], field[v, z, pl.ds(sectors - 1, 1), :]
         ta[v, pl.ds(z, 1), :] = jnp.where(t_up, last, first)
-        tb[v, pl.ds(z, 1), :] = jnp.where(t_up, first, last)
 
 
 def prelude_kernel(
@@ -136,7 +143,8 @@
     copies[5].wait()
     copies[0].wait()
     for v in range(N):
-        pack_edges(u, v, za, zb, ta, tb)
+        pack_edges(u, v, za, zb, ta)
+        pack_far_sector(u, v, tb)
 
 
 def append_kernel(low, high, out):
@@ -429,7 +437,7 @@
 
 
 def forward_second_kernel(
-    u, za, zb, ta, tb, mask_ref, f1, f2, scal, cst, e_ref, o_ref, y_ref, rhs_t
+    u, za, zb, tb, ta, mask_ref, f1, f2, scal, cst, e_ref, o_ref, y_ref, rhs_t
 ):
     planes = u.shape[1]
     mask = mask_ref[...]
@@ -497,21 +505,26 @@
     _, planes, sectors, radial = out.shape
     for v in range(N):
         out[v] = x_t[v].T.reshape(planes, sectors, radial)
-        pack_edges(out, v, za, zb, ta, tb)
+        pack_edges(out, v, za, zb, ta)
+        pack_far_sector(out, v, tb)
 
 
 def backward_second_kernel(
-    y_own, y_other, j_ref, m1, m2, scal, cst, e_ref, o_ref, first, out, x_ref, x_t
+    y_own, y_other, j_ref, m1, m2, scal, cst, e_ref, o_ref, first, out, x_ref, x_t, stage, sem
 ):
     own = [y_own[pl.ds(v, 1), :] for v in range(N)]
     other = [y_other[pl.ds(v, 1), :] for v in range(N)]
     backward_body(own, other, j_ref, m1, m2, scal, cst, e_ref, o_ref, x_ref, x_t)
     _, planes, sectors, radial = out.shape
-    for v in range(N):
-        out[v] = first[v] + 0.5 * x_t[v].T.reshape(planes, sectors, radial)
-
-
-def call(kernel, inputs, outs, scratch, us, hbm=False, aliases=None):
+    copies = [pltpu.make_async_copy(stage.at[v], out.at[v], sem.at[v]) for v in range(N)]
+    for v in range(N):
+        stage[v] = first[v] + 0.5 * x_t[v].T.reshape(planes, sectors, radial)
+        copies[v].start()
+    for copy in copies:
+        copy.wait()
+
+
+def call(kernel, inputs, outs, scratch, us, hbm=False, out_hbm=False):
     vmem = pl.BlockSpec(memory_space=pltpu.VMEM)
     if hbm:
         inputs = [pltpu.with_memory_space_constraint(x, pltpu.HBM) for x in inputs]
@@ -521,9 +534,8 @@
         kernel,
         out_shape=out_shape,
         in_specs=[in_spec] * len(inputs),
-        out_specs=[vmem] * len(outs),
+        out_specs=[pl.BlockSpec(memory_space=pltpu.HBM) if out_hbm else vmem] * len(outs),
         scratch_shapes=[pltpu.VMEM(s, F32) if isinstance(s, tuple) else s for s in scratch],
-        input_output_aliases=aliases or {},
         compiler_params=pltpu.CompilerParams(vmem_limit_bytes=VMEM_LIMIT),
         cost_estimate=pl.CostEstimate(
             flops=int(us * 1e9), bytes_accessed=int(us * 3e6), transcendentals=0
@@ -541,13 +553,20 @@
     return lax.ppermute(x, axis, pairs)
 
 
-def halos(za, zb, ta, tb):
-    return (
-        swapped_along(za, "ax", 0, False),
-        swapped_along(zb, "ax", 1, False),
-        swapped_along(ta, "az", 0, True),
-        swapped_along(tb, "az", 1, True),
-    )
+def z_near(x):
+    return swapped_along(x, "ax", 0, False)
+
+
+def z_far(x):
+    return swapped_along(x, "ax", 1, False)
+
+
+def t_near(x):
+    return swapped_along(x, "az", 0, True)
+
+
+def t_far(x):
+    return swapped_along(x, "az", 1, True)
 
 
 def xor_swap(x, bit):
@@ -576,7 +595,7 @@
 
     rows = canard_table[0].transpose(1, 0, 2)
     got = xor_swap(rows, bits[0])
-    u, coef, mask, place, cst, *first_edges = call(
+    u, coef, mask, place, cst, za, zb, ta, tb = call(
         prelude_kernel,
         (flow_state, radial_coef, blanking, canard_index, coupling, upwind_split),
         [
@@ -597,7 +616,7 @@
         1.2,
         hbm=True,
     )
-    first_halos = halos(*first_edges)
+    first = {"zb": z_far(zb)}
     rows = append(rows, after(got, cst))
     done = {}
 
@@ -617,7 +636,13 @@
         )
         return after(got, done["one"][3])
 
+    def far_halos(rows, got):
+        first["tb"] = t_far(after(tb, rows))
+        first["za"] = z_near(after(za, rows))
+        return after(got, first["zb"])
+
     def factor_rest(rows, got):
+        first["ta"] = t_near(after(ta, rows))
         done["rest"] = call(
             factor_rest_kernel,
             (after(done["one"][0], rows), done["one"][3]),
@@ -629,12 +654,9 @@
             [],
             3.0,
         )
-        return after(got, done["rest"][2], *first_halos[:2])
-
-    def sector_halos(rows, got):
-        return after(got, *first_halos[2:])
-
-    fillers = [factor, factor_rest, sector_halos]
+        return after(got, done["rest"][2], first["za"], first["ta"], first["tb"])
+
+    fillers = [factor, far_halos, factor_rest]
     for i, bit in enumerate(bits[1:-1]):
         rows = append(rows, fillers[i](rows, xor_swap(rows, bit)))
     for filler in fillers[len(bits) - 2 :]:
@@ -643,7 +665,11 @@
     m1, f1, scal, _, mask_t = done["one"]
     m2, f2, sd = done["rest"]
     (rhs,) = call(
-        rhs_kernel, (u, *first_halos, mask, mask_t, place, rows), [columns], [], 1.3
+        rhs_kernel,
+        (u, first["za"], first["zb"], first["ta"], first["tb"], mask, mask_t, place, rows),
+        [columns],
+        [],
+        1.3,
     )
     others = after(others, rhs)
 
@@ -657,17 +683,17 @@
         1.2,
     )
     other_joint = xor_swap(joint, half_turn)
-    first, *second_edges, axis_inverse = call(
+    delta, za, zb, ta, tb, axis_inverse = call(
         backward_first_kernel,
         (joint, other_joint, m1, m2, scal, cst, e1, o1),
         [field] + edges + [(2 * NN, LANES)],
         back_scratch,
         1.3,
     )
-    second_halos = halos(*second_edges)
+    tb, zb, za, ta = t_far(tb), z_far(zb), z_near(za), t_near(ta)
     e2, o2, y2 = call(
         forward_second_kernel,
-        (first, *second_halos, mask, f1, f2, scal, cst),
+        (delta, za, zb, tb, ta, mask, f1, f2, scal, cst),
         fwd_outs + [tile],
         [columns],
         1.3,
@@ -675,10 +701,11 @@
     other_y2 = xor_swap(y2, half_turn)
     (update,) = call(
         backward_second_kernel,
-        (y2, other_y2, axis_inverse, m1, m2, scal, cst, e2, o2, first),
+        (y2, other_y2, axis_inverse, m1, m2, scal, cst, e2, o2, delta),
         [field],
-        back_scratch,
+        back_scratch + [field, pltpu.SemaphoreType.DMA((N,))],
         2.0,
+        out_hbm=True,
     )
     return update
 

time: 66.8 us -> 64.6 us (0.967)
  waiting for transfers between devices: 27.2 us -> 21.6 us
  starting transfers between devices: 24.6 us -> 28.6 us
    ppermute x8, waiting for transfers between devices: 13.3 us -> 5.33 us  [swapped_along(): return lax.ppermute(x, axis, pairs)]
    ppermute x8, starting transfers between devices: 9.01 us -> 11.6 us  [swapped_along(): return lax.ppermute(x, axis, pairs)]
    ppermute x7, waiting for transfers between devices: 13.9 us -> 16.2 us  [xor_swap(): lax.ppermute(x, 'az', [(i, i ^ bit) for i in range(lax.axis_size('az'))])]
    ppermute x7, starting transfers between devices: 15.5 us -> 17 us  [xor_swap(): lax.ppermute(x, 'az', [(i, i ^ bit) for i in range(lax.axis_size('az'))])]
  transfers between devices with their start and end apart: 15 -> 15, of which waited for: 9 -> 7; matrix products, arithmetic and copies ran while one was open for 0% -> 0% of each run, Pallas kernels for 12% -> 12%
where the time goes in v3:
time: 64.6 us; the launch traced here: 64.4 us
  starting transfers between devices  28.6 us (44%)
  waiting for transfers between devices  21.6 us (33%)
  Pallas kernels  14 us (22%)
    ppermute x7, starting transfers between devices, xor_swap(): lax.ppermute(x, 'az', [(i, i ^ bit) for i in range(lax.axis_size('az'))])  17 us
    ppermute x7, waiting for transfers between devices, xor_swap(): lax.ppermute(x, 'az', [(i, i ^ bit) for i in range(lax.axis_size('az'))])  16.2 us
    pallas_call x12, Pallas kernels, call(): pl.pallas_call(kernel, out_shape=out_shape, in_specs=[in_spec] * len(inpu...  14 us
    ppermute x8, starting transfers between devices, swapped_along(): return lax.ppermute(x, axis, pairs)  11.6 us
    ppermute x8, waiting for transfers between devices, swapped_along(): return lax.ppermute(x, axis, pairs)  5.33 us
  transfers between devices with their start and end apart: 15, of which 7 were waited for; matrix products, arithmetic and copies ran while one was open for 0% of the time, Pallas kernels for 12%

profile of v3, /device:TPU:6, one launch (start us, length us, event | category | flops | bytes accessed | tf_op | source)
XLA Modules:
  0.0 64.4 jit_solution(11180986953561567430)
XLA Ops:
  0.0 0.0 copy-start
  0.0 6.3 %collective-permute-start = (f32[5,4,256]{2,1,0:T(4,128)}, f32[5,4,256]{2,1,0:T(4,128)S(1)}, u32[]{:S(2)}, u32[]{:S(2)}) collective-permute-start(f32[5,4,256]{2,1,0:T(4,128)} %bitcast.3), channel_id=1, source_target_pairs={{0,24},{1,25},{2,26},{3,27},{4,28},{5,29},{6,30},{7,31},{8,16},{9,... | collective-permute-start | bytes 61448 | tf_op jit(solution)/shard_map/ppermute | solution.py:573
  6.3 1.3 %shard_map.73 = (f32[5,4,32,256]{3,2,1,0:T(8,128)S(1)}, f32[4,32,256]{2,1,0:T(8,128)S(1)}, f32[128,256]{1,0:T(8,128)S(1)}, s32[4,32]{1,0:T(4,128)S(1)}, f32[2,25...) custom-call(f32[5,4,32,256]{3,2,1,0:T(8,128)} %flow.1, ...), custom_call_target="tpu_custom_call" | custom-call | flops 1200000000 | bytes 3600000 | tf_op jit(solution)/shard_map/pallas_call | solution.py:533
  7.6 3.8 %collective-permute-start.3 = (f32[5,32,256]{2,1,0:T(8,128)S(1)}, f32[5,32,256]{2,1,0:T(8,128)S(1)}, u32[]{:S(2)}, u32[]{:S(2)}) collective-permute-start(f32[5,32,256]{2,1,0:T(8,128)S(1)} %get-tuple-element.54), channel_id=1, source_target_pairs={{32,64},{64,32},{96,128},{128,96},{160,192},{192,160},{33,65},{65,... | collective-permute-start | bytes 491528 | tf_op jit(solution)/shard_map/ppermute | solution.py:553
  11.3 0.0 collective-permute-done.high
  11.3 0.0 copy-done
  11.4 1.5 %collective-permute-start.1 = (f32[5,8,256]{2,1,0:T(8,128)S(1)}, f32[5,8,256]{2,1,0:T(8,128)S(1)}, u32[]{:S(2)}, u32[]{:S(2)}) collective-permute-start(f32[5,8,256]{2,1,0:T(8,128)S(1)} %shard_map.74.low), channel_id=1, source_target_pairs={{0,8},{1,9},{2,10},{3,11},{4,12},{5,13},{6,14},{7,15},{8,0},{9,1},... | collective-permute-start | bytes 122888 | tf_op jit(solution)/shard_map/ppermute | solution.py:573
  12.9 3.0 %shard_map.75 = (f32[17,75,8,128]{3,2,1,0:T(8,128)S(1)}, f32[8,50,8,128]{3,2,1,0:T(8,128)S(1)}, f32[16,3,8,128]{3,2,1,0:T(8,128)S(1)}, f32[32,128]{1,0:T(8,128)S(1)}, f32[256,128]{1,0:T(8,128)S(1)}) custom-call(f32[4,32,256]{2,1,0:T(8,128)S(1)} %get-tuple-element.49.coef_ref, f32[128,256]{1,0:T(8,128)S(1)} %get-tuple-element.50.mask_ref, ...), custom_call_target="tpu_custom_call" | custom-call | flops 3200000000 | bytes 9600000 | tf_op jit(solution)/shard_map/pallas_call | solution.py:533
  15.9 0.4 collective-permute-done.1.high
  16.4 1.0 %collective-permute-start.4 = (f32[5,16,256]{2,1,0:T(8,128)S(1)}, f32[5,16,256]{2,1,0:T(8,128)S(1)}, u32[]{:S(2)}, u32[]{:S(2)}) collective-permute-start(f32[5,16,256]{2,1,0:T(8,128)S(1)} %shard_map.76.low), channel_id=1, source_target_pairs={{0,4},{1,5},{2,6},{3,7},{4,0},{5,1},{6,2},{7,3},{8,12},{9,13},{10,... | collective-permute-start | bytes 245768 | tf_op jit(solution)/shard_map/ppermute | solution.py:573
  17.4 0.7 %collective-permute-start.6 = (f32[5,4,256]{2,1,0:T(4,128)S(1)}, f32[5,4,256]{2,1,0:T(4,128)S(1)}, u32[]{:S(2)}, u32[]{:S(2)}) collective-permute-start(f32[5,4,256]{2,1,0:T(4,128)S(1)} %get-tuple-element.59), channel_id=1, source_target_pairs={{1,2},{2,1},{3,4},{4,3},{5,6},{6,5},{7,8},{8,7},{9,10},{10,9},{11,... | collective-permute-start | bytes 61448 | tf_op jit(solution)/shard_map/ppermute | solution.py:553
  18.0 0.7 %collective-permute-start.2 = (f32[5,32,256]{2,1,0:T(8,128)S(1)}, f32[5,32,256]{2,1,0:T(8,128)S(1)}, u32[]{:S(2)}, u32[]{:S(2)}) collective-permute-start(f32[5,32,256]{2,1,0:T(8,128)S(1)} %get-tuple-element.53), channel_id=1, source_target_pairs={{0,32},{32,0},{64,96},{96,64},{128,160},{160,128},{192,224},{224,1... | collective-permute-start | bytes 491528 | tf_op jit(solution)/shard_map/ppermute | solution.py:553
  18.7 2.1 %collective-permute-done.4.high = f32[5,16,256]{2,1,0:T(8,128)S(1)} collective-permute-done((f32[5,16,256]{2,1,0:T(8,128)S(1)}, f32[5,16,256]{2,1,0:T(8,128)S(1)}, u32[]{:S(2)}, u32[]{:S(2)}) %collective-permute-start.4) | collective-permute-done | bytes 81952 | tf_op jit(solution)/shard_map/ppermute | solution.py:573
  20.8 0.0 collective-permute-done.3.zb
  20.8 3.0 %collective-permute-start.7 = (f32[5,32,256]{2,1,0:T(8,128)S(1)}, f32[5,32,256]{2,1,0:T(8,128)S(1)}, u32[]{:S(2)}, u32[]{:S(2)}) collective-permute-start(f32[5,32,256]{2,1,0:T(8,128)S(1)} %shard_map.77.low), channel_id=1, source_target_pairs={{0,2},{1,3},{2,0},{3,1},{4,6},{5,7},{6,4},{7,5},{8,10},{9,11},{10,... | collective-permute-start | bytes 491528 | tf_op jit(solution)/shard_map/ppermute | solution.py:573
  23.8 0.0 collective-permute-start.5
  23.8 2.7 %shard_map.78 = (f32[11,75,8,128]{3,2,1,0:T(8,128)S(1)}, f32[10,50,8,128]{3,2,1,0:T(8,128)S(1)}, f32[32,128]{1,0:T(8,128)S(1)}) custom-call(f32[17,75,8,128]{3,2,1,0:T(8,128)S(1)} %get-tuple-element.63.m1, f32[32,128]{1,0:T(8,128)S(1)} %get-tuple-element.51.sd_in), custom_call_target="tpu_custom_call" | custom-call | flops 3000000000 | bytes 9000000 | tf_op jit(solution)/shard_map/pallas_call | solution.py:533
  26.5 0.0 collective-permute-done.6.tb
  26.5 0.0 collective-permute-done.5.ta
  26.5 0.0 collective-permute-done.2.za
  26.5 2.8 %collective-permute-done.7.high = f32[5,32,256]{2,1,0:T(8,128)S(1)} collective-permute-done((f32[5,32,256]{2,1,0:T(8,128)S(1)}, f32[5,32,256]{2,1,0:T(8,128)S(1)}, u32[]{:S(2)}, u32[]{:S(2)}) %collective-permute-start.7) | collective-permute-done | bytes 163872 | tf_op jit(solution)/shard_map/ppermute | solution.py:573
  29.3 0.1 collective-permute-start.8
  29.4 0.9 %shard_map.80.rhs_in = f32[5,256,128]{2,1,0:T(8,128)S(1)} custom-call(f32[5,4,32,256]{3,2,1,0:T(8,128)S(1)} %get-tuple-element.44.u, f32[5,32,256]{2,1,0:T(8,128)S(1)} %collective-permute-done.2.za, f32[5,32,256]{2,1,0:T(8,128)S(1)} %collective-permute-done.3.zb, f32[5,4,256]{2,1,0:T(4,128)S(1)} %collective-permute-done.5.ta, ...), custom_call_target="tpu_custom_call" | custom-call | flops 1300000000 | bytes 3900000 | tf_op jit(solution)/shard_map/pallas_call | solution.py:533
  30.3 0.7 %collective-permute-done.8.high = f32[5,64,256]{2,1,0:T(8,128)S(1)} collective-permute-done((f32[5,64,256]{2,1,0:T(8,128)S(1)}, f32[5,64,256]{2,1,0:T(8,128)S(1)}, u32[]{:S(2)}, u32[]{:S(2)}) %collective-permute-start.8) | collective-permute-done | bytes 327712 | tf_op jit(solution)/shard_map/ppermute | solution.py:573
  31.0 1.6 %shard_map.81 = (f32[20,5,8,128]{3,2,1,0:T(8,128)S(1)}, f32[16,5,8,128]{3,2,1,0:T(8,128)S(1)}, f32[32,128]{1,0:T(8,128)S(1)}) custom-call(f32[5,256,128]{2,1,0:T(8,128)S(1)} %shard_map.80.rhs_in, f32[256,128]{1,0:T(8,128)S(1)} %get-tuple-element.60.mask_t, s32[4,32]{1,0:T(4,128)S(1)} %get-tuple-element.61.place, ...), custom_call_target="tpu_custom_call" | custom-call | flops 1200000000 | bytes 3600000 | tf_op jit(solution)/shard_map/pallas_call | solution.py:533
  32.6 2.9 %collective-permute-start.9 = (f32[32,128]{1,0:T(8,128)S(1)}, f32[32,128]{1,0:T(8,128)S(1)}, u32[]{:S(2)}, u32[]{:S(2)}) collective-permute-start(f32[32,128]{1,0:T(8,128)S(1)} %get-tuple-element.70.joint), channel_id=1, source_target_pairs={{0,16},{1,17},{2,18},{3,19},{4,20},{5,21},{6,22},{7,23},{8,24},{9,... | collective-permute-start | bytes 49160 | tf_op jit(solution)/shard_map/ppermute | solution.py:573
  35.5 4.9 %collective-permute-done.9.other_joint = f32[32,128]{1,0:T(8,128)S(1)} collective-permute-done((f32[32,128]{1,0:T(8,128)S(1)}, f32[32,128]{1,0:T(8,128)S(1)}, u32[]{:S(2)}, u32[]{:S(2)}) %collective-permute-start.9) | collective-permute-done | bytes 16416 | tf_op jit(solution)/shard_map/ppermute | solution.py:573
  40.4 1.3 %shard_map.82 = (f32[5,4,32,256]{3,2,1,0:T(8,128)S(1)}, f32[5,32,256]{2,1,0:T(8,128)S(1)}, f32[5,32,256]{2,1,0:T(8,128)S(1)}, f32[5,4,256]{2,1,0:T(4,128)S(1)}, ...) custom-call(f32[32,128]{1,0:T(8,128)S(1)} %get-tuple-element.70.joint, f32[32,128]{1,0:T(8,128)S(1)} %collective-permute-done.9.other_joint, ...), custom_call_target="tpu_custom_call" | custom-call | flops 1300000000 | bytes 3900000 | tf_op jit(solution)/shard_map/pallas_call | solution.py:533
  41.7 0.8 %collective-permute-start.10 = (f32[5,32,256]{2,1,0:T(8,128)S(1)}, f32[5,32,256]{2,1,0:T(8,128)S(1)}, u32[]{:S(2)}, u32[]{:S(2)}) collective-permute-start(f32[5,32,256]{2,1,0:T(8,128)S(1)} %get-tuple-element.75), channel_id=1, source_target_pairs={{0,32},{32,0},{64,96},{96,64},{128,160},{160,128},{192,224},{224,1... | collective-permute-start | bytes 491528 | tf_op jit(solution)/shard_map/ppermute | solution.py:553
  42.5 4.0 %collective-permute-start.11 = (f32[5,32,256]{2,1,0:T(8,128)S(1)}, f32[5,32,256]{2,1,0:T(8,128)S(1)}, u32[]{:S(2)}, u32[]{:S(2)}) collective-permute-start(f32[5,32,256]{2,1,0:T(8,128)S(1)} %get-tuple-element.76), channel_id=1, source_target_pairs={{32,64},{64,32},{96,128},{128,96},{160,192},{192,160},{33,65},{65,... | collective-permute-start | bytes 491528 | tf_op jit(solution)/shard_map/ppermute | solution.py:553
  46.6 0.2 collective-permute-start.12
  46.8 1.4 %collective-permute-start.13 = (f32[5,4,256]{2,1,0:T(4,128)S(1)}, f32[5,4,256]{2,1,0:T(4,128)S(1)}, u32[]{:S(2)}, u32[]{:S(2)}) collective-permute-start(f32[5,4,256]{2,1,0:T(4,128)S(1)} %get-tuple-element.78), channel_id=1, source_target_pairs={{0,1},{1,0},{2,3},{3,2},{4,5},{5,4},{6,7},{7,6},{8,9},{9,8},{10,11... | collective-permute-start | bytes 61448 | tf_op jit(solution)/shard_map/ppermute | solution.py:553
  48.2 5.3 %collective-permute-done.12.tb = f32[5,4,256]{2,1,0:T(4,128)S(1)} collective-permute-done((f32[5,4,256]{2,1,0:T(4,128)S(1)}, f32[5,4,256]{2,1,0:T(4,128)S(1)}, u32[]{:S(2)}, u32[]{:S(2)}) %collective-permute-start.12) | collective-permute-done | bytes 20512 | tf_op jit(solution)/shard_map/ppermute | solution.py:553
  53.5 0.0 collective-permute-done.13.ta
  53.5 0.0 collective-permute-done.10.za
  53.5 0.0 collective-permute-done.11.zb
  53.5 1.3 %shard_map.83 = (f32[20,5,8,128]{3,2,1,0:T(8,128)S(1)}, f32[16,5,8,128]{3,2,1,0:T(8,128)S(1)}, f32[8,128]{1,0:T(8,128)S(1)}) custom-call(f32[5,4,32,256]{3,2,1,0:T(8,128)S(1)} %get-tuple-element.74.u.first, f32[5,32,256]{2,1,0:T(8,128)S(1)} %collective-permute-done.10.za, f32[5,32,256]{2,1,0:T(8,128)S(1)} %collective-permute-done.11.zb, ...), custom_call_target="tpu_custom_call" | custom-call | flops 1300000000 | bytes 3900000 | tf_op jit(solution)/shard_map/pallas_call | solution.py:533
  54.8 2.3 %collective-permute-start.14 = (f32[8,128]{1,0:T(8,128)S(1)}, f32[8,128]{1,0:T(8,128)S(1)}, u32[]{:S(2)}, u32[]{:S(2)}) collective-permute-start(f32[8,128]{1,0:T(8,128)S(1)} %get-tuple-element.79.y_own), channel_id=1, source_target_pairs={{0,16},{1,17},{2,18},{3,19},{4,20},{5,21},{6,22},{7,23},{8,24},{9,... | collective-permute-start | bytes 12296 | tf_op jit(solution)/shard_map/ppermute | solution.py:573
  57.1 5.4 %collective-permute-done.14.y_other = f32[8,128]{1,0:T(8,128)S(1)} collective-permute-done((f32[8,128]{1,0:T(8,128)S(1)}, f32[8,128]{1,0:T(8,128)S(1)}, u32[]{:S(2)}, u32[]{:S(2)}) %collective-permute-start.14) | collective-permute-done | bytes 4128 | tf_op jit(solution)/shard_map/ppermute | solution.py:573
  62.4 1.9 %shard_map.84 = f32[5,4,32,256]{3,2,1,0:T(8,128)} custom-call(f32[8,128]{1,0:T(8,128)S(1)} %get-tuple-element.79.y_own, f32[8,128]{1,0:T(8,128)S(1)} %collective-permute-done.14.y_other, f32[50,128]{1,0:T(8,128)S(1)} %get-tuple-element.80.j_ref, f32[17,75,8,128]{3,2,1,0:T(8,128)S(1)} %get-tuple-element.63.m1, f32[11,75,8,128]{3,2,1,0:T(8,128)S(1)} %get-tuple-element.71.m2, ...), custom_call_target="tpu_custom_call" | custom-call | flops 2000000000 | bytes 6000000 | tf_op jit(solution)/shard_map/pallas_call | solution.py:533
  (4 shorter events, 0.0 us)
Async XLA Ops:
  0.0 11.3 %copy-start = (f32[1,4,5,256]{3,1,2,0:T(4,128)S(1)}, f32[1,4,5,256]{3,1,2,0:T(4,128)}, u32[]{:S(2)}) copy-start(f32[1,4,5,256]{3,1,2,0:T(4,128)} %param.11) | copy-start | bytes 61444
  0.0 11.3 %collective-permute-start = (f32[5,4,256]{2,1,0:T(4,128)}, f32[5,4,256]{2,1,0:T(4,128)S(1)}, u32[]{:S(2)}, u32[]{:S(2)}) collective-permute-start(f32[5,4,256]{2,1,0:T(4,128)} %bitcast.3), channel_id=1, source_target_pairs={{0,24},{1,25},{2,26},{3,27},{4,28},{5,29},{6,30},{7,31},{8,16},{9,... | collective-permute-start | bytes 61448 | tf_op jit(solution)/shard_map/ppermute | solution.py:573
  7.6 13.2 %collective-permute-start.3 = (f32[5,32,256]{2,1,0:T(8,128)S(1)}, f32[5,32,256]{2,1,0:T(8,128)S(1)}, u32[]{:S(2)}, u32[]{:S(2)}) collective-permute-start(f32[5,32,256]{2,1,0:T(8,128)S(1)} %get-tuple-element.54), channel_id=1, source_target_pairs={{32,64},{64,32},{96,128},{128,96},{160,192},{192,160},{33,65},{65,... | collective-permute-start | bytes 491528 | tf_op jit(solution)/shard_map/ppermute | solution.py:553
  11.4 5.0 %collective-permute-start.1 = (f32[5,8,256]{2,1,0:T(8,128)S(1)}, f32[5,8,256]{2,1,0:T(8,128)S(1)}, u32[]{:S(2)}, u32[]{:S(2)}) collective-permute-start(f32[5,8,256]{2,1,0:T(8,128)S(1)} %shard_map.74.low), channel_id=1, source_target_pairs={{0,8},{1,9},{2,10},{3,11},{4,12},{5,13},{6,14},{7,15},{8,0},{9,1},... | collective-permute-start | bytes 122888 | tf_op jit(solution)/shard_map/ppermute | solution.py:573
  16.4 4.4 %collective-permute-start.4 = (f32[5,16,256]{2,1,0:T(8,128)S(1)}, f32[5,16,256]{2,1,0:T(8,128)S(1)}, u32[]{:S(2)}, u32[]{:S(2)}) collective-permute-start(f32[5,16,256]{2,1,0:T(8,128)S(1)} %shard_map.76.low), channel_id=1, source_target_pairs={{0,4},{1,5},{2,6},{3,7},{4,0},{5,1},{6,2},{7,3},{8,12},{9,13},{10,... | collective-permute-start | bytes 245768 | tf_op jit(solution)/shard_map/ppermute | solution.py:573
  17.4 9.1 %collective-permute-start.6 = (f32[5,4,256]{2,1,0:T(4,128)S(1)}, f32[5,4,256]{2,1,0:T(4,128)S(1)}, u32[]{:S(2)}, u32[]{:S(2)}) collective-permute-start(f32[5,4,256]{2,1,0:T(4,128)S(1)} %get-tuple-element.59), channel_id=1, source_target_pairs={{1,2},{2,1},{3,4},{4,3},{5,6},{6,5},{7,8},{8,7},{9,10},{10,9},{11,... | collective-permute-start | bytes 61448 | tf_op jit(solution)/shard_map/ppermute | solution.py:553
  18.0 8.5 %collective-permute-start.2 = (f32[5,32,256]{2,1,0:T(8,128)S(1)}, f32[5,32,256]{2,1,0:T(8,128)S(1)}, u32[]{:S(2)}, u32[]{:S(2)}) collective-permute-start(f32[5,32,256]{2,1,0:T(8,128)S(1)} %get-tuple-element.53), channel_id=1, source_target_pairs={{0,32},{32,0},{64,96},{96,64},{128,160},{160,128},{192,224},{224,1... | collective-permute-start | bytes 491528 | tf_op jit(solution)/shard_map/ppermute | solution.py:553
  20.8 8.5 %collective-permute-start.7 = (f32[5,32,256]{2,1,0:T(8,128)S(1)}, f32[5,32,256]{2,1,0:T(8,128)S(1)}, u32[]{:S(2)}, u32[]{:S(2)}) collective-permute-start(f32[5,32,256]{2,1,0:T(8,128)S(1)} %shard_map.77.low), channel_id=1, source_target_pairs={{0,2},{1,3},{2,0},{3,1},{4,6},{5,7},{6,4},{7,5},{8,10},{9,11},{10,... | collective-permute-start | bytes 491528 | tf_op jit(solution)/shard_map/ppermute | solution.py:573
  23.8 2.7 %collective-permute-start.5 = (f32[5,4,256]{2,1,0:T(4,128)S(1)}, f32[5,4,256]{2,1,0:T(4,128)S(1)}, u32[]{:S(2)}, u32[]{:S(2)}) collective-permute-start(f32[5,4,256]{2,1,0:T(4,128)S(1)} %get-tuple-element.57), channel_id=1, source_target_pairs={{0,1},{1,0},{2,3},{3,2},{4,5},{5,4},{6,7},{7,6},{8,9},{9,8},{10,11... | collective-permute-start | bytes 61448 | tf_op jit(solution)/shard_map/ppermute | solution.py:553
  29.3 1.7 %collective-permute-start.8 = (f32[5,64,256]{2,1,0:T(8,128)S(1)}, f32[5,64,256]{2,1,0:T(8,128)S(1)}, u32[]{:S(2)}, u32[]{:S(2)}) collective-permute-start(f32[5,64,256]{2,1,0:T(8,128)S(1)} %shard_map.79.low), channel_id=1, source_target_pairs={{0,1},{1,0},{2,3},{3,2},{4,5},{5,4},{6,7},{7,6},{8,9},{9,8},{10,11... | collective-permute-start | bytes 983048 | tf_op jit(solution)/shard_map/ppermute | solution.py:573
  32.6 7.7 %collective-permute-start.9 = (f32[32,128]{1,0:T(8,128)S(1)}, f32[32,128]{1,0:T(8,128)S(1)}, u32[]{:S(2)}, u32[]{:S(2)}) collective-permute-start(f32[32,128]{1,0:T(8,128)S(1)} %get-tuple-element.70.joint), channel_id=1, source_target_pairs={{0,16},{1,17},{2,18},{3,19},{4,20},{5,21},{6,22},{7,23},{8,24},{9,... | collective-permute-start | bytes 49160 | tf_op jit(solution)/shard_map/ppermute | solution.py:573
  41.7 11.8 %collective-permute-start.10 = (f32[5,32,256]{2,1,0:T(8,128)S(1)}, f32[5,32,256]{2,1,0:T(8,128)S(1)}, u32[]{:S(2)}, u32[]{:S(2)}) collective-permute-start(f32[5,32,256]{2,1,0:T(8,128)S(1)} %get-tuple-element.75), channel_id=1, source_target_pairs={{0,32},{32,0},{64,96},{96,64},{128,160},{160,128},{192,224},{224,1... | collective-permute-start | bytes 491528 | tf_op jit(solution)/shard_map/ppermute | solution.py:553
  42.5 11.0 %collective-permute-start.11 = (f32[5,32,256]{2,1,0:T(8,128)S(1)}, f32[5,32,256]{2,1,0:T(8,128)S(1)}, u32[]{:S(2)}, u32[]{:S(2)}) collective-permute-start(f32[5,32,256]{2,1,0:T(8,128)S(1)} %get-tuple-element.76), channel_id=1, source_target_pairs={{32,64},{64,32},{96,128},{128,96},{160,192},{192,160},{33,65},{65,... | collective-permute-start | bytes 491528 | tf_op jit(solution)/shard_map/ppermute | solution.py:553
  46.6 6.9 %collective-permute-start.12 = (f32[5,4,256]{2,1,0:T(4,128)S(1)}, f32[5,4,256]{2,1,0:T(4,128)S(1)}, u32[]{:S(2)}, u32[]{:S(2)}) collective-permute-start(f32[5,4,256]{2,1,0:T(4,128)S(1)} %get-tuple-element.77), channel_id=1, source_target_pairs={{1,2},{2,1},{3,4},{4,3},{5,6},{6,5},{7,8},{8,7},{9,10},{10,9},{11,... | collective-permute-start | bytes 61448 | tf_op jit(solution)/shard_map/ppermute | solution.py:553
  46.8 6.7 %collective-permute-start.13 = (f32[5,4,256]{2,1,0:T(4,128)S(1)}, f32[5,4,256]{2,1,0:T(4,128)S(1)}, u32[]{:S(2)}, u32[]{:S(2)}) collective-permute-start(f32[5,4,256]{2,1,0:T(4,128)S(1)} %get-tuple-element.78), channel_id=1, source_target_pairs={{0,1},{1,0},{2,3},{3,2},{4,5},{5,4},{6,7},{7,6},{8,9},{9,8},{10,11... | collective-permute-start | bytes 61448 | tf_op jit(solution)/shard_map/ppermute | solution.py:553
  54.8 7.6 %collective-permute-start.14 = (f32[8,128]{1,0:T(8,128)S(1)}, f32[8,128]{1,0:T(8,128)S(1)}, u32[]{:S(2)}, u32[]{:S(2)}) collective-permute-start(f32[8,128]{1,0:T(8,128)S(1)} %get-tuple-element.79.y_own), channel_id=1, source_target_pairs={{0,16},{1,17},{2,18},{3,19},{4,20},{5,21},{6,22},{7,23},{8,24},{9,... | collective-permute-start | bytes 12296 | tf_op jit(solution)/shard_map/ppermute | solution.py:573

commit v4 on v3

--- a/solution.py
+++ b/solution.py
@@ -335,17 +335,27 @@
             j_ref[pl.ds(NN + i * N + j, 1), :] = c * j2[i][j]
 
 
-def stencil_block(u, v, z, planes, za, zb, ta, tb):
-    z_up, t_up = is_even("ax"), is_even("az")
+def plane_neighbours(za, zb, v):
+    z_up = is_even("ax")
+    return jnp.where(z_up, zb[v], za[v]), jnp.where(z_up, za[v], zb[v])
+
+
+def stencil_block(u, v, z, before, after, ta, tb):
+    planes, sectors = u.shape[1], u.shape[2]
+    t_up = is_even("az")
     cur = u[v, z]
     rows = lax.broadcasted_iota(jnp.int32, cur.shape, 0)
-    behind = u[v, z - 1] if z > 0 else jnp.where(z_up, zb[v], za[v])
-    ahead = u[v, z + 1] if z < planes - 1 else jnp.where(z_up, za[v], zb[v])
-    sectors = cur.shape[0]
+    behind = u[v, z - 1] if z > 0 else before
+    ahead = u[v, z + 1] if z < planes - 1 else after
     t_a, t_b = ta[v, pl.ds(z, 1), :], tb[v, pl.ds(z, 1), :]
     before_t = jnp.where(rows == 0, jnp.where(t_up, t_b, t_a), pltpu.roll(cur, 1, 0))
     after_t = jnp.where(rows == sectors - 1, jnp.where(t_up, t_a, t_b), pltpu.roll(cur, sectors - 1, 0))
-    return behind + ahead + before_t + after_t - 4.0 * cur + 0.5 * (behind - ahead)
+    total = before_t + after_t - 4.0 * cur
+    if behind is not None:
+        total = total + 1.5 * behind
+    if ahead is not None:
+        total = total + 0.5 * ahead
+    return total
 
 
 def forward_body(rhs_t, f1, f2, scal, cst, e_ref, o_ref):
@@ -420,7 +430,8 @@
     mask = mask_ref[...]
     hot = one_hot(place, 0, low.shape[1])
     for v in range(N):
-        blocks = [stencil_block(u, v, z, planes, za, zb, ta, tb) for z in range(planes)]
+        before, after = plane_neighbours(za, zb, v)
+        blocks = [stencil_block(u, v, z, before, after, ta, tb) for z in range(planes)]
         rhs_t[v] = (mask * jnp.concatenate(blocks, axis=0)).T + mask_t[...] * pick(low[v], hot)
 
 
@@ -436,14 +447,23 @@
         joint[pl.ds(VEC_ROW + v, 1), :] = reduced[v]
 
 
-def forward_second_kernel(
-    u, za, zb, tb, ta, mask_ref, f1, f2, scal, cst, e_ref, o_ref, y_ref, rhs_t
-):
+def rhs_second_kernel(u, tb, ta, mask_ref, rhs_t):
     planes = u.shape[1]
     mask = mask_ref[...]
     for v in range(N):
-        blocks = [stencil_block(u, v, z, planes, za, zb, ta, tb) for z in range(planes)]
+        blocks = [stencil_block(u, v, z, None, None, ta, tb) for z in range(planes)]
         rhs_t[v] = (mask * jnp.concatenate(blocks, axis=0)).T
+
+
+def forward_second_kernel(
+    rhs_in, za, zb, mask_t, f1, f2, scal, cst, e_ref, o_ref, y_ref, rhs_t
+):
+    sectors, radial = za.shape[1], za.shape[2]
+    zero = jnp.zeros((LANES - 2 * sectors, radial), F32)
+    for v in range(N):
+        before, after = plane_neighbours(za, zb, v)
+        outer = jnp.concatenate([1.5 * before, zero, 0.5 * after], axis=0)
+        rhs_t[v] = rhs_in[v] + mask_t[...] * outer.T
     reduced = forward_body(rhs_t, f1, f2, scal, cst, e_ref, o_ref)
     y_ref[...] = jnp.zeros((SEG, LANES), F32)
     for v in range(N):
@@ -616,57 +636,58 @@
         1.2,
         hbm=True,
     )
-    first = {"zb": z_far(zb)}
     rows = append(rows, after(got, cst))
-    done = {}
+    halo, done = {"za": z_near(za), "zb": z_far(zb)}, []
 
     def factor(rows, got):
-        done["one"] = call(
-            factor_kernel,
-            (after(coef, rows), mask, cst),
-            [
-                (HALF + 1, 3 * NN) + tile,
-                (HALF // 2, 2 * NN) + tile,
-                (HALF, 3) + tile,
-                (JOINT_ROWS, LANES),
-                (radial, LANES),
-            ],
-            [(radial, LANES), (2 * HALF + 1,) + tile, (4, NN) + tile],
-            3.2,
+        done.extend(
+            call(
+                factor_kernel,
+                (after(coef, rows), mask, cst),
+                [
+                    (HALF + 1, 3 * NN) + tile,
+                    (HALF // 2, 2 * NN) + tile,
+                    (HALF, 3) + tile,
+                    (JOINT_ROWS, LANES),
+                    (radial, LANES),
+                ],
+                [(radial, LANES), (2 * HALF + 1,) + tile, (4, NN) + tile],
+                3.2,
+            )
         )
-        return after(got, done["one"][3])
-
-    def far_halos(rows, got):
-        first["tb"] = t_far(after(tb, rows))
-        first["za"] = z_near(after(za, rows))
-        return after(got, first["zb"])
+        return after(got, done[3])
+
+    def sector_halos(rows, got):
+        halo["tb"], halo["ta"] = t_far(after(tb, rows)), t_near(after(ta, rows))
+        return after(got, halo["za"], halo["zb"])
 
     def factor_rest(rows, got):
-        first["ta"] = t_near(after(ta, rows))
-        done["rest"] = call(
-            factor_rest_kernel,
-            (after(done["one"][0], rows), done["one"][3]),
-            [
-                (HALF // 2 + 3, 3 * NN) + tile,
-                (HALF // 2 + 2, 2 * NN) + tile,
-                (JOINT_ROWS, LANES),
-            ],
-            [],
-            3.0,
+        m1, sd = done[0], done[3]
+        done.extend(
+            call(
+                factor_rest_kernel,
+                (after(m1, rows), sd),
+                [
+                    (HALF // 2 + 3, 3 * NN) + tile,
+                    (HALF // 2 + 2, 2 * NN) + tile,
+                    (JOINT_ROWS, LANES),
+                ],
+                [],
+                3.0,
+            )
         )
-        return after(got, done["rest"][2], first["za"], first["ta"], first["tb"])
-
-    fillers = [factor, far_halos, factor_rest]
+        return after(got, done[-1], halo["ta"], halo["tb"])
+
+    fillers = [factor, sector_halos, factor_rest]
     for i, bit in enumerate(bits[1:-1]):
         rows = append(rows, fillers[i](rows, xor_swap(rows, bit)))
     for filler in fillers[len(bits) - 2 :]:
         rows = filler(rows, rows)
+    m1, f1, scal, _, mask_t, m2, f2, sd = done
     others = xor_swap(rows, bits[-1])
-    m1, f1, scal, _, mask_t = done["one"]
-    m2, f2, sd = done["rest"]
     (rhs,) = call(
         rhs_kernel,
-        (u, first["za"], first["zb"], first["ta"], first["tb"], mask, mask_t, place, rows),
+        (u, halo["za"], halo["zb"], halo["ta"], halo["tb"], mask, mask_t, place, rows),
         [columns],
         [],
         1.3,
@@ -691,9 +712,10 @@
         1.3,
     )
     tb, zb, za, ta = t_far(tb), z_far(zb), z_near(za), t_near(ta)
+    (rhs,) = call(rhs_second_kernel, (delta, tb, ta, mask), [columns], [], 4.0)
     e2, o2, y2 = call(
         forward_second_kernel,
-        (delta, za, zb, tb, ta, mask, f1, f2, scal, cst),
+        (rhs, za, zb, mask_t, f1, f2, scal, cst),
         fwd_outs + [tile],
         [columns],
         1.3,

time: 64.6 us -> 65 us (level)
  waiting for transfers between devices: 21.6 us -> 17.5 us
  starting transfers between devices: 28.6 us -> 32.6 us
    ppermute x7, waiting for transfers between devices: 16.2 us -> 12.2 us  [xor_swap(): lax.ppermute(x, 'az', [(i, i ^ bit) for i in range(lax.axis_size('az'))])]
    ppermute x8, starting transfers between devices: 11.6 us -> 13.7 us  [swapped_along(): return lax.ppermute(x, axis, pairs)]
    ppermute x7, starting transfers between devices: 17 us -> 18.9 us  [xor_swap(): lax.ppermute(x, 'az', [(i, i ^ bit) for i in range(lax.axis_size('az'))])]
    pallas_call x12 -> x13, Pallas kernels: 14 us -> 14.3 us  [call(): pl.pallas_call(kernel, out_shape=out_shape, in_specs=[in_spec] * len(inpu...]
  transfers between devices with their start and end apart: 15 -> 15, of which waited for: 7 -> 8; matrix products, arithmetic and copies ran while one was open for 0% -> 0% of each run, Pallas kernels for 12% -> 13%
where the time goes in v4:
time: 65 us; the launch traced here: 64.7 us
  starting transfers between devices  32.6 us (50%)
  waiting for transfers between devices  17.5 us (27%)
  Pallas kernels  14.3 us (22%)
    ppermute x7, starting transfers between devices, xor_swap(): lax.ppermute(x, 'az', [(i, i ^ bit) for i in range(lax.axis_size('az'))])  18.9 us
    pallas_call x13, Pallas kernels, call(): pl.pallas_call(kernel, out_shape=out_shape, in_specs=[in_spec] * len(inpu...  14.3 us
    ppermute x8, starting transfers between devices, swapped_along(): return lax.ppermute(x, axis, pairs)  13.7 us
    ppermute x7, waiting for transfers between devices, xor_swap(): lax.ppermute(x, 'az', [(i, i ^ bit) for i in range(lax.axis_size('az'))])  12.2 us
    ppermute x8, waiting for transfers between devices, swapped_along(): return lax.ppermute(x, axis, pairs)  5.33 us
  transfers between devices with their start and end apart: 15, of which 8 were waited for; matrix products, arithmetic and copies ran while one was open for 0% of the time, Pallas kernels for 13%

profile of v4, /device:TPU:6, one launch (start us, length us, event | category | flops | bytes accessed | tf_op | source)
XLA Modules:
  0.0 64.7 jit_solution(17715950946904814627)
XLA Ops:
  0.0 0.0 copy-start
  0.0 6.3 %collective-permute-start.2 = (f32[5,4,256]{2,1,0:T(4,128)}, f32[5,4,256]{2,1,0:T(4,128)S(1)}, u32[]{:S(2)}, u32[]{:S(2)}) collective-permute-start(f32[5,4,256]{2,1,0:T(4,128)} %bitcast.3), channel_id=1, source_target_pairs={{0,24},{1,25},{2,26},{3,27},{4,28},{5,29},{6,30},{7,31},{8,16},{9,... | collective-permute-start | bytes 61448 | tf_op jit(solution)/shard_map/ppermute | solution.py:593
  6.3 1.3 %shard_map.73 = (f32[5,4,32,256]{3,2,1,0:T(8,128)S(1)}, f32[4,32,256]{2,1,0:T(8,128)S(1)}, f32[128,256]{1,0:T(8,128)S(1)}, s32[4,32]{1,0:T(4,128)S(1)}, f32[2,25...) custom-call(f32[5,4,32,256]{3,2,1,0:T(8,128)} %flow.1, ...), custom_call_target="tpu_custom_call" | custom-call | flops 1200000000 | bytes 3600000 | tf_op jit(solution)/shard_map/pallas_call | solution.py:553
  7.6 1.7 %collective-permute-start = (f32[5,32,256]{2,1,0:T(8,128)S(1)}, f32[5,32,256]{2,1,0:T(8,128)S(1)}, u32[]{:S(2)}, u32[]{:S(2)}) collective-permute-start(f32[5,32,256]{2,1,0:T(8,128)S(1)} %get-tuple-element.44), channel_id=1, source_target_pairs={{0,32},{32,0},{64,96},{96,64},{128,160},{160,128},{192,224},{224,1... | collective-permute-start | bytes 491528 | tf_op jit(solution)/shard_map/ppermute | solution.py:573
  9.2 2.6 %collective-permute-start.1 = (f32[5,32,256]{2,1,0:T(8,128)S(1)}, f32[5,32,256]{2,1,0:T(8,128)S(1)}, u32[]{:S(2)}, u32[]{:S(2)}) collective-permute-start(f32[5,32,256]{2,1,0:T(8,128)S(1)} %get-tuple-element.45), channel_id=1, source_target_pairs={{32,64},{64,32},{96,128},{128,96},{160,192},{192,160},{33,65},{65,... | collective-permute-start | bytes 491528 | tf_op jit(solution)/shard_map/ppermute | solution.py:573
  11.8 0.0 collective-permute-done.2.high
  11.9 0.0 copy-done
  11.9 1.5 %collective-permute-start.3 = (f32[5,8,256]{2,1,0:T(8,128)S(1)}, f32[5,8,256]{2,1,0:T(8,128)S(1)}, u32[]{:S(2)}, u32[]{:S(2)}) collective-permute-start(f32[5,8,256]{2,1,0:T(8,128)S(1)} %shard_map.74.low), channel_id=1, source_target_pairs={{0,8},{1,9},{2,10},{3,11},{4,12},{5,13},{6,14},{7,15},{8,0},{9,1},... | collective-permute-start | bytes 122888 | tf_op jit(solution)/shard_map/ppermute | solution.py:593
  13.4 3.1 %shard_map.75 = (f32[17,75,8,128]{3,2,1,0:T(8,128)S(1)}, f32[8,50,8,128]{3,2,1,0:T(8,128)S(1)}, f32[16,3,8,128]{3,2,1,0:T(8,128)S(1)}, f32[32,128]{1,0:T(8,128)S(1)}, f32[256,128]{1,0:T(8,128)S(1)}) custom-call(f32[4,32,256]{2,1,0:T(8,128)S(1)} %get-tuple-element.50.coef_ref, f32[128,256]{1,0:T(8,128)S(1)} %get-tuple-element.51.mask_ref, ...), custom_call_target="tpu_custom_call" | custom-call | flops 3200000000 | bytes 9600000 | tf_op jit(solution)/shard_map/pallas_call | solution.py:553
  16.5 0.4 collective-permute-done.3.high
  16.9 1.0 %collective-permute-start.6 = (f32[5,16,256]{2,1,0:T(8,128)S(1)}, f32[5,16,256]{2,1,0:T(8,128)S(1)}, u32[]{:S(2)}, u32[]{:S(2)}) collective-permute-start(f32[5,16,256]{2,1,0:T(8,128)S(1)} %shard_map.76.low), channel_id=1, source_target_pairs={{0,4},{1,5},{2,6},{3,7},{4,0},{5,1},{6,2},{7,3},{8,12},{9,13},{10,... | collective-permute-start | bytes 245768 | tf_op jit(solution)/shard_map/ppermute | solution.py:593
  17.9 0.0 collective-permute-start.4
  17.9 2.8 %collective-permute-start.5 = (f32[5,4,256]{2,1,0:T(4,128)S(1)}, f32[5,4,256]{2,1,0:T(4,128)S(1)}, u32[]{:S(2)}, u32[]{:S(2)}) collective-permute-start(f32[5,4,256]{2,1,0:T(4,128)S(1)} %get-tuple-element.56), channel_id=1, source_target_pairs={{1,2},{2,1},{3,4},{4,3},{5,6},{6,5},{7,8},{8,7},{9,10},{10,9},{11,... | collective-permute-start | bytes 61448 | tf_op jit(solution)/shard_map/ppermute | solution.py:573
  20.7 0.6 collective-permute-done.6.high
  21.3 0.0 collective-permute-done.za
  21.3 0.0 collective-permute-done.1.zb
  21.3 3.3 %collective-permute-start.7 = (f32[5,32,256]{2,1,0:T(8,128)S(1)}, f32[5,32,256]{2,1,0:T(8,128)S(1)}, u32[]{:S(2)}, u32[]{:S(2)}) collective-permute-start(f32[5,32,256]{2,1,0:T(8,128)S(1)} %shard_map.77.low), channel_id=1, source_target_pairs={{0,2},{1,3},{2,0},{3,1},{4,6},{5,7},{6,4},{7,5},{8,10},{9,11},{10,... | collective-permute-start | bytes 491528 | tf_op jit(solution)/shard_map/ppermute | solution.py:593
  24.6 2.7 %shard_map.78 = (f32[11,75,8,128]{3,2,1,0:T(8,128)S(1)}, f32[10,50,8,128]{3,2,1,0:T(8,128)S(1)}, f32[32,128]{1,0:T(8,128)S(1)}) custom-call(f32[17,75,8,128]{3,2,1,0:T(8,128)S(1)} %get-tuple-element.61.m1, f32[32,128]{1,0:T(8,128)S(1)} %get-tuple-element.52.sd_in), custom_call_target="tpu_custom_call" | custom-call | flops 3000000000 | bytes 9000000 | tf_op jit(solution)/shard_map/pallas_call | solution.py:553
  27.3 0.0 collective-permute-done.4.ta
  27.3 0.0 collective-permute-done.5.tb
  27.3 1.6 %collective-permute-done.7.high = f32[5,32,256]{2,1,0:T(8,128)S(1)} collective-permute-done((f32[5,32,256]{2,1,0:T(8,128)S(1)}, f32[5,32,256]{2,1,0:T(8,128)S(1)}, u32[]{:S(2)}, u32[]{:S(2)}) %collective-permute-start.7) | collective-permute-done | bytes 163872 | tf_op jit(solution)/shard_map/ppermute | solution.py:593
  29.0 0.1 collective-permute-start.8
  29.1 0.9 %shard_map.80.rhs_in = f32[5,256,128]{2,1,0:T(8,128)S(1)} custom-call(f32[5,4,32,256]{3,2,1,0:T(8,128)S(1)} %get-tuple-element.43.u, f32[5,32,256]{2,1,0:T(8,128)S(1)} %collective-permute-done.za, f32[5,32,256]{2,1,0:T(8,128)S(1)} %collective-permute-done.1.zb, f32[5,4,256]{2,1,0:T(4,128)S(1)} %collective-permute-done.4.ta, ...), custom_call_target="tpu_custom_call" | custom-call | flops 1300000000 | bytes 3900000 | tf_op jit(solution)/shard_map/pallas_call | solution.py:553
  30.0 0.7 %collective-permute-done.8.high = f32[5,64,256]{2,1,0:T(8,128)S(1)} collective-permute-done((f32[5,64,256]{2,1,0:T(8,128)S(1)}, f32[5,64,256]{2,1,0:T(8,128)S(1)}, u32[]{:S(2)}, u32[]{:S(2)}) %collective-permute-start.8) | collective-permute-done | bytes 327712 | tf_op jit(solution)/shard_map/ppermute | solution.py:593
  30.7 1.6 %shard_map.81 = (f32[20,5,8,128]{3,2,1,0:T(8,128)S(1)}, f32[16,5,8,128]{3,2,1,0:T(8,128)S(1)}, f32[32,128]{1,0:T(8,128)S(1)}) custom-call(f32[5,256,128]{2,1,0:T(8,128)S(1)} %shard_map.80.rhs_in, f32[256,128]{1,0:T(8,128)S(1)} %get-tuple-element.57.mask_t, s32[4,32]{1,0:T(4,128)S(1)} %get-tuple-element.58.place, ...), custom_call_target="tpu_custom_call" | custom-call | flops 1200000000 | bytes 3600000 | tf_op jit(solution)/shard_map/pallas_call | solution.py:553
  32.3 3.3 %collective-permute-start.9 = (f32[32,128]{1,0:T(8,128)S(1)}, f32[32,128]{1,0:T(8,128)S(1)}, u32[]{:S(2)}, u32[]{:S(2)}) collective-permute-start(f32[32,128]{1,0:T(8,128)S(1)} %get-tuple-element.68.joint), channel_id=1, source_target_pairs={{0,16},{1,17},{2,18},{3,19},{4,20},{5,21},{6,22},{7,23},{8,24},{9,... | collective-permute-start | bytes 49160 | tf_op jit(solution)/shard_map/ppermute | solution.py:593
  35.6 4.6 %collective-permute-done.9.other_joint = f32[32,128]{1,0:T(8,128)S(1)} collective-permute-done((f32[32,128]{1,0:T(8,128)S(1)}, f32[32,128]{1,0:T(8,128)S(1)}, u32[]{:S(2)}, u32[]{:S(2)}) %collective-permute-start.9) | collective-permute-done | bytes 16416 | tf_op jit(solution)/shard_map/ppermute | solution.py:593
  40.2 1.3 %shard_map.82 = (f32[5,4,32,256]{3,2,1,0:T(8,128)S(1)}, f32[5,32,256]{2,1,0:T(8,128)S(1)}, f32[5,32,256]{2,1,0:T(8,128)S(1)}, f32[5,4,256]{2,1,0:T(4,128)S(1)}, ...) custom-call(f32[32,128]{1,0:T(8,128)S(1)} %get-tuple-element.68.joint, f32[32,128]{1,0:T(8,128)S(1)} %collective-permute-done.9.other_joint, ...), custom_call_target="tpu_custom_call" | custom-call | flops 1300000000 | bytes 3900000 | tf_op jit(solution)/shard_map/pallas_call | solution.py:553
  41.5 1.2 %collective-permute-start.10 = (f32[5,4,256]{2,1,0:T(4,128)S(1)}, f32[5,4,256]{2,1,0:T(4,128)S(1)}, u32[]{:S(2)}, u32[]{:S(2)}) collective-permute-start(f32[5,4,256]{2,1,0:T(4,128)S(1)} %get-tuple-element.73), channel_id=1, source_target_pairs={{1,2},{2,1},{3,4},{4,3},{5,6},{6,5},{7,8},{8,7},{9,10},{10,9},{11,... | collective-permute-start | bytes 61448 | tf_op jit(solution)/shard_map/ppermute | solution.py:573
  42.7 1.5 %collective-permute-start.11 = (f32[5,4,256]{2,1,0:T(4,128)S(1)}, f32[5,4,256]{2,1,0:T(4,128)S(1)}, u32[]{:S(2)}, u32[]{:S(2)}) collective-permute-start(f32[5,4,256]{2,1,0:T(4,128)S(1)} %get-tuple-element.74), channel_id=1, source_target_pairs={{0,1},{1,0},{2,3},{3,2},{4,5},{5,4},{6,7},{7,6},{8,9},{9,8},{10,11... | collective-permute-start | bytes 61448 | tf_op jit(solution)/shard_map/ppermute | solution.py:573
  44.2 0.0 collective-permute-start.12
  44.2 3.9 %collective-permute-start.13 = (f32[5,32,256]{2,1,0:T(8,128)S(1)}, f32[5,32,256]{2,1,0:T(8,128)S(1)}, u32[]{:S(2)}, u32[]{:S(2)}) collective-permute-start(f32[5,32,256]{2,1,0:T(8,128)S(1)} %get-tuple-element.76), channel_id=1, source_target_pairs={{32,64},{64,32},{96,128},{128,96},{160,192},{192,160},{33,65},{65,... | collective-permute-start | bytes 491528 | tf_op jit(solution)/shard_map/ppermute | solution.py:573
  48.1 0.4 collective-permute-done.10.tb
  48.5 0.0 collective-permute-done.11.ta
  48.5 0.3 shard_map.83.rhs_in
  48.9 4.9 %collective-permute-done.12.za = f32[5,32,256]{2,1,0:T(8,128)S(1)} collective-permute-done((f32[5,32,256]{2,1,0:T(8,128)S(1)}, f32[5,32,256]{2,1,0:T(8,128)S(1)}, u32[]{:S(2)}, u32[]{:S(2)}) %collective-permute-start.12) | collective-permute-done | bytes 163872 | tf_op jit(solution)/shard_map/ppermute | solution.py:573
  53.8 0.0 collective-permute-done.13.zb
  53.8 1.2 %shard_map.84 = (f32[20,5,8,128]{3,2,1,0:T(8,128)S(1)}, f32[16,5,8,128]{3,2,1,0:T(8,128)S(1)}, f32[8,128]{1,0:T(8,128)S(1)}) custom-call(f32[5,256,128]{2,1,0:T(8,128)S(1)} %shard_map.83.rhs_in, f32[5,32,256]{2,1,0:T(8,128)S(1)} %collective-permute-done.12.za, f32[5,32,256]{2,1,0:T(8,128)S(1)} %collective-permute-done.13.zb, ...), custom_call_target="tpu_custom_call" | custom-call | flops 1300000000 | bytes 3900000 | tf_op jit(solution)/shard_map/pallas_call | solution.py:553
  55.1 3.3 %collective-permute-start.14 = (f32[8,128]{1,0:T(8,128)S(1)}, f32[8,128]{1,0:T(8,128)S(1)}, u32[]{:S(2)}, u32[]{:S(2)}) collective-permute-start(f32[8,128]{1,0:T(8,128)S(1)} %get-tuple-element.77.y_own), channel_id=1, source_target_pairs={{0,16},{1,17},{2,18},{3,19},{4,20},{5,21},{6,22},{7,23},{8,24},{9,... | collective-permute-start | bytes 12296 | tf_op jit(solution)/shard_map/ppermute | solution.py:593
  58.4 4.3 %collective-permute-done.14.y_other = f32[8,128]{1,0:T(8,128)S(1)} collective-permute-done((f32[8,128]{1,0:T(8,128)S(1)}, f32[8,128]{1,0:T(8,128)S(1)}, u32[]{:S(2)}, u32[]{:S(2)}) %collective-permute-start.14) | collective-permute-done | bytes 4128 | tf_op jit(solution)/shard_map/ppermute | solution.py:593
  62.7 1.9 %shard_map.85 = f32[5,4,32,256]{3,2,1,0:T(8,128)} custom-call(f32[8,128]{1,0:T(8,128)S(1)} %get-tuple-element.77.y_own, f32[8,128]{1,0:T(8,128)S(1)} %collective-permute-done.14.y_other, f32[50,128]{1,0:T(8,128)S(1)} %get-tuple-element.78.j_ref, f32[17,75,8,128]{3,2,1,0:T(8,128)S(1)} %get-tuple-element.61.m1, f32[11,75,8,128]{3,2,1,0:T(8,128)S(1)} %get-tuple-element.69.m2, ...), custom_call_target="tpu_custom_call" | custom-call | flops 2000000000 | bytes 6000000 | tf_op jit(solution)/shard_map/pallas_call | solution.py:553
  (4 shorter events, 0.0 us)
Async XLA Ops:
  0.0 11.9 %copy-start = (f32[1,4,5,256]{3,1,2,0:T(4,128)S(1)}, f32[1,4,5,256]{3,1,2,0:T(4,128)}, u32[]{:S(2)}) copy-start(f32[1,4,5,256]{3,1,2,0:T(4,128)} %param.11) | copy-start | bytes 61444
  0.0 11.8 %collective-permute-start.2 = (f32[5,4,256]{2,1,0:T(4,128)}, f32[5,4,256]{2,1,0:T(4,128)S(1)}, u32[]{:S(2)}, u32[]{:S(2)}) collective-permute-start(f32[5,4,256]{2,1,0:T(4,128)} %bitcast.3), channel_id=1, source_target_pairs={{0,24},{1,25},{2,26},{3,27},{4,28},{5,29},{6,30},{7,31},{8,16},{9,... | collective-permute-start | bytes 61448 | tf_op jit(solution)/shard_map/ppermute | solution.py:593
  7.6 13.8 %collective-permute-start = (f32[5,32,256]{2,1,0:T(8,128)S(1)}, f32[5,32,256]{2,1,0:T(8,128)S(1)}, u32[]{:S(2)}, u32[]{:S(2)}) collective-permute-start(f32[5,32,256]{2,1,0:T(8,128)S(1)} %get-tuple-element.44), channel_id=1, source_target_pairs={{0,32},{32,0},{64,96},{96,64},{128,160},{160,128},{192,224},{224,1... | collective-permute-start | bytes 491528 | tf_op jit(solution)/shard_map/ppermute | solution.py:573
  9.2 12.1 %collective-permute-start.1 = (f32[5,32,256]{2,1,0:T(8,128)S(1)}, f32[5,32,256]{2,1,0:T(8,128)S(1)}, u32[]{:S(2)}, u32[]{:S(2)}) collective-permute-start(f32[5,32,256]{2,1,0:T(8,128)S(1)} %get-tuple-element.45), channel_id=1, source_target_pairs={{32,64},{64,32},{96,128},{128,96},{160,192},{192,160},{33,65},{65,... | collective-permute-start | bytes 491528 | tf_op jit(solution)/shard_map/ppermute | solution.py:573
  11.9 5.0 %collective-permute-start.3 = (f32[5,8,256]{2,1,0:T(8,128)S(1)}, f32[5,8,256]{2,1,0:T(8,128)S(1)}, u32[]{:S(2)}, u32[]{:S(2)}) collective-permute-start(f32[5,8,256]{2,1,0:T(8,128)S(1)} %shard_map.74.low), channel_id=1, source_target_pairs={{0,8},{1,9},{2,10},{3,11},{4,12},{5,13},{6,14},{7,15},{8,0},{9,1},... | collective-permute-start | bytes 122888 | tf_op jit(solution)/shard_map/ppermute | solution.py:593
  16.9 4.4 %collective-permute-start.6 = (f32[5,16,256]{2,1,0:T(8,128)S(1)}, f32[5,16,256]{2,1,0:T(8,128)S(1)}, u32[]{:S(2)}, u32[]{:S(2)}) collective-permute-start(f32[5,16,256]{2,1,0:T(8,128)S(1)} %shard_map.76.low), channel_id=1, source_target_pairs={{0,4},{1,5},{2,6},{3,7},{4,0},{5,1},{6,2},{7,3},{8,12},{9,13},{10,... | collective-permute-start | bytes 245768 | tf_op jit(solution)/shard_map/ppermute | solution.py:593
  17.9 9.4 %collective-permute-start.4 = (f32[5,4,256]{2,1,0:T(4,128)S(1)}, f32[5,4,256]{2,1,0:T(4,128)S(1)}, u32[]{:S(2)}, u32[]{:S(2)}) collective-permute-start(f32[5,4,256]{2,1,0:T(4,128)S(1)} %get-tuple-element.54), channel_id=1, source_target_pairs={{0,1},{1,0},{2,3},{3,2},{4,5},{5,4},{6,7},{7,6},{8,9},{9,8},{10,11... | collective-permute-start | bytes 61448 | tf_op jit(solution)/shard_map/ppermute | solution.py:573
  17.9 9.4 %collective-permute-start.5 = (f32[5,4,256]{2,1,0:T(4,128)S(1)}, f32[5,4,256]{2,1,0:T(4,128)S(1)}, u32[]{:S(2)}, u32[]{:S(2)}) collective-permute-start(f32[5,4,256]{2,1,0:T(4,128)S(1)} %get-tuple-element.56), channel_id=1, source_target_pairs={{1,2},{2,1},{3,4},{4,3},{5,6},{6,5},{7,8},{8,7},{9,10},{10,9},{11,... | collective-permute-start | bytes 61448 | tf_op jit(solution)/shard_map/ppermute | solution.py:573
  21.3 7.6 %collective-permute-start.7 = (f32[5,32,256]{2,1,0:T(8,128)S(1)}, f32[5,32,256]{2,1,0:T(8,128)S(1)}, u32[]{:S(2)}, u32[]{:S(2)}) collective-permute-start(f32[5,32,256]{2,1,0:T(8,128)S(1)} %shard_map.77.low), channel_id=1, source_target_pairs={{0,2},{1,3},{2,0},{3,1},{4,6},{5,7},{6,4},{7,5},{8,10},{9,11},{10,... | collective-permute-start | bytes 491528 | tf_op jit(solution)/shard_map/ppermute | solution.py:593
  29.0 1.7 %collective-permute-start.8 = (f32[5,64,256]{2,1,0:T(8,128)S(1)}, f32[5,64,256]{2,1,0:T(8,128)S(1)}, u32[]{:S(2)}, u32[]{:S(2)}) collective-permute-start(f32[5,64,256]{2,1,0:T(8,128)S(1)} %shard_map.79.low), channel_id=1, source_target_pairs={{0,1},{1,0},{2,3},{3,2},{4,5},{5,4},{6,7},{7,6},{8,9},{9,8},{10,11... | collective-permute-start | bytes 983048 | tf_op jit(solution)/shard_map/ppermute | solution.py:593
  32.3 7.9 %collective-permute-start.9 = (f32[32,128]{1,0:T(8,128)S(1)}, f32[32,128]{1,0:T(8,128)S(1)}, u32[]{:S(2)}, u32[]{:S(2)}) collective-permute-start(f32[32,128]{1,0:T(8,128)S(1)} %get-tuple-element.68.joint), channel_id=1, source_target_pairs={{0,16},{1,17},{2,18},{3,19},{4,20},{5,21},{6,22},{7,23},{8,24},{9,... | collective-permute-start | bytes 49160 | tf_op jit(solution)/shard_map/ppermute | solution.py:593
  41.5 7.0 %collective-permute-start.10 = (f32[5,4,256]{2,1,0:T(4,128)S(1)}, f32[5,4,256]{2,1,0:T(4,128)S(1)}, u32[]{:S(2)}, u32[]{:S(2)}) collective-permute-start(f32[5,4,256]{2,1,0:T(4,128)S(1)} %get-tuple-element.73), channel_id=1, source_target_pairs={{1,2},{2,1},{3,4},{4,3},{5,6},{6,5},{7,8},{8,7},{9,10},{10,9},{11,... | collective-permute-start | bytes 61448 | tf_op jit(solution)/shard_map/ppermute | solution.py:573
  42.7 5.8 %collective-permute-start.11 = (f32[5,4,256]{2,1,0:T(4,128)S(1)}, f32[5,4,256]{2,1,0:T(4,128)S(1)}, u32[]{:S(2)}, u32[]{:S(2)}) collective-permute-start(f32[5,4,256]{2,1,0:T(4,128)S(1)} %get-tuple-element.74), channel_id=1, source_target_pairs={{0,1},{1,0},{2,3},{3,2},{4,5},{5,4},{6,7},{7,6},{8,9},{9,8},{10,11... | collective-permute-start | bytes 61448 | tf_op jit(solution)/shard_map/ppermute | solution.py:573
  44.2 9.6 %collective-permute-start.12 = (f32[5,32,256]{2,1,0:T(8,128)S(1)}, f32[5,32,256]{2,1,0:T(8,128)S(1)}, u32[]{:S(2)}, u32[]{:S(2)}) collective-permute-start(f32[5,32,256]{2,1,0:T(8,128)S(1)} %get-tuple-element.75), channel_id=1, source_target_pairs={{0,32},{32,0},{64,96},{96,64},{128,160},{160,128},{192,224},{224,1... | collective-permute-start | bytes 491528 | tf_op jit(solution)/shard_map/ppermute | solution.py:573
  44.2 9.6 %collective-permute-start.13 = (f32[5,32,256]{2,1,0:T(8,128)S(1)}, f32[5,32,256]{2,1,0:T(8,128)S(1)}, u32[]{:S(2)}, u32[]{:S(2)}) collective-permute-start(f32[5,32,256]{2,1,0:T(8,128)S(1)} %get-tuple-element.76), channel_id=1, source_target_pairs={{32,64},{64,32},{96,128},{128,96},{160,192},{192,160},{33,65},{65,... | collective-permute-start | bytes 491528 | tf_op jit(solution)/shard_map/ppermute | solution.py:573
  55.1 7.6 %collective-permute-start.14 = (f32[8,128]{1,0:T(8,128)S(1)}, f32[8,128]{1,0:T(8,128)S(1)}, u32[]{:S(2)}, u32[]{:S(2)}) collective-permute-start(f32[8,128]{1,0:T(8,128)S(1)} %get-tuple-element.77.y_own), channel_id=1, source_target_pairs={{0,16},{1,17},{2,18},{3,19},{4,20},{5,21},{6,22},{7,23},{8,24},{9,... | collective-permute-start | bytes 12296 | tf_op jit(solution)/shard_map/ppermute | solution.py:593

commit v5 on v4

--- a/solution.py
+++ b/solution.py
@@ -45,11 +45,9 @@
 
 def mat_vec(x, v):
     out = []
-    for i in range(N):
-        acc = x[i][0] * v[0]
-        for k in range(1, N):
-            acc = acc + x[i][k] * v[k]
-        out.append(acc)
+    for row in x:
+        t = [row[k] * v[k] for k in range(N)]
+        out.append((t[0] + t[1]) + (t[2] + t[3]) + t[4])
     return out
 
 
@@ -350,12 +348,7 @@
     t_a, t_b = ta[v, pl.ds(z, 1), :], tb[v, pl.ds(z, 1), :]
     before_t = jnp.where(rows == 0, jnp.where(t_up, t_b, t_a), pltpu.roll(cur, 1, 0))
     after_t = jnp.where(rows == sectors - 1, jnp.where(t_up, t_a, t_b), pltpu.roll(cur, sectors - 1, 0))
-    total = before_t + after_t - 4.0 * cur
-    if behind is not None:
-        total = total + 1.5 * behind
-    if ahead is not None:
-        total = total + 0.5 * ahead
-    return total
+    return (before_t + after_t) + (1.5 * behind + 0.5 * ahead) - 4.0 * cur
 
 
 def forward_body(rhs_t, f1, f2, scal, cst, e_ref, o_ref):
@@ -412,15 +405,19 @@
     planes, sectors = place.shape
     rows = start + lax.broadcasted_iota(jnp.int32, (count, sectors), 0)
     hot = [jnp.where(rows == place[pl.ds(z, 1), :], 1.0, 0.0) for z in range(planes)]
-    return jnp.concatenate(hot, axis=1)
+    hot = jnp.concatenate(hot, axis=1)
+    return jnp.concatenate([hot, hot, hot], axis=0).astype(jnp.bfloat16)
 
 
 def pick(rows, hot):
+    high = rows.astype(jnp.bfloat16)
+    rest = rows - high.astype(F32)
+    middle = rest.astype(jnp.bfloat16)
+    low = (rest - middle.astype(F32)).astype(jnp.bfloat16)
     return lax.dot_general(
-        rows,
+        jnp.concatenate([high, middle, low], axis=0),
         hot,
         (((0,), (0,)), ((), ())),
-        precision=lax.Precision.HIGHEST,
         preferred_element_type=F32,
     )
 
@@ -447,23 +444,15 @@
         joint[pl.ds(VEC_ROW + v, 1), :] = reduced[v]
 
 
-def rhs_second_kernel(u, tb, ta, mask_ref, rhs_t):
+def forward_second_kernel(
+    u, za, zb, tb, ta, mask_ref, f1, f2, scal, cst, e_ref, o_ref, y_ref, rhs_t
+):
     planes = u.shape[1]
     mask = mask_ref[...]
     for v in range(N):
-        blocks = [stencil_block(u, v, z, None, None, ta, tb) for z in range(planes)]
+        before, after = plane_neighbours(za, zb, v)
+        blocks = [stencil_block(u, v, z, before, after, ta, tb) for z in range(planes)]
         rhs_t[v] = (mask * jnp.concatenate(blocks, axis=0)).T
-
-
-def forward_second_kernel(
-    rhs_in, za, zb, mask_t, f1, f2, scal, cst, e_ref, o_ref, y_ref, rhs_t
-):
-    sectors, radial = za.shape[1], za.shape[2]
-    zero = jnp.zeros((LANES - 2 * sectors, radial), F32)
-    for v in range(N):
-        before, after = plane_neighbours(za, zb, v)
-        outer = jnp.concatenate([1.5 * before, zero, 0.5 * after], axis=0)
-        rhs_t[v] = rhs_in[v] + mask_t[...] * outer.T
     reduced = forward_body(rhs_t, f1, f2, scal, cst, e_ref, o_ref)
     y_ref[...] = jnp.zeros((SEG, LANES), F32)
     for v in range(N):
@@ -712,10 +701,9 @@
         1.3,
     )
     tb, zb, za, ta = t_far(tb), z_far(zb), z_near(za), t_near(ta)
-    (rhs,) = call(rhs_second_kernel, (delta, tb, ta, mask), [columns], [], 4.0)
     e2, o2, y2 = call(
         forward_second_kernel,
-        (rhs, za, zb, mask_t, f1, f2, scal, cst),
+        (delta, za, zb, tb, ta, mask, f1, f2, scal, cst),
         fwd_outs + [tile],
         [columns],
         1.3,

time: 65 us -> 64.1 us (0.986); the launches traced: 64.7 us -> 63 us
  Pallas kernels: 14.3 us -> 13.5 us
  waiting for transfers between devices: 17.5 us -> 16.7 us
    ppermute x8, waiting for transfers between devices: 5.33 us -> 4.21 us  [swapped_along(): return lax.ppermute(x, axis, pairs)]
    pallas_call x13 -> x12, Pallas kernels: 14.3 us -> 13.5 us  [call(): pl.pallas_call(kernel, out_shape=out_shape, in_specs=[in_spec] * len(inpu...]
  transfers between devices with their start and end apart: 15 -> 15, of which waited for: 8 -> 7; matrix products, arithmetic and copies ran while one was open for 0% -> 0% of each run, Pallas kernels for 13% -> 12%
where the time goes in v5:
time: 64.1 us; the launch traced here: 63 us
  starting transfers between devices  32.5 us (51%)
  waiting for transfers between devices  16.7 us (26%)
  Pallas kernels  13.5 us (21%)
    ppermute x7, starting transfers between devices, xor_swap(): lax.ppermute(x, 'az', [(i, i ^ bit) for i in range(lax.axis_size('az'))])  18.8 us
    ppermute x8, starting transfers between devices, swapped_along(): return lax.ppermute(x, axis, pairs)  13.6 us
    pallas_call x12, Pallas kernels, call(): pl.pallas_call(kernel, out_shape=out_shape, in_specs=[in_spec] * len(inpu...  13.5 us
    ppermute x7, waiting for transfers between devices, xor_swap(): lax.ppermute(x, 'az', [(i, i ^ bit) for i in range(lax.axis_size('az'))])  12.5 us
    ppermute x8, waiting for transfers between devices, swapped_along(): return lax.ppermute(x, axis, pairs)  4.21 us
  transfers between devices with their start and end apart: 15, of which 7 were waited for; matrix products, arithmetic and copies ran while one was open for 0% of the time, Pallas kernels for 12%

profile of v5, /device:TPU:6, one launch (start us, length us, event | category | flops | bytes accessed | tf_op | source)
XLA Modules:
  0.0 63.0 jit_solution(16213750918244394079)
XLA Ops:
  0.0 0.0 copy-start
  0.0 6.3 %collective-permute-start.2 = (f32[5,4,256]{2,1,0:T(4,128)}, f32[5,4,256]{2,1,0:T(4,128)S(1)}, u32[]{:S(2)}, u32[]{:S(2)}) collective-permute-start(f32[5,4,256]{2,1,0:T(4,128)} %bitcast.3), channel_id=1, source_target_pairs={{0,24},{1,25},{2,26},{3,27},{4,28},{5,29},{6,30},{7,31},{8,16},{9,... | collective-permute-start | bytes 61448 | tf_op jit(solution)/shard_map/ppermute | solution.py:582
  6.3 1.3 %shard_map.73 = (f32[5,4,32,256]{3,2,1,0:T(8,128)S(1)}, f32[4,32,256]{2,1,0:T(8,128)S(1)}, f32[128,256]{1,0:T(8,128)S(1)}, s32[4,32]{1,0:T(4,128)S(1)}, f32[2,25...) custom-call(f32[5,4,32,256]{3,2,1,0:T(8,128)} %flow.1, ...), custom_call_target="tpu_custom_call" | custom-call | flops 1200000000 | bytes 3600000 | tf_op jit(solution)/shard_map/pallas_call | solution.py:542
  7.6 1.7 %collective-permute-start = (f32[5,32,256]{2,1,0:T(8,128)S(1)}, f32[5,32,256]{2,1,0:T(8,128)S(1)}, u32[]{:S(2)}, u32[]{:S(2)}) collective-permute-start(f32[5,32,256]{2,1,0:T(8,128)S(1)} %get-tuple-element.44), channel_id=1, source_target_pairs={{0,32},{32,0},{64,96},{96,64},{128,160},{160,128},{192,224},{224,1... | collective-permute-start | bytes 491528 | tf_op jit(solution)/shard_map/ppermute | solution.py:562
  9.2 2.6 %collective-permute-start.1 = (f32[5,32,256]{2,1,0:T(8,128)S(1)}, f32[5,32,256]{2,1,0:T(8,128)S(1)}, u32[]{:S(2)}, u32[]{:S(2)}) collective-permute-start(f32[5,32,256]{2,1,0:T(8,128)S(1)} %get-tuple-element.45), channel_id=1, source_target_pairs={{32,64},{64,32},{96,128},{128,96},{160,192},{192,160},{33,65},{65,... | collective-permute-start | bytes 491528 | tf_op jit(solution)/shard_map/ppermute | solution.py:562
  11.8 0.0 collective-permute-done.2.high
  11.9 0.0 copy-done
  11.9 1.5 %collective-permute-start.3 = (f32[5,8,256]{2,1,0:T(8,128)S(1)}, f32[5,8,256]{2,1,0:T(8,128)S(1)}, u32[]{:S(2)}, u32[]{:S(2)}) collective-permute-start(f32[5,8,256]{2,1,0:T(8,128)S(1)} %shard_map.74.low), channel_id=1, source_target_pairs={{0,8},{1,9},{2,10},{3,11},{4,12},{5,13},{6,14},{7,15},{8,0},{9,1},... | collective-permute-start | bytes 122888 | tf_op jit(solution)/shard_map/ppermute | solution.py:582
  13.4 3.0 %shard_map.75 = (f32[17,75,8,128]{3,2,1,0:T(8,128)S(1)}, f32[8,50,8,128]{3,2,1,0:T(8,128)S(1)}, f32[16,3,8,128]{3,2,1,0:T(8,128)S(1)}, f32[32,128]{1,0:T(8,128)S(1)}, f32[256,128]{1,0:T(8,128)S(1)}) custom-call(f32[4,32,256]{2,1,0:T(8,128)S(1)} %get-tuple-element.50.coef_ref, f32[128,256]{1,0:T(8,128)S(1)} %get-tuple-element.51.mask_ref, ...), custom_call_target="tpu_custom_call" | custom-call | flops 3200000000 | bytes 9600000 | tf_op jit(solution)/shard_map/pallas_call | solution.py:542
  16.5 0.4 collective-permute-done.3.high
  16.9 1.0 %collective-permute-start.6 = (f32[5,16,256]{2,1,0:T(8,128)S(1)}, f32[5,16,256]{2,1,0:T(8,128)S(1)}, u32[]{:S(2)}, u32[]{:S(2)}) collective-permute-start(f32[5,16,256]{2,1,0:T(8,128)S(1)} %shard_map.76.low), channel_id=1, source_target_pairs={{0,4},{1,5},{2,6},{3,7},{4,0},{5,1},{6,2},{7,3},{8,12},{9,13},{10,... | collective-permute-start | bytes 245768 | tf_op jit(solution)/shard_map/ppermute | solution.py:582
  17.9 0.0 collective-permute-start.4
  17.9 2.8 %collective-permute-start.5 = (f32[5,4,256]{2,1,0:T(4,128)S(1)}, f32[5,4,256]{2,1,0:T(4,128)S(1)}, u32[]{:S(2)}, u32[]{:S(2)}) collective-permute-start(f32[5,4,256]{2,1,0:T(4,128)S(1)} %get-tuple-element.56), channel_id=1, source_target_pairs={{1,2},{2,1},{3,4},{4,3},{5,6},{6,5},{7,8},{8,7},{9,10},{10,9},{11,... | collective-permute-start | bytes 61448 | tf_op jit(solution)/shard_map/ppermute | solution.py:562
  20.7 0.6 collective-permute-done.6.high
  21.3 0.0 collective-permute-done.za
  21.3 0.0 collective-permute-done.1.zb
  21.3 3.3 %collective-permute-start.7 = (f32[5,32,256]{2,1,0:T(8,128)S(1)}, f32[5,32,256]{2,1,0:T(8,128)S(1)}, u32[]{:S(2)}, u32[]{:S(2)}) collective-permute-start(f32[5,32,256]{2,1,0:T(8,128)S(1)} %shard_map.77.low), channel_id=1, source_target_pairs={{0,2},{1,3},{2,0},{3,1},{4,6},{5,7},{6,4},{7,5},{8,10},{9,11},{10,... | collective-permute-start | bytes 491528 | tf_op jit(solution)/shard_map/ppermute | solution.py:582
  24.6 2.7 %shard_map.78 = (f32[11,75,8,128]{3,2,1,0:T(8,128)S(1)}, f32[10,50,8,128]{3,2,1,0:T(8,128)S(1)}, f32[32,128]{1,0:T(8,128)S(1)}) custom-call(f32[17,75,8,128]{3,2,1,0:T(8,128)S(1)} %get-tuple-element.61.m1, f32[32,128]{1,0:T(8,128)S(1)} %get-tuple-element.52.sd_in), custom_call_target="tpu_custom_call" | custom-call | flops 3000000000 | bytes 9000000 | tf_op jit(solution)/shard_map/pallas_call | solution.py:542
  27.3 0.0 collective-permute-done.4.ta
  27.3 0.0 collective-permute-done.5.tb
  27.3 1.6 %collective-permute-done.7.high = f32[5,32,256]{2,1,0:T(8,128)S(1)} collective-permute-done((f32[5,32,256]{2,1,0:T(8,128)S(1)}, f32[5,32,256]{2,1,0:T(8,128)S(1)}, u32[]{:S(2)}, u32[]{:S(2)}) %collective-permute-start.7) | collective-permute-done | bytes 163872 | tf_op jit(solution)/shard_map/ppermute | solution.py:582
  29.0 0.1 collective-permute-start.8
  29.1 0.6 shard_map.80.rhs_in
  29.7 1.0 %collective-permute-done.8.high = f32[5,64,256]{2,1,0:T(8,128)S(1)} collective-permute-done((f32[5,64,256]{2,1,0:T(8,128)S(1)}, f32[5,64,256]{2,1,0:T(8,128)S(1)}, u32[]{:S(2)}, u32[]{:S(2)}) %collective-permute-start.8) | collective-permute-done | bytes 327712 | tf_op jit(solution)/shard_map/ppermute | solution.py:582
  30.7 1.4 %shard_map.81 = (f32[20,5,8,128]{3,2,1,0:T(8,128)S(1)}, f32[16,5,8,128]{3,2,1,0:T(8,128)S(1)}, f32[32,128]{1,0:T(8,128)S(1)}) custom-call(f32[5,256,128]{2,1,0:T(8,128)S(1)} %shard_map.80.rhs_in, f32[256,128]{1,0:T(8,128)S(1)} %get-tuple-element.57.mask_t, s32[4,32]{1,0:T(4,128)S(1)} %get-tuple-element.58.place, ...), custom_call_target="tpu_custom_call" | custom-call | flops 1200000000 | bytes 3600000 | tf_op jit(solution)/shard_map/pallas_call | solution.py:542
  32.1 3.3 %collective-permute-start.9 = (f32[32,128]{1,0:T(8,128)S(1)}, f32[32,128]{1,0:T(8,128)S(1)}, u32[]{:S(2)}, u32[]{:S(2)}) collective-permute-start(f32[32,128]{1,0:T(8,128)S(1)} %get-tuple-element.68.joint), channel_id=1, source_target_pairs={{0,16},{1,17},{2,18},{3,19},{4,20},{5,21},{6,22},{7,23},{8,24},{9,... | collective-permute-start | bytes 49160 | tf_op jit(solution)/shard_map/ppermute | solution.py:582
  35.4 4.6 %collective-permute-done.9.other_joint = f32[32,128]{1,0:T(8,128)S(1)} collective-permute-done((f32[32,128]{1,0:T(8,128)S(1)}, f32[32,128]{1,0:T(8,128)S(1)}, u32[]{:S(2)}, u32[]{:S(2)}) %collective-permute-start.9) | collective-permute-done | bytes 16416 | tf_op jit(solution)/shard_map/ppermute | solution.py:582
  39.9 1.3 %shard_map.82 = (f32[5,4,32,256]{3,2,1,0:T(8,128)S(1)}, f32[5,32,256]{2,1,0:T(8,128)S(1)}, f32[5,32,256]{2,1,0:T(8,128)S(1)}, f32[5,4,256]{2,1,0:T(4,128)S(1)}, ...) custom-call(f32[32,128]{1,0:T(8,128)S(1)} %get-tuple-element.68.joint, f32[32,128]{1,0:T(8,128)S(1)} %collective-permute-done.9.other_joint, ...), custom_call_target="tpu_custom_call" | custom-call | flops 1300000000 | bytes 3900000 | tf_op jit(solution)/shard_map/pallas_call | solution.py:542
  41.3 0.1 collective-permute-start.10
  41.4 3.7 %collective-permute-start.11 = (f32[5,32,256]{2,1,0:T(8,128)S(1)}, f32[5,32,256]{2,1,0:T(8,128)S(1)}, u32[]{:S(2)}, u32[]{:S(2)}) collective-permute-start(f32[5,32,256]{2,1,0:T(8,128)S(1)} %get-tuple-element.74), channel_id=1, source_target_pairs={{32,64},{64,32},{96,128},{128,96},{160,192},{192,160},{33,65},{65,... | collective-permute-start | bytes 491528 | tf_op jit(solution)/shard_map/ppermute | solution.py:562
  45.1 1.7 %collective-permute-start.12 = (f32[5,4,256]{2,1,0:T(4,128)S(1)}, f32[5,4,256]{2,1,0:T(4,128)S(1)}, u32[]{:S(2)}, u32[]{:S(2)}) collective-permute-start(f32[5,4,256]{2,1,0:T(4,128)S(1)} %get-tuple-element.75), channel_id=1, source_target_pairs={{1,2},{2,1},{3,4},{4,3},{5,6},{6,5},{7,8},{8,7},{9,10},{10,9},{11,... | collective-permute-start | bytes 61448 | tf_op jit(solution)/shard_map/ppermute | solution.py:562
  46.8 1.0 %collective-permute-start.13 = (f32[5,4,256]{2,1,0:T(4,128)S(1)}, f32[5,4,256]{2,1,0:T(4,128)S(1)}, u32[]{:S(2)}, u32[]{:S(2)}) collective-permute-start(f32[5,4,256]{2,1,0:T(4,128)S(1)} %get-tuple-element.76), channel_id=1, source_target_pairs={{0,1},{1,0},{2,3},{3,2},{4,5},{5,4},{6,7},{7,6},{8,9},{9,8},{10,11... | collective-permute-start | bytes 61448 | tf_op jit(solution)/shard_map/ppermute | solution.py:562
  47.8 4.2 %collective-permute-done.12.tb = f32[5,4,256]{2,1,0:T(4,128)S(1)} collective-permute-done((f32[5,4,256]{2,1,0:T(4,128)S(1)}, f32[5,4,256]{2,1,0:T(4,128)S(1)}, u32[]{:S(2)}, u32[]{:S(2)}) %collective-permute-start.12) | collective-permute-done | bytes 20512 | tf_op jit(solution)/shard_map/ppermute | solution.py:562
  52.0 0.0 collective-permute-done.13.ta
  52.0 0.0 collective-permute-done.10.za
  52.0 0.0 collective-permute-done.11.zb
  52.0 1.4 %shard_map.83 = (f32[20,5,8,128]{3,2,1,0:T(8,128)S(1)}, f32[16,5,8,128]{3,2,1,0:T(8,128)S(1)}, f32[8,128]{1,0:T(8,128)S(1)}) custom-call(f32[5,4,32,256]{3,2,1,0:T(8,128)S(1)} %get-tuple-element.72.u.first, f32[5,32,256]{2,1,0:T(8,128)S(1)} %collective-permute-done.10.za, f32[5,32,256]{2,1,0:T(8,128)S(1)} %collective-permute-done.11.zb, ...), custom_call_target="tpu_custom_call" | custom-call | flops 1300000000 | bytes 3900000 | tf_op jit(solution)/shard_map/pallas_call | solution.py:542
  53.4 3.3 %collective-permute-start.14 = (f32[8,128]{1,0:T(8,128)S(1)}, f32[8,128]{1,0:T(8,128)S(1)}, u32[]{:S(2)}, u32[]{:S(2)}) collective-permute-start(f32[8,128]{1,0:T(8,128)S(1)} %get-tuple-element.77.y_own), channel_id=1, source_target_pairs={{0,16},{1,17},{2,18},{3,19},{4,20},{5,21},{6,22},{7,23},{8,24},{9,... | collective-permute-start | bytes 12296 | tf_op jit(solution)/shard_map/ppermute | solution.py:582
  56.7 4.3 %collective-permute-done.14.y_other = f32[8,128]{1,0:T(8,128)S(1)} collective-permute-done((f32[8,128]{1,0:T(8,128)S(1)}, f32[8,128]{1,0:T(8,128)S(1)}, u32[]{:S(2)}, u32[]{:S(2)}) %collective-permute-start.14) | collective-permute-done | bytes 4128 | tf_op jit(solution)/shard_map/ppermute | solution.py:582
  61.0 1.9 %shard_map.84 = f32[5,4,32,256]{3,2,1,0:T(8,128)} custom-call(f32[8,128]{1,0:T(8,128)S(1)} %get-tuple-element.77.y_own, f32[8,128]{1,0:T(8,128)S(1)} %collective-permute-done.14.y_other, f32[50,128]{1,0:T(8,128)S(1)} %get-tuple-element.78.j_ref, f32[17,75,8,128]{3,2,1,0:T(8,128)S(1)} %get-tuple-element.61.m1, f32[11,75,8,128]{3,2,1,0:T(8,128)S(1)} %get-tuple-element.69.m2, ...), custom_call_target="tpu_custom_call" | custom-call | flops 2000000000 | bytes 6000000 | tf_op jit(solution)/shard_map/pallas_call | solution.py:542
  (4 shorter events, 0.0 us)
Async XLA Ops:
  0.0 11.9 %copy-start = (f32[1,4,5,256]{3,1,2,0:T(4,128)S(1)}, f32[1,4,5,256]{3,1,2,0:T(4,128)}, u32[]{:S(2)}) copy-start(f32[1,4,5,256]{3,1,2,0:T(4,128)} %param.11) | copy-start | bytes 61444
  0.0 11.8 %collective-permute-start.2 = (f32[5,4,256]{2,1,0:T(4,128)}, f32[5,4,256]{2,1,0:T(4,128)S(1)}, u32[]{:S(2)}, u32[]{:S(2)}) collective-permute-start(f32[5,4,256]{2,1,0:T(4,128)} %bitcast.3), channel_id=1, source_target_pairs={{0,24},{1,25},{2,26},{3,27},{4,28},{5,29},{6,30},{7,31},{8,16},{9,... | collective-permute-start | bytes 61448 | tf_op jit(solution)/shard_map/ppermute | solution.py:582
  7.6 13.8 %collective-permute-start = (f32[5,32,256]{2,1,0:T(8,128)S(1)}, f32[5,32,256]{2,1,0:T(8,128)S(1)}, u32[]{:S(2)}, u32[]{:S(2)}) collective-permute-start(f32[5,32,256]{2,1,0:T(8,128)S(1)} %get-tuple-element.44), channel_id=1, source_target_pairs={{0,32},{32,0},{64,96},{96,64},{128,160},{160,128},{192,224},{224,1... | collective-permute-start | bytes 491528 | tf_op jit(solution)/shard_map/ppermute | solution.py:562
  9.2 12.1 %collective-permute-start.1 = (f32[5,32,256]{2,1,0:T(8,128)S(1)}, f32[5,32,256]{2,1,0:T(8,128)S(1)}, u32[]{:S(2)}, u32[]{:S(2)}) collective-permute-start(f32[5,32,256]{2,1,0:T(8,128)S(1)} %get-tuple-element.45), channel_id=1, source_target_pairs={{32,64},{64,32},{96,128},{128,96},{160,192},{192,160},{33,65},{65,... | collective-permute-start | bytes 491528 | tf_op jit(solution)/shard_map/ppermute | solution.py:562
  11.9 5.0 %collective-permute-start.3 = (f32[5,8,256]{2,1,0:T(8,128)S(1)}, f32[5,8,256]{2,1,0:T(8,128)S(1)}, u32[]{:S(2)}, u32[]{:S(2)}) collective-permute-start(f32[5,8,256]{2,1,0:T(8,128)S(1)} %shard_map.74.low), channel_id=1, source_target_pairs={{0,8},{1,9},{2,10},{3,11},{4,12},{5,13},{6,14},{7,15},{8,0},{9,1},... | collective-permute-start | bytes 122888 | tf_op jit(solution)/shard_map/ppermute | solution.py:582
  16.9 4.4 %collective-permute-start.6 = (f32[5,16,256]{2,1,0:T(8,128)S(1)}, f32[5,16,256]{2,1,0:T(8,128)S(1)}, u32[]{:S(2)}, u32[]{:S(2)}) collective-permute-start(f32[5,16,256]{2,1,0:T(8,128)S(1)} %shard_map.76.low), channel_id=1, source_target_pairs={{0,4},{1,5},{2,6},{3,7},{4,0},{5,1},{6,2},{7,3},{8,12},{9,13},{10,... | collective-permute-start | bytes 245768 | tf_op jit(solution)/shard_map/ppermute | solution.py:582
  17.9 9.4 %collective-permute-start.4 = (f32[5,4,256]{2,1,0:T(4,128)S(1)}, f32[5,4,256]{2,1,0:T(4,128)S(1)}, u32[]{:S(2)}, u32[]{:S(2)}) collective-permute-start(f32[5,4,256]{2,1,0:T(4,128)S(1)} %get-tuple-element.54), channel_id=1, source_target_pairs={{0,1},{1,0},{2,3},{3,2},{4,5},{5,4},{6,7},{7,6},{8,9},{9,8},{10,11... | collective-permute-start | bytes 61448 | tf_op jit(solution)/shard_map/ppermute | solution.py:562
  17.9 9.4 %collective-permute-start.5 = (f32[5,4,256]{2,1,0:T(4,128)S(1)}, f32[5,4,256]{2,1,0:T(4,128)S(1)}, u32[]{:S(2)}, u32[]{:S(2)}) collective-permute-start(f32[5,4,256]{2,1,0:T(4,128)S(1)} %get-tuple-element.56), channel_id=1, source_target_pairs={{1,2},{2,1},{3,4},{4,3},{5,6},{6,5},{7,8},{8,7},{9,10},{10,9},{11,... | collective-permute-start | bytes 61448 | tf_op jit(solution)/shard_map/ppermute | solution.py:562
  21.3 7.6 %collective-permute-start.7 = (f32[5,32,256]{2,1,0:T(8,128)S(1)}, f32[5,32,256]{2,1,0:T(8,128)S(1)}, u32[]{:S(2)}, u32[]{:S(2)}) collective-permute-start(f32[5,32,256]{2,1,0:T(8,128)S(1)} %shard_map.77.low), channel_id=1, source_target_pairs={{0,2},{1,3},{2,0},{3,1},{4,6},{5,7},{6,4},{7,5},{8,10},{9,11},{10,... | collective-permute-start | bytes 491528 | tf_op jit(solution)/shard_map/ppermute | solution.py:582
  29.0 1.7 %collective-permute-start.8 = (f32[5,64,256]{2,1,0:T(8,128)S(1)}, f32[5,64,256]{2,1,0:T(8,128)S(1)}, u32[]{:S(2)}, u32[]{:S(2)}) collective-permute-start(f32[5,64,256]{2,1,0:T(8,128)S(1)} %shard_map.79.low), channel_id=1, source_target_pairs={{0,1},{1,0},{2,3},{3,2},{4,5},{5,4},{6,7},{7,6},{8,9},{9,8},{10,11... | collective-permute-start | bytes 983048 | tf_op jit(solution)/shard_map/ppermute | solution.py:582
  32.1 7.9 %collective-permute-start.9 = (f32[32,128]{1,0:T(8,128)S(1)}, f32[32,128]{1,0:T(8,128)S(1)}, u32[]{:S(2)}, u32[]{:S(2)}) collective-permute-start(f32[32,128]{1,0:T(8,128)S(1)} %get-tuple-element.68.joint), channel_id=1, source_target_pairs={{0,16},{1,17},{2,18},{3,19},{4,20},{5,21},{6,22},{7,23},{8,24},{9,... | collective-permute-start | bytes 49160 | tf_op jit(solution)/shard_map/ppermute | solution.py:582
  41.3 10.8 %collective-permute-start.10 = (f32[5,32,256]{2,1,0:T(8,128)S(1)}, f32[5,32,256]{2,1,0:T(8,128)S(1)}, u32[]{:S(2)}, u32[]{:S(2)}) collective-permute-start(f32[5,32,256]{2,1,0:T(8,128)S(1)} %get-tuple-element.73), channel_id=1, source_target_pairs={{0,32},{32,0},{64,96},{96,64},{128,160},{160,128},{192,224},{224,1... | collective-permute-start | bytes 491528 | tf_op jit(solution)/shard_map/ppermute | solution.py:562
  41.4 10.7 %collective-permute-start.11 = (f32[5,32,256]{2,1,0:T(8,128)S(1)}, f32[5,32,256]{2,1,0:T(8,128)S(1)}, u32[]{:S(2)}, u32[]{:S(2)}) collective-permute-start(f32[5,32,256]{2,1,0:T(8,128)S(1)} %get-tuple-element.74), channel_id=1, source_target_pairs={{32,64},{64,32},{96,128},{128,96},{160,192},{192,160},{33,65},{65,... | collective-permute-start | bytes 491528 | tf_op jit(solution)/shard_map/ppermute | solution.py:562
  45.1 6.9 %collective-permute-start.12 = (f32[5,4,256]{2,1,0:T(4,128)S(1)}, f32[5,4,256]{2,1,0:T(4,128)S(1)}, u32[]{:S(2)}, u32[]{:S(2)}) collective-permute-start(f32[5,4,256]{2,1,0:T(4,128)S(1)} %get-tuple-element.75), channel_id=1, source_target_pairs={{1,2},{2,1},{3,4},{4,3},{5,6},{6,5},{7,8},{8,7},{9,10},{10,9},{11,... | collective-permute-start | bytes 61448 | tf_op jit(solution)/shard_map/ppermute | solution.py:562
  46.8 5.2 %collective-permute-start.13 = (f32[5,4,256]{2,1,0:T(4,128)S(1)}, f32[5,4,256]{2,1,0:T(4,128)S(1)}, u32[]{:S(2)}, u32[]{:S(2)}) collective-permute-start(f32[5,4,256]{2,1,0:T(4,128)S(1)} %get-tuple-element.76), channel_id=1, source_target_pairs={{0,1},{1,0},{2,3},{3,2},{4,5},{5,4},{6,7},{7,6},{8,9},{9,8},{10,11... | collective-permute-start | bytes 61448 | tf_op jit(solution)/shard_map/ppermute | solution.py:562
  53.4 7.6 %collective-permute-start.14 = (f32[8,128]{1,0:T(8,128)S(1)}, f32[8,128]{1,0:T(8,128)S(1)}, u32[]{:S(2)}, u32[]{:S(2)}) collective-permute-start(f32[8,128]{1,0:T(8,128)S(1)} %get-tuple-element.77.y_own), channel_id=1, source_target_pairs={{0,16},{1,17},{2,18},{3,19},{4,20},{5,21},{6,22},{7,23},{8,24},{9,... | collective-permute-start | bytes 12296 | tf_op jit(solution)/shard_map/ppermute | solution.py:582

commit v6 on v5

--- a/solution.py
+++ b/solution.py
@@ -388,7 +388,7 @@
 
 
 def doubling_bits():
-    return [bit for bit in (24, 8, 4, 2, 1) if bit < lax.axis_size("az")]
+    return [bit for bit in (24, 8, 2, 4, 1) if bit < lax.axis_size("az")]
 
 
 def table_place(index):
@@ -459,22 +459,14 @@
         y_ref[pl.ds(v, 1), :] = reduced[v]
 
 
-def backward_body(own, other, j_ref, m1, m2, scal, cst, e_ref, o_ref, x_ref, x_t):
-    a, b = load_mat(cst, 0, 0), load_mat(cst, 1, 0)
+def particular(m1, m2, e_ref, x_ref):
     sub = lax.broadcasted_iota(jnp.int32, (SEG, LANES), 0)
-    cur = []
-    for i in range(N):
-        acc = j_ref[pl.ds(i * N, 1), :] * own[0]
-        for k in range(N):
-            if k > 0:
-                acc = acc + j_ref[pl.ds(i * N + k, 1), :] * own[k]
-            acc = acc + j_ref[pl.ds(NN + i * N + k, 1), :] * other[k]
-        cur.append(jnp.broadcast_to(acc, (SEG, LANES)))
+    cur = [jnp.zeros((SEG, LANES), F32)] * N
 
     def recover(mb, slot, rhs, high, low):
         o = mat_vec(load_mat(mb, slot, OUT0), high)
         i = mat_vec(load_mat(mb, slot, IN0), low)
-        total = [e_ref[rhs, v] + o[v] + i[v] for v in range(N)]
+        total = [e_ref[rhs, v] + (o[v] + i[v]) for v in range(N)]
         return mat_vec(load_mat(mb, slot, D0), total)
 
     for level, s in ((2, 4), (1, 2), (0, 1)):
@@ -490,10 +482,79 @@
         )
         for v in range(N):
             x_ref[m, v] = new[v]
-    low = [x_ref[0, v] for v in range(N)]
+
+
+def response(m1, m2, q):
+    sub = lax.broadcasted_iota(jnp.int32, (SEG, LANES), 0)
+    one, zero = jnp.ones((SEG, LANES), F32), jnp.zeros((SEG, LANES), F32)
+    cur = [[one if i == j else zero for j in range(N)] for i in range(N)]
+
+    def recover(mb, slot, high, low):
+        o = mat_mul(load_mat(mb, slot, OUT0), high)
+        i = mat_mul(load_mat(mb, slot, IN0), low)
+        total = [[o[r][c] + i[r][c] for c in range(N)] for r in range(N)]
+        return mat_mul(load_mat(mb, slot, D0), total)
+
+    for level, s in ((2, 4), (1, 2), (0, 1)):
+        high = [[up(x, s) for x in row] for row in cur]
+        low = [[down(x, s) for x in row] for row in cur]
+        new = recover(m2, level, high, low)
+        cur = [
+            [jnp.where(sub % (2 * s) == s, new[r][c], cur[r][c]) for c in range(N)] for r in range(N)
+        ]
+    store_mat(q, 0, 0, cur)
+    store_mat(q, HALF, 0, [[up(x, 1) for x in row] for row in cur])
+
+    def later(it, c):
+        s = jnp.where(it < 1, 4, jnp.where(it < 3, 2, 1))
+        n = s * (2 * (it - jnp.where(it < 1, 0, jnp.where(it < 3, 1, 3))) + 1)
+        high, low = load_mat(q, 2 * (n + s), 0), load_mat(q, 2 * (n - s), 0)
+        store_mat(q, 2 * n, 0, recover(m2, slot_of(n), high, low))
+        return c
+
+    lax.fori_loop(0, HALF // 2 - 1, later, 0)
+
+    def first(it, c):
+        m = 2 * it + 1
+        store_mat(q, m, 0, recover(m1, m, load_mat(q, m + 1, 0), load_mat(q, m - 1, 0)))
+        return c
+
+    lax.fori_loop(0, HALF // 2, first, 0)
+
+
+def response_kernel(m1, m2, e_ref, q, x_ref):
+    particular(m1, m2, e_ref, x_ref)
+    response(m1, m2, q)
+
+
+def particular_kernel(m1, m2, e_ref, x_ref):
+    particular(m1, m2, e_ref, x_ref)
+
+
+def axis_value(own, other, j_ref):
+    cur = []
+    for i in range(N):
+        acc = j_ref[pl.ds(i * N, 1), :] * own[0]
+        for k in range(N):
+            if k > 0:
+                acc = acc + j_ref[pl.ds(i * N + k, 1), :] * own[k]
+            acc = acc + j_ref[pl.ds(NN + i * N + k, 1), :] * other[k]
+        cur.append(jnp.broadcast_to(acc, (SEG, LANES)))
+    return cur
+
+
+def backward_body(own, other, j_ref, q, part, scal, cst, o_ref, x_t):
+    a, b = load_mat(cst, 0, 0), load_mat(cst, 1, 0)
+    axis = axis_value(own, other, j_ref)
+
+    def even(p):
+        add = mat_vec(load_mat(q, p, 0), axis)
+        return [part[p, v] + add[v] for v in range(N)]
+
+    low = even(0)
     for m in range(HALF):
         inv, fl, fr = scal[m, 0], scal[m, 1], scal[m, 2]
-        high = [x_ref[m + 1, v] for v in range(N)]
+        high = even(m + 1)
         ta = mat_vec(a, high)
         tb = mat_vec(b, low)
         for v in range(N):
@@ -504,13 +565,13 @@
 
 
 def backward_first_kernel(
-    joint, other_joint, m1, m2, scal, cst, e_ref, o_ref,
-    out, za, zb, ta, tb, j_ref, x_ref, x_t,
+    joint, other_joint, q, part, scal, cst, o_ref,
+    out, za, zb, ta, tb, j_ref, x_t,
 ):
     join(joint, other_joint, j_ref)
     own = [joint[pl.ds(VEC_ROW + v, 1), :] for v in range(N)]
     other = [other_joint[pl.ds(VEC_ROW + v, 1), :] for v in range(N)]
-    backward_body(own, other, j_ref, m1, m2, scal, cst, e_ref, o_ref, x_ref, x_t)
+    backward_body(own, other, j_ref, q, part, scal, cst, o_ref, x_t)
     _, planes, sectors, radial = out.shape
     for v in range(N):
         out[v] = x_t[v].T.reshape(planes, sectors, radial)
@@ -519,11 +580,11 @@
 
 
 def backward_second_kernel(
-    y_own, y_other, j_ref, m1, m2, scal, cst, e_ref, o_ref, first, out, x_ref, x_t, stage, sem
+    y_own, y_other, j_ref, q, part, scal, cst, o_ref, first, out, x_t, stage, sem
 ):
     own = [y_own[pl.ds(v, 1), :] for v in range(N)]
     other = [y_other[pl.ds(v, 1), :] for v in range(N)]
-    backward_body(own, other, j_ref, m1, m2, scal, cst, e_ref, o_ref, x_ref, x_t)
+    backward_body(own, other, j_ref, q, part, scal, cst, o_ref, x_t)
     _, planes, sectors, radial = out.shape
     copies = [pltpu.make_async_copy(stage.at[v], out.at[v], sem.at[v]) for v in range(N)]
     for v in range(N):
@@ -626,7 +687,7 @@
         hbm=True,
     )
     rows = append(rows, after(got, cst))
-    halo, done = {"za": z_near(za), "zb": z_far(zb)}, []
+    halo, done = {"zb": z_far(zb)}, []
 
     def factor(rows, got):
         done.extend(
@@ -648,9 +709,10 @@
 
     def sector_halos(rows, got):
         halo["tb"], halo["ta"] = t_far(after(tb, rows)), t_near(after(ta, rows))
-        return after(got, halo["za"], halo["zb"])
+        return after(got, halo["zb"])
 
     def factor_rest(rows, got):
+        halo["za"] = z_near(after(za, rows))
         m1, sd = done[0], done[3]
         done.extend(
             call(
@@ -665,7 +727,7 @@
                 3.0,
             )
         )
-        return after(got, done[-1], halo["ta"], halo["tb"])
+        return after(got, done[-1], halo["ta"], halo["tb"], halo["za"])
 
     fillers = [factor, sector_halos, factor_rest]
     for i, bit in enumerate(bits[1:-1]):
@@ -684,7 +746,8 @@
     others = after(others, rhs)
 
     fwd_outs = [(HALF + 4, N) + tile, (HALF, N) + tile]
-    back_scratch = [(HALF + 1, N) + tile, columns]
+    back_scratch = [columns]
+    evens = (HALF + 1, N) + tile
     e1, o1, joint = call(
         forward_first_kernel,
         (rhs, mask_t, place, others, f1, f2, scal, cst, sd),
@@ -692,10 +755,11 @@
         [columns],
         1.2,
     )
-    other_joint = xor_swap(joint, half_turn)
+    q, part = call(response_kernel, (m1, m2, e1), [(HALF + 1, NN) + tile, evens], [], 3.0)
+    other_joint = after(xor_swap(joint, half_turn), q)
     delta, za, zb, ta, tb, axis_inverse = call(
         backward_first_kernel,
-        (joint, other_joint, m1, m2, scal, cst, e1, o1),
+        (joint, other_joint, q, part, scal, cst, o1),
         [field] + edges + [(2 * NN, LANES)],
         back_scratch,
         1.3,
@@ -708,10 +772,11 @@
         [columns],
         1.3,
     )
-    other_y2 = xor_swap(y2, half_turn)
+    (part,) = call(particular_kernel, (m1, m2, e2), [evens], [], 1.0)
+    other_y2 = after(xor_swap(y2, half_turn), part)
     (update,) = call(
         backward_second_kernel,
-        (y2, other_y2, axis_inverse, m1, m2, scal, cst, e2, o2, delta),
+        (y2, other_y2, axis_inverse, q, part, scal, cst, o2, delta),
         [field],
         back_scratch + [field, pltpu.SemaphoreType.DMA((N,))],
         2.0,

time: 64.1 us -> 63.2 us (0.986)
  starting transfers between devices: 32.5 us -> 28.2 us
  Pallas kernels: 13.5 us -> 15.7 us
  waiting for transfers between devices: 16.7 us -> 18.3 us
    ppermute x7, starting transfers between devices: 18.8 us -> 16.2 us  [xor_swap(): lax.ppermute(x, 'az', [(i, i ^ bit) for i in range(lax.axis_size('az'))])]
    pallas_call x12 -> x14, Pallas kernels: 13.5 us -> 15.7 us  [call(): pl.pallas_call(kernel, out_shape=out_shape, in_specs=[in_spec] * len(inpu...]
    ppermute x8, waiting for transfers between devices: 4.21 us -> 6.18 us  [swapped_along(): return lax.ppermute(x, axis, pairs)]
    ppermute x8, starting transfers between devices: 13.6 us -> 12 us  [swapped_along(): return lax.ppermute(x, axis, pairs)]
  transfers between devices with their start and end apart: 15 -> 15, of which waited for: 7 -> 8; matrix products, arithmetic and copies ran while one was open for 0% -> 0% of each run, Pallas kernels for 12% -> 16%
where the time goes in v6:
time: 63.2 us; the launch traced here: 62.6 us
  starting transfers between devices  28.2 us (45%)
  waiting for transfers between devices  18.3 us (29%)
  Pallas kernels  15.7 us (25%)
    ppermute x7, starting transfers between devices, xor_swap(): lax.ppermute(x, 'az', [(i, i ^ bit) for i in range(lax.axis_size('az'))])  16.2 us
    pallas_call x14, Pallas kernels, call(): pl.pallas_call(kernel, out_shape=out_shape, in_specs=[in_spec] * len(inpu...  15.7 us
    ppermute x7, waiting for transfers between devices, xor_swap(): lax.ppermute(x, 'az', [(i, i ^ bit) for i in range(lax.axis_size('az'))])  12.2 us
    ppermute x8, starting transfers between devices, swapped_along(): return lax.ppermute(x, axis, pairs)  12 us
    ppermute x8, waiting for transfers between devices, swapped_along(): return lax.ppermute(x, axis, pairs)  6.18 us
  transfers between devices with their start and end apart: 15, of which 8 were waited for; matrix products, arithmetic and copies ran while one was open for 0% of the time, Pallas kernels for 16%

profile of v6, /device:TPU:6, one launch (start us, length us, event | category | flops | bytes accessed | tf_op | source)
XLA Modules:
  0.0 62.6 jit_solution(1763117375562981729)
XLA Ops:
  0.0 0.0 copy-start
  0.0 6.3 %collective-permute-start = (f32[5,4,256]{2,1,0:T(4,128)}, f32[5,4,256]{2,1,0:T(4,128)S(1)}, u32[]{:S(2)}, u32[]{:S(2)}) collective-permute-start(f32[5,4,256]{2,1,0:T(4,128)} %bitcast.3), channel_id=1, source_target_pairs={{0,24},{1,25},{2,26},{3,27},{4,28},{5,29},{6,30},{7,31},{8,16},{9,... | collective-permute-start | bytes 61448 | tf_op jit(solution)/shard_map/ppermute | solution.py:643
  6.3 1.3 %shard_map.73 = (f32[5,4,32,256]{3,2,1,0:T(8,128)S(1)}, f32[4,32,256]{2,1,0:T(8,128)S(1)}, f32[128,256]{1,0:T(8,128)S(1)}, s32[4,32]{1,0:T(4,128)S(1)}, f32[2,25...) custom-call(f32[5,4,32,256]{3,2,1,0:T(8,128)} %flow.1, ...), custom_call_target="tpu_custom_call" | custom-call | flops 1200000000 | bytes 3600000 | tf_op jit(solution)/shard_map/pallas_call | solution.py:603
  7.6 3.8 %collective-permute-start.3 = (f32[5,32,256]{2,1,0:T(8,128)S(1)}, f32[5,32,256]{2,1,0:T(8,128)S(1)}, u32[]{:S(2)}, u32[]{:S(2)}) collective-permute-start(f32[5,32,256]{2,1,0:T(8,128)S(1)} %get-tuple-element.57), channel_id=1, source_target_pairs={{32,64},{64,32},{96,128},{128,96},{160,192},{192,160},{33,65},{65,... | collective-permute-start | bytes 491528 | tf_op jit(solution)/shard_map/ppermute | solution.py:623
  11.3 0.0 collective-permute-done.high
  11.3 0.0 copy-done
  11.4 1.5 %collective-permute-start.1 = (f32[5,8,256]{2,1,0:T(8,128)S(1)}, f32[5,8,256]{2,1,0:T(8,128)S(1)}, u32[]{:S(2)}, u32[]{:S(2)}) collective-permute-start(f32[5,8,256]{2,1,0:T(8,128)S(1)} %shard_map.74.low), channel_id=1, source_target_pairs={{0,8},{1,9},{2,10},{3,11},{4,12},{5,13},{6,14},{7,15},{8,0},{9,1},... | collective-permute-start | bytes 122888 | tf_op jit(solution)/shard_map/ppermute | solution.py:643
  12.9 3.0 %shard_map.75 = (f32[17,75,8,128]{3,2,1,0:T(8,128)S(1)}, f32[8,50,8,128]{3,2,1,0:T(8,128)S(1)}, f32[16,3,8,128]{3,2,1,0:T(8,128)S(1)}, f32[32,128]{1,0:T(8,128)S(1)}, f32[256,128]{1,0:T(8,128)S(1)}) custom-call(f32[4,32,256]{2,1,0:T(8,128)S(1)} %get-tuple-element.53.coef_ref, f32[128,256]{1,0:T(8,128)S(1)} %get-tuple-element.54.mask_ref, ...), custom_call_target="tpu_custom_call" | custom-call | flops 3200000000 | bytes 9600000 | tf_op jit(solution)/shard_map/pallas_call | solution.py:603
  15.9 0.4 collective-permute-done.1.high
  16.4 2.9 %collective-permute-start.2 = (f32[5,16,256]{2,1,0:T(8,128)S(1)}, f32[5,16,256]{2,1,0:T(8,128)S(1)}, u32[]{:S(2)}, u32[]{:S(2)}) collective-permute-start(f32[5,16,256]{2,1,0:T(8,128)S(1)} %shard_map.76.low), channel_id=1, source_target_pairs={{0,2},{1,3},{2,0},{3,1},{4,6},{5,7},{6,4},{7,5},{8,10},{9,11},{10,... | collective-permute-start | bytes 245768 | tf_op jit(solution)/shard_map/ppermute | solution.py:643
  19.3 0.0 collective-permute-start.5
  19.3 0.8 %collective-permute-start.6 = (f32[5,4,256]{2,1,0:T(4,128)S(1)}, f32[5,4,256]{2,1,0:T(4,128)S(1)}, u32[]{:S(2)}, u32[]{:S(2)}) collective-permute-start(f32[5,4,256]{2,1,0:T(4,128)S(1)} %get-tuple-element.63), channel_id=1, source_target_pairs={{1,2},{2,1},{3,4},{4,3},{5,6},{6,5},{7,8},{8,7},{9,10},{10,9},{11,... | collective-permute-start | bytes 61448 | tf_op jit(solution)/shard_map/ppermute | solution.py:623
  20.1 2.2 %collective-permute-done.2.high = f32[5,16,256]{2,1,0:T(8,128)S(1)} collective-permute-done((f32[5,16,256]{2,1,0:T(8,128)S(1)}, f32[5,16,256]{2,1,0:T(8,128)S(1)}, u32[]{:S(2)}, u32[]{:S(2)}) %collective-permute-start.2) | collective-permute-done | bytes 81952 | tf_op jit(solution)/shard_map/ppermute | solution.py:643
  22.3 0.0 collective-permute-done.3.zb
  22.3 1.1 %collective-permute-start.7 = (f32[5,32,256]{2,1,0:T(8,128)S(1)}, f32[5,32,256]{2,1,0:T(8,128)S(1)}, u32[]{:S(2)}, u32[]{:S(2)}) collective-permute-start(f32[5,32,256]{2,1,0:T(8,128)S(1)} %shard_map.77.low), channel_id=1, source_target_pairs={{0,4},{1,5},{2,6},{3,7},{4,0},{5,1},{6,2},{7,3},{8,12},{9,13},{10,... | collective-permute-start | bytes 491528 | tf_op jit(solution)/shard_map/ppermute | solution.py:643
  23.4 0.0 collective-permute-start.4
  23.4 2.7 %shard_map.78 = (f32[11,75,8,128]{3,2,1,0:T(8,128)S(1)}, f32[10,50,8,128]{3,2,1,0:T(8,128)S(1)}, f32[32,128]{1,0:T(8,128)S(1)}) custom-call(f32[17,75,8,128]{3,2,1,0:T(8,128)S(1)} %get-tuple-element.67.m1, f32[32,128]{1,0:T(8,128)S(1)} %get-tuple-element.55.sd_in), custom_call_target="tpu_custom_call" | custom-call | flops 3000000000 | bytes 9000000 | tf_op jit(solution)/shard_map/pallas_call | solution.py:603
  26.1 0.0 collective-permute-done.5.ta
  26.1 0.1 collective-permute-done.6.tb
  26.2 2.6 %collective-permute-done.4.za = f32[5,32,256]{2,1,0:T(8,128)S(1)} collective-permute-done((f32[5,32,256]{2,1,0:T(8,128)S(1)}, f32[5,32,256]{2,1,0:T(8,128)S(1)}, u32[]{:S(2)}, u32[]{:S(2)}) %collective-permute-start.4) | collective-permute-done | bytes 163872 | tf_op jit(solution)/shard_map/ppermute | solution.py:623
  28.7 0.0 collective-permute-done.7.high
  28.8 0.1 collective-permute-start.8
  28.9 0.6 shard_map.80.rhs_in
  29.5 1.0 %collective-permute-done.8.high = f32[5,64,256]{2,1,0:T(8,128)S(1)} collective-permute-done((f32[5,64,256]{2,1,0:T(8,128)S(1)}, f32[5,64,256]{2,1,0:T(8,128)S(1)}, u32[]{:S(2)}, u32[]{:S(2)}) %collective-permute-start.8) | collective-permute-done | bytes 327712 | tf_op jit(solution)/shard_map/ppermute | solution.py:643
  30.5 1.4 %shard_map.81 = (f32[20,5,8,128]{3,2,1,0:T(8,128)S(1)}, f32[16,5,8,128]{3,2,1,0:T(8,128)S(1)}, f32[32,128]{1,0:T(8,128)S(1)}) custom-call(f32[5,256,128]{2,1,0:T(8,128)S(1)} %shard_map.80.rhs_in, f32[256,128]{1,0:T(8,128)S(1)} %get-tuple-element.64.mask_t, s32[4,32]{1,0:T(4,128)S(1)} %get-tuple-element.65.place, ...), custom_call_target="tpu_custom_call" | custom-call | flops 1200000000 | bytes 3600000 | tf_op jit(solution)/shard_map/pallas_call | solution.py:603
  31.9 2.0 %collective-permute-start.9 = (f32[32,128]{1,0:T(8,128)S(1)}, f32[32,128]{1,0:T(8,128)S(1)}, u32[]{:S(2)}, u32[]{:S(2)}) collective-permute-start(f32[32,128]{1,0:T(8,128)S(1)} %get-tuple-element.74.joint), channel_id=1, source_target_pairs={{0,16},{1,17},{2,18},{3,19},{4,20},{5,21},{6,22},{7,23},{8,24},{9,... | collective-permute-start | bytes 49160 | tf_op jit(solution)/shard_map/ppermute | solution.py:643
  33.9 2.2 %shard_map.82 = (f32[17,25,8,128]{3,2,1,0:T(8,128)S(1)}, f32[17,5,8,128]{3,2,1,0:T(8,128)S(1)}) custom-call(f32[17,75,8,128]{3,2,1,0:T(8,128)S(1)} %get-tuple-element.67.m1, f32[11,75,8,128]{3,2,1,0:T(8,128)S(1)} %get-tuple-element.75.m2, f32[20,5,8,128]{3,2,1,0:T(8,128)S(1)} %get-tuple-element.76.e_ref), custom_call_target="tpu_custom_call" | custom-call | flops 3000000000 | bytes 9000000 | tf_op jit(solution)/shard_map/pallas_call | solution.py:603
  36.1 3.5 %collective-permute-done.9.other_joint = f32[32,128]{1,0:T(8,128)S(1)} collective-permute-done((f32[32,128]{1,0:T(8,128)S(1)}, f32[32,128]{1,0:T(8,128)S(1)}, u32[]{:S(2)}, u32[]{:S(2)}) %collective-permute-start.9) | collective-permute-done | bytes 16416 | tf_op jit(solution)/shard_map/ppermute | solution.py:643
  39.6 1.1 %shard_map.83 = (f32[5,4,32,256]{3,2,1,0:T(8,128)S(1)}, f32[5,32,256]{2,1,0:T(8,128)S(1)}, f32[5,32,256]{2,1,0:T(8,128)S(1)}, f32[5,4,256]{2,1,0:T(4,128)S(1)}, ...) custom-call(f32[32,128]{1,0:T(8,128)S(1)} %get-tuple-element.74.joint, f32[32,128]{1,0:T(8,128)S(1)} %collective-permute-done.9.other_joint, ...), custom_call_target="tpu_custom_call" | custom-call | flops 1300000000 | bytes 3900000 | tf_op jit(solution)/shard_map/pallas_call | solution.py:603
  40.7 0.1 collective-permute-start.10
  40.8 4.0 %collective-permute-start.11 = (f32[5,32,256]{2,1,0:T(8,128)S(1)}, f32[5,32,256]{2,1,0:T(8,128)S(1)}, u32[]{:S(2)}, u32[]{:S(2)}) collective-permute-start(f32[5,32,256]{2,1,0:T(8,128)S(1)} %get-tuple-element.83), channel_id=1, source_target_pairs={{32,64},{64,32},{96,128},{128,96},{160,192},{192,160},{33,65},{65,... | collective-permute-start | bytes 491528 | tf_op jit(solution)/shard_map/ppermute | solution.py:623
  44.8 1.7 %collective-permute-start.12 = (f32[5,4,256]{2,1,0:T(4,128)S(1)}, f32[5,4,256]{2,1,0:T(4,128)S(1)}, u32[]{:S(2)}, u32[]{:S(2)}) collective-permute-start(f32[5,4,256]{2,1,0:T(4,128)S(1)} %get-tuple-element.84), channel_id=1, source_target_pairs={{1,2},{2,1},{3,4},{4,3},{5,6},{6,5},{7,8},{8,7},{9,10},{10,9},{11,... | collective-permute-start | bytes 61448 | tf_op jit(solution)/shard_map/ppermute | solution.py:623
  46.5 1.7 %collective-permute-start.13 = (f32[5,4,256]{2,1,0:T(4,128)S(1)}, f32[5,4,256]{2,1,0:T(4,128)S(1)}, u32[]{:S(2)}, u32[]{:S(2)}) collective-permute-start(f32[5,4,256]{2,1,0:T(4,128)S(1)} %get-tuple-element.85), channel_id=1, source_target_pairs={{0,1},{1,0},{2,3},{3,2},{4,5},{5,4},{6,7},{7,6},{8,9},{9,8},{10,11... | collective-permute-start | bytes 61448 | tf_op jit(solution)/shard_map/ppermute | solution.py:623
  48.2 3.5 %collective-permute-done.12.tb = f32[5,4,256]{2,1,0:T(4,128)S(1)} collective-permute-done((f32[5,4,256]{2,1,0:T(4,128)S(1)}, f32[5,4,256]{2,1,0:T(4,128)S(1)}, u32[]{:S(2)}, u32[]{:S(2)}) %collective-permute-start.12) | collective-permute-done | bytes 20512 | tf_op jit(solution)/shard_map/ppermute | solution.py:623
  51.7 0.0 collective-permute-done.13.ta
  51.7 0.0 collective-permute-done.10.za
  51.7 0.0 collective-permute-done.11.zb
  51.7 1.4 %shard_map.84 = (f32[20,5,8,128]{3,2,1,0:T(8,128)S(1)}, f32[16,5,8,128]{3,2,1,0:T(8,128)S(1)}, f32[8,128]{1,0:T(8,128)S(1)}) custom-call(f32[5,4,32,256]{3,2,1,0:T(8,128)S(1)} %get-tuple-element.81.u.first, f32[5,32,256]{2,1,0:T(8,128)S(1)} %collective-permute-done.10.za, f32[5,32,256]{2,1,0:T(8,128)S(1)} %collective-permute-done.11.zb, ...), custom_call_target="tpu_custom_call" | custom-call | flops 1300000000 | bytes 3900000 | tf_op jit(solution)/shard_map/pallas_call | solution.py:603
  53.1 2.2 %collective-permute-start.14 = (f32[8,128]{1,0:T(8,128)S(1)}, f32[8,128]{1,0:T(8,128)S(1)}, u32[]{:S(2)}, u32[]{:S(2)}) collective-permute-start(f32[8,128]{1,0:T(8,128)S(1)} %get-tuple-element.86.y_own), channel_id=1, source_target_pairs={{0,16},{1,17},{2,18},{3,19},{4,20},{5,21},{6,22},{7,23},{8,24},{9,... | collective-permute-start | bytes 12296 | tf_op jit(solution)/shard_map/ppermute | solution.py:643
  55.3 0.4 shard_map.85.part
  55.7 5.0 %collective-permute-done.14.y_other = f32[8,128]{1,0:T(8,128)S(1)} collective-permute-done((f32[8,128]{1,0:T(8,128)S(1)}, f32[8,128]{1,0:T(8,128)S(1)}, u32[]{:S(2)}, u32[]{:S(2)}) %collective-permute-start.14) | collective-permute-done | bytes 4128 | tf_op jit(solution)/shard_map/ppermute | solution.py:643
  60.7 1.7 %shard_map.86 = f32[5,4,32,256]{3,2,1,0:T(8,128)} custom-call(f32[8,128]{1,0:T(8,128)S(1)} %get-tuple-element.86.y_own, f32[8,128]{1,0:T(8,128)S(1)} %collective-permute-done.14.y_other, f32[50,128]{1,0:T(8,128)S(1)} %get-tuple-element.89.j_ref, f32[17,25,8,128]{3,2,1,0:T(8,128)S(1)} %get-tuple-element.77.q, f32[17,5,8,128]{3,2,1,0:T(8,128)S(1)} %shard_map.85.part, ...), custom_call_target="tpu_custom_call" | custom-call | flops 2000000000 | bytes 6000000 | tf_op jit(solution)/shard_map/pallas_call | solution.py:603
  (4 shorter events, 0.0 us)
Async XLA Ops:
  0.0 11.3 %copy-start = (f32[1,4,5,256]{3,1,2,0:T(4,128)S(1)}, f32[1,4,5,256]{3,1,2,0:T(4,128)}, u32[]{:S(2)}) copy-start(f32[1,4,5,256]{3,1,2,0:T(4,128)} %param.11) | copy-start | bytes 61444
  0.0 11.3 %collective-permute-start = (f32[5,4,256]{2,1,0:T(4,128)}, f32[5,4,256]{2,1,0:T(4,128)S(1)}, u32[]{:S(2)}, u32[]{:S(2)}) collective-permute-start(f32[5,4,256]{2,1,0:T(4,128)} %bitcast.3), channel_id=1, source_target_pairs={{0,24},{1,25},{2,26},{3,27},{4,28},{5,29},{6,30},{7,31},{8,16},{9,... | collective-permute-start | bytes 61448 | tf_op jit(solution)/shard_map/ppermute | solution.py:643
  7.6 14.7 %collective-permute-start.3 = (f32[5,32,256]{2,1,0:T(8,128)S(1)}, f32[5,32,256]{2,1,0:T(8,128)S(1)}, u32[]{:S(2)}, u32[]{:S(2)}) collective-permute-start(f32[5,32,256]{2,1,0:T(8,128)S(1)} %get-tuple-element.57), channel_id=1, source_target_pairs={{32,64},{64,32},{96,128},{128,96},{160,192},{192,160},{33,65},{65,... | collective-permute-start | bytes 491528 | tf_op jit(solution)/shard_map/ppermute | solution.py:623
  11.4 5.0 %collective-permute-start.1 = (f32[5,8,256]{2,1,0:T(8,128)S(1)}, f32[5,8,256]{2,1,0:T(8,128)S(1)}, u32[]{:S(2)}, u32[]{:S(2)}) collective-permute-start(f32[5,8,256]{2,1,0:T(8,128)S(1)} %shard_map.74.low), channel_id=1, source_target_pairs={{0,8},{1,9},{2,10},{3,11},{4,12},{5,13},{6,14},{7,15},{8,0},{9,1},... | collective-permute-start | bytes 122888 | tf_op jit(solution)/shard_map/ppermute | solution.py:643
  16.4 5.9 %collective-permute-start.2 = (f32[5,16,256]{2,1,0:T(8,128)S(1)}, f32[5,16,256]{2,1,0:T(8,128)S(1)}, u32[]{:S(2)}, u32[]{:S(2)}) collective-permute-start(f32[5,16,256]{2,1,0:T(8,128)S(1)} %shard_map.76.low), channel_id=1, source_target_pairs={{0,2},{1,3},{2,0},{3,1},{4,6},{5,7},{6,4},{7,5},{8,10},{9,11},{10,... | collective-permute-start | bytes 245768 | tf_op jit(solution)/shard_map/ppermute | solution.py:643
  19.3 6.9 %collective-permute-start.5 = (f32[5,4,256]{2,1,0:T(4,128)S(1)}, f32[5,4,256]{2,1,0:T(4,128)S(1)}, u32[]{:S(2)}, u32[]{:S(2)}) collective-permute-start(f32[5,4,256]{2,1,0:T(4,128)S(1)} %get-tuple-element.61), channel_id=1, source_target_pairs={{0,1},{1,0},{2,3},{3,2},{4,5},{5,4},{6,7},{7,6},{8,9},{9,8},{10,11... | collective-permute-start | bytes 61448 | tf_op jit(solution)/shard_map/ppermute | solution.py:623
  19.3 6.9 %collective-permute-start.6 = (f32[5,4,256]{2,1,0:T(4,128)S(1)}, f32[5,4,256]{2,1,0:T(4,128)S(1)}, u32[]{:S(2)}, u32[]{:S(2)}) collective-permute-start(f32[5,4,256]{2,1,0:T(4,128)S(1)} %get-tuple-element.63), channel_id=1, source_target_pairs={{1,2},{2,1},{3,4},{4,3},{5,6},{6,5},{7,8},{8,7},{9,10},{10,9},{11,... | collective-permute-start | bytes 61448 | tf_op jit(solution)/shard_map/ppermute | solution.py:623
  22.3 6.4 %collective-permute-start.7 = (f32[5,32,256]{2,1,0:T(8,128)S(1)}, f32[5,32,256]{2,1,0:T(8,128)S(1)}, u32[]{:S(2)}, u32[]{:S(2)}) collective-permute-start(f32[5,32,256]{2,1,0:T(8,128)S(1)} %shard_map.77.low), channel_id=1, source_target_pairs={{0,4},{1,5},{2,6},{3,7},{4,0},{5,1},{6,2},{7,3},{8,12},{9,13},{10,... | collective-permute-start | bytes 491528 | tf_op jit(solution)/shard_map/ppermute | solution.py:643
  23.4 5.3 %collective-permute-start.4 = (f32[5,32,256]{2,1,0:T(8,128)S(1)}, f32[5,32,256]{2,1,0:T(8,128)S(1)}, u32[]{:S(2)}, u32[]{:S(2)}) collective-permute-start(f32[5,32,256]{2,1,0:T(8,128)S(1)} %get-tuple-element.59), channel_id=1, source_target_pairs={{0,32},{32,0},{64,96},{96,64},{128,160},{160,128},{192,224},{224,1... | collective-permute-start | bytes 491528 | tf_op jit(solution)/shard_map/ppermute | solution.py:623
  28.8 1.7 %collective-permute-start.8 = (f32[5,64,256]{2,1,0:T(8,128)S(1)}, f32[5,64,256]{2,1,0:T(8,128)S(1)}, u32[]{:S(2)}, u32[]{:S(2)}) collective-permute-start(f32[5,64,256]{2,1,0:T(8,128)S(1)} %shard_map.79.low), channel_id=1, source_target_pairs={{0,1},{1,0},{2,3},{3,2},{4,5},{5,4},{6,7},{7,6},{8,9},{9,8},{10,11... | collective-permute-start | bytes 983048 | tf_op jit(solution)/shard_map/ppermute | solution.py:643
  31.9 7.7 %collective-permute-start.9 = (f32[32,128]{1,0:T(8,128)S(1)}, f32[32,128]{1,0:T(8,128)S(1)}, u32[]{:S(2)}, u32[]{:S(2)}) collective-permute-start(f32[32,128]{1,0:T(8,128)S(1)} %get-tuple-element.74.joint), channel_id=1, source_target_pairs={{0,16},{1,17},{2,18},{3,19},{4,20},{5,21},{6,22},{7,23},{8,24},{9,... | collective-permute-start | bytes 49160 | tf_op jit(solution)/shard_map/ppermute | solution.py:643
  40.7 11.0 %collective-permute-start.10 = (f32[5,32,256]{2,1,0:T(8,128)S(1)}, f32[5,32,256]{2,1,0:T(8,128)S(1)}, u32[]{:S(2)}, u32[]{:S(2)}) collective-permute-start(f32[5,32,256]{2,1,0:T(8,128)S(1)} %get-tuple-element.82), channel_id=1, source_target_pairs={{0,32},{32,0},{64,96},{96,64},{128,160},{160,128},{192,224},{224,1... | collective-permute-start | bytes 491528 | tf_op jit(solution)/shard_map/ppermute | solution.py:623
  40.8 10.9 %collective-permute-start.11 = (f32[5,32,256]{2,1,0:T(8,128)S(1)}, f32[5,32,256]{2,1,0:T(8,128)S(1)}, u32[]{:S(2)}, u32[]{:S(2)}) collective-permute-start(f32[5,32,256]{2,1,0:T(8,128)S(1)} %get-tuple-element.83), channel_id=1, source_target_pairs={{32,64},{64,32},{96,128},{128,96},{160,192},{192,160},{33,65},{65,... | collective-permute-start | bytes 491528 | tf_op jit(solution)/shard_map/ppermute | solution.py:623
  44.8 6.9 %collective-permute-start.12 = (f32[5,4,256]{2,1,0:T(4,128)S(1)}, f32[5,4,256]{2,1,0:T(4,128)S(1)}, u32[]{:S(2)}, u32[]{:S(2)}) collective-permute-start(f32[5,4,256]{2,1,0:T(4,128)S(1)} %get-tuple-element.84), channel_id=1, source_target_pairs={{1,2},{2,1},{3,4},{4,3},{5,6},{6,5},{7,8},{8,7},{9,10},{10,9},{11,... | collective-permute-start | bytes 61448 | tf_op jit(solution)/shard_map/ppermute | solution.py:623
  46.5 5.3 %collective-permute-start.13 = (f32[5,4,256]{2,1,0:T(4,128)S(1)}, f32[5,4,256]{2,1,0:T(4,128)S(1)}, u32[]{:S(2)}, u32[]{:S(2)}) collective-permute-start(f32[5,4,256]{2,1,0:T(4,128)S(1)} %get-tuple-element.85), channel_id=1, source_target_pairs={{0,1},{1,0},{2,3},{3,2},{4,5},{5,4},{6,7},{7,6},{8,9},{9,8},{10,11... | collective-permute-start | bytes 61448 | tf_op jit(solution)/shard_map/ppermute | solution.py:623
  53.1 7.6 %collective-permute-start.14 = (f32[8,128]{1,0:T(8,128)S(1)}, f32[8,128]{1,0:T(8,128)S(1)}, u32[]{:S(2)}, u32[]{:S(2)}) collective-permute-start(f32[8,128]{1,0:T(8,128)S(1)} %get-tuple-element.86.y_own), channel_id=1, source_target_pairs={{0,16},{1,17},{2,18},{3,19},{4,20},{5,21},{6,22},{7,23},{8,24},{9,... | collective-permute-start | bytes 12296 | tf_op jit(solution)/shard_map/ppermute | solution.py:643

commit v7 on v6

--- a/solution.py
+++ b/solution.py
@@ -708,11 +708,11 @@
         return after(got, done[3])
 
     def sector_halos(rows, got):
-        halo["tb"], halo["ta"] = t_far(after(tb, rows)), t_near(after(ta, rows))
+        halo["za"], halo["tb"] = z_near(after(za, rows)), t_far(after(tb, rows))
         return after(got, halo["zb"])
 
     def factor_rest(rows, got):
-        halo["za"] = z_near(after(za, rows))
+        halo["ta"] = t_near(after(ta, rows))
         m1, sd = done[0], done[3]
         done.extend(
             call(

time: 63.2 us -> 62.8 us (level)
  waiting for transfers between devices: 18.3 us -> 17.6 us
    ppermute x8, waiting for transfers between devices: 6.18 us -> 3.14 us  [swapped_along(): return lax.ppermute(x, axis, pairs)]
    ppermute x7, waiting for transfers between devices: 12.2 us -> 14.5 us  [xor_swap(): lax.ppermute(x, 'az', [(i, i ^ bit) for i in range(lax.axis_size('az'))])]
  transfers between devices with their start and end apart: 15 -> 15, of which waited for: 8 -> 8; matrix products, arithmetic and copies ran while one was open for 0% -> 0% of each run, Pallas kernels for 16% -> 17%
where the time goes in v7:
time: 62.8 us; the launch traced here: 61.5 us
  starting transfers between devices  27.9 us (44%)
  waiting for transfers between devices  17.6 us (28%)
  Pallas kernels  15.7 us (25%)
    ppermute x7, starting transfers between devices, xor_swap(): lax.ppermute(x, 'az', [(i, i ^ bit) for i in range(lax.axis_size('az'))])  16.2 us
    pallas_call x14, Pallas kernels, call(): pl.pallas_call(kernel, out_shape=out_shape, in_specs=[in_spec] * len(inpu...  15.7 us
    ppermute x7, waiting for transfers between devices, xor_swap(): lax.ppermute(x, 'az', [(i, i ^ bit) for i in range(lax.axis_size('az'))])  14.5 us
    ppermute x8, starting transfers between devices, swapped_along(): return lax.ppermute(x, axis, pairs)  11.7 us
    ppermute x8, waiting for transfers between devices, swapped_along(): return lax.ppermute(x, axis, pairs)  3.14 us
  transfers between devices with their start and end apart: 15, of which 8 were waited for; matrix products, arithmetic and copies ran while one was open for 0% of the time, Pallas kernels for 17%

profile of v7, /device:TPU:6, one launch (start us, length us, event | category | flops | bytes accessed | tf_op | source)
XLA Modules:
  0.0 61.5 jit_solution(10305317644580841818)
XLA Ops:
  0.0 0.0 copy-start
  0.0 6.3 %collective-permute-start = (f32[5,4,256]{2,1,0:T(4,128)}, f32[5,4,256]{2,1,0:T(4,128)S(1)}, u32[]{:S(2)}, u32[]{:S(2)}) collective-permute-start(f32[5,4,256]{2,1,0:T(4,128)} %bitcast.3), channel_id=1, source_target_pairs={{0,24},{1,25},{2,26},{3,27},{4,28},{5,29},{6,30},{7,31},{8,16},{9,... | collective-permute-start | bytes 61448 | tf_op jit(solution)/shard_map/ppermute | solution.py:643
  6.3 1.3 %shard_map.73 = (f32[5,4,32,256]{3,2,1,0:T(8,128)S(1)}, f32[4,32,256]{2,1,0:T(8,128)S(1)}, f32[128,256]{1,0:T(8,128)S(1)}, s32[4,32]{1,0:T(4,128)S(1)}, f32[2,25...) custom-call(f32[5,4,32,256]{3,2,1,0:T(8,128)} %flow.1, ...), custom_call_target="tpu_custom_call" | custom-call | flops 1200000000 | bytes 3600000 | tf_op jit(solution)/shard_map/pallas_call | solution.py:603
  7.6 3.8 %collective-permute-start.3 = (f32[5,32,256]{2,1,0:T(8,128)S(1)}, f32[5,32,256]{2,1,0:T(8,128)S(1)}, u32[]{:S(2)}, u32[]{:S(2)}) collective-permute-start(f32[5,32,256]{2,1,0:T(8,128)S(1)} %get-tuple-element.58), channel_id=1, source_target_pairs={{32,64},{64,32},{96,128},{128,96},{160,192},{192,160},{33,65},{65,... | collective-permute-start | bytes 491528 | tf_op jit(solution)/shard_map/ppermute | solution.py:623
  11.3 0.0 collective-permute-done.high
  11.3 0.0 copy-done
  11.4 1.5 %collective-permute-start.1 = (f32[5,8,256]{2,1,0:T(8,128)S(1)}, f32[5,8,256]{2,1,0:T(8,128)S(1)}, u32[]{:S(2)}, u32[]{:S(2)}) collective-permute-start(f32[5,8,256]{2,1,0:T(8,128)S(1)} %shard_map.74.low), channel_id=1, source_target_pairs={{0,8},{1,9},{2,10},{3,11},{4,12},{5,13},{6,14},{7,15},{8,0},{9,1},... | collective-permute-start | bytes 122888 | tf_op jit(solution)/shard_map/ppermute | solution.py:643
  12.9 3.0 %shard_map.75 = (f32[17,75,8,128]{3,2,1,0:T(8,128)S(1)}, f32[8,50,8,128]{3,2,1,0:T(8,128)S(1)}, f32[16,3,8,128]{3,2,1,0:T(8,128)S(1)}, f32[32,128]{1,0:T(8,128)S(1)}, f32[256,128]{1,0:T(8,128)S(1)}) custom-call(f32[4,32,256]{2,1,0:T(8,128)S(1)} %get-tuple-element.53.coef_ref, f32[128,256]{1,0:T(8,128)S(1)} %get-tuple-element.54.mask_ref, ...), custom_call_target="tpu_custom_call" | custom-call | flops 3200000000 | bytes 9600000 | tf_op jit(solution)/shard_map/pallas_call | solution.py:603
  15.9 0.4 collective-permute-done.1.high
  16.4 2.9 %collective-permute-start.4 = (f32[5,16,256]{2,1,0:T(8,128)S(1)}, f32[5,16,256]{2,1,0:T(8,128)S(1)}, u32[]{:S(2)}, u32[]{:S(2)}) collective-permute-start(f32[5,16,256]{2,1,0:T(8,128)S(1)} %shard_map.76.low), channel_id=1, source_target_pairs={{0,2},{1,3},{2,0},{3,1},{4,6},{5,7},{6,4},{7,5},{8,10},{9,11},{10,... | collective-permute-start | bytes 245768 | tf_op jit(solution)/shard_map/ppermute | solution.py:643
  19.3 0.0 collective-permute-start.6
  19.3 0.0 collective-permute-start.2
  19.3 3.0 %collective-permute-done.4.high = f32[5,16,256]{2,1,0:T(8,128)S(1)} collective-permute-done((f32[5,16,256]{2,1,0:T(8,128)S(1)}, f32[5,16,256]{2,1,0:T(8,128)S(1)}, u32[]{:S(2)}, u32[]{:S(2)}) %collective-permute-start.4) | collective-permute-done | bytes 81952 | tf_op jit(solution)/shard_map/ppermute | solution.py:643
  22.3 0.0 collective-permute-done.3.zb
  22.3 1.1 %collective-permute-start.7 = (f32[5,32,256]{2,1,0:T(8,128)S(1)}, f32[5,32,256]{2,1,0:T(8,128)S(1)}, u32[]{:S(2)}, u32[]{:S(2)}) collective-permute-start(f32[5,32,256]{2,1,0:T(8,128)S(1)} %shard_map.77.low), channel_id=1, source_target_pairs={{0,4},{1,5},{2,6},{3,7},{4,0},{5,1},{6,2},{7,3},{8,12},{9,13},{10,... | collective-permute-start | bytes 491528 | tf_op jit(solution)/shard_map/ppermute | solution.py:643
  23.4 0.0 collective-permute-start.5
  23.4 2.7 %shard_map.78 = (f32[11,75,8,128]{3,2,1,0:T(8,128)S(1)}, f32[10,50,8,128]{3,2,1,0:T(8,128)S(1)}, f32[32,128]{1,0:T(8,128)S(1)}) custom-call(f32[17,75,8,128]{3,2,1,0:T(8,128)S(1)} %get-tuple-element.67.m1, f32[32,128]{1,0:T(8,128)S(1)} %get-tuple-element.55.sd_in), custom_call_target="tpu_custom_call" | custom-call | flops 3000000000 | bytes 9000000 | tf_op jit(solution)/shard_map/pallas_call | solution.py:603
  26.1 0.1 collective-permute-done.6.tb
  26.2 0.0 collective-permute-done.5.ta
  26.2 0.0 collective-permute-done.2.za
  26.2 1.5 %collective-permute-done.7.high = f32[5,32,256]{2,1,0:T(8,128)S(1)} collective-permute-done((f32[5,32,256]{2,1,0:T(8,128)S(1)}, f32[5,32,256]{2,1,0:T(8,128)S(1)}, u32[]{:S(2)}, u32[]{:S(2)}) %collective-permute-start.7) | collective-permute-done | bytes 163872 | tf_op jit(solution)/shard_map/ppermute | solution.py:643
  27.8 0.1 collective-permute-start.8
  27.9 0.6 shard_map.80.rhs_in
  28.4 1.0 %collective-permute-done.8.high = f32[5,64,256]{2,1,0:T(8,128)S(1)} collective-permute-done((f32[5,64,256]{2,1,0:T(8,128)S(1)}, f32[5,64,256]{2,1,0:T(8,128)S(1)}, u32[]{:S(2)}, u32[]{:S(2)}) %collective-permute-start.8) | collective-permute-done | bytes 327712 | tf_op jit(solution)/shard_map/ppermute | solution.py:643
  29.5 1.4 %shard_map.81 = (f32[20,5,8,128]{3,2,1,0:T(8,128)S(1)}, f32[16,5,8,128]{3,2,1,0:T(8,128)S(1)}, f32[32,128]{1,0:T(8,128)S(1)}) custom-call(f32[5,256,128]{2,1,0:T(8,128)S(1)} %shard_map.80.rhs_in, f32[256,128]{1,0:T(8,128)S(1)} %get-tuple-element.64.mask_t, s32[4,32]{1,0:T(4,128)S(1)} %get-tuple-element.65.place, ...), custom_call_target="tpu_custom_call" | custom-call | flops 1200000000 | bytes 3600000 | tf_op jit(solution)/shard_map/pallas_call | solution.py:603
  30.9 2.0 %collective-permute-start.9 = (f32[32,128]{1,0:T(8,128)S(1)}, f32[32,128]{1,0:T(8,128)S(1)}, u32[]{:S(2)}, u32[]{:S(2)}) collective-permute-start(f32[32,128]{1,0:T(8,128)S(1)} %get-tuple-element.74.joint), channel_id=1, source_target_pairs={{0,16},{1,17},{2,18},{3,19},{4,20},{5,21},{6,22},{7,23},{8,24},{9,... | collective-permute-start | bytes 49160 | tf_op jit(solution)/shard_map/ppermute | solution.py:643
  32.9 2.2 %shard_map.82 = (f32[17,25,8,128]{3,2,1,0:T(8,128)S(1)}, f32[17,5,8,128]{3,2,1,0:T(8,128)S(1)}) custom-call(f32[17,75,8,128]{3,2,1,0:T(8,128)S(1)} %get-tuple-element.67.m1, f32[11,75,8,128]{3,2,1,0:T(8,128)S(1)} %get-tuple-element.75.m2, f32[20,5,8,128]{3,2,1,0:T(8,128)S(1)} %get-tuple-element.76.e_ref), custom_call_target="tpu_custom_call" | custom-call | flops 3000000000 | bytes 9000000 | tf_op jit(solution)/shard_map/pallas_call | solution.py:603
  35.1 3.5 %collective-permute-done.9.other_joint = f32[32,128]{1,0:T(8,128)S(1)} collective-permute-done((f32[32,128]{1,0:T(8,128)S(1)}, f32[32,128]{1,0:T(8,128)S(1)}, u32[]{:S(2)}, u32[]{:S(2)}) %collective-permute-start.9) | collective-permute-done | bytes 16416 | tf_op jit(solution)/shard_map/ppermute | solution.py:643
  38.6 1.1 %shard_map.83 = (f32[5,4,32,256]{3,2,1,0:T(8,128)S(1)}, f32[5,32,256]{2,1,0:T(8,128)S(1)}, f32[5,32,256]{2,1,0:T(8,128)S(1)}, f32[5,4,256]{2,1,0:T(4,128)S(1)}, ...) custom-call(f32[32,128]{1,0:T(8,128)S(1)} %get-tuple-element.74.joint, f32[32,128]{1,0:T(8,128)S(1)} %collective-permute-done.9.other_joint, ...), custom_call_target="tpu_custom_call" | custom-call | flops 1300000000 | bytes 3900000 | tf_op jit(solution)/shard_map/pallas_call | solution.py:603
  39.7 0.3 collective-permute-start.10
  40.0 3.8 %collective-permute-start.11 = (f32[5,32,256]{2,1,0:T(8,128)S(1)}, f32[5,32,256]{2,1,0:T(8,128)S(1)}, u32[]{:S(2)}, u32[]{:S(2)}) collective-permute-start(f32[5,32,256]{2,1,0:T(8,128)S(1)} %get-tuple-element.83), channel_id=1, source_target_pairs={{32,64},{64,32},{96,128},{128,96},{160,192},{192,160},{33,65},{65,... | collective-permute-start | bytes 491528 | tf_op jit(solution)/shard_map/ppermute | solution.py:623
  43.8 2.6 %collective-permute-start.12 = (f32[5,4,256]{2,1,0:T(4,128)S(1)}, f32[5,4,256]{2,1,0:T(4,128)S(1)}, u32[]{:S(2)}, u32[]{:S(2)}) collective-permute-start(f32[5,4,256]{2,1,0:T(4,128)S(1)} %get-tuple-element.84), channel_id=1, source_target_pairs={{1,2},{2,1},{3,4},{4,3},{5,6},{6,5},{7,8},{8,7},{9,10},{10,9},{11,... | collective-permute-start | bytes 61448 | tf_op jit(solution)/shard_map/ppermute | solution.py:623
  46.4 1.2 %collective-permute-start.13 = (f32[5,4,256]{2,1,0:T(4,128)S(1)}, f32[5,4,256]{2,1,0:T(4,128)S(1)}, u32[]{:S(2)}, u32[]{:S(2)}) collective-permute-start(f32[5,4,256]{2,1,0:T(4,128)S(1)} %get-tuple-element.85), channel_id=1, source_target_pairs={{0,1},{1,0},{2,3},{3,2},{4,5},{5,4},{6,7},{7,6},{8,9},{9,8},{10,11... | collective-permute-start | bytes 61448 | tf_op jit(solution)/shard_map/ppermute | solution.py:623
  47.7 3.1 %collective-permute-done.12.tb = f32[5,4,256]{2,1,0:T(4,128)S(1)} collective-permute-done((f32[5,4,256]{2,1,0:T(4,128)S(1)}, f32[5,4,256]{2,1,0:T(4,128)S(1)}, u32[]{:S(2)}, u32[]{:S(2)}) %collective-permute-start.12) | collective-permute-done | bytes 20512 | tf_op jit(solution)/shard_map/ppermute | solution.py:623
  50.7 0.0 collective-permute-done.13.ta
  50.7 0.0 collective-permute-done.10.za
  50.7 0.0 collective-permute-done.11.zb
  50.7 1.4 %shard_map.84 = (f32[20,5,8,128]{3,2,1,0:T(8,128)S(1)}, f32[16,5,8,128]{3,2,1,0:T(8,128)S(1)}, f32[8,128]{1,0:T(8,128)S(1)}) custom-call(f32[5,4,32,256]{3,2,1,0:T(8,128)S(1)} %get-tuple-element.81.u.first, f32[5,32,256]{2,1,0:T(8,128)S(1)} %collective-permute-done.10.za, f32[5,32,256]{2,1,0:T(8,128)S(1)} %collective-permute-done.11.zb, ...), custom_call_target="tpu_custom_call" | custom-call | flops 1300000000 | bytes 3900000 | tf_op jit(solution)/shard_map/pallas_call | solution.py:603
  52.1 2.2 %collective-permute-start.14 = (f32[8,128]{1,0:T(8,128)S(1)}, f32[8,128]{1,0:T(8,128)S(1)}, u32[]{:S(2)}, u32[]{:S(2)}) collective-permute-start(f32[8,128]{1,0:T(8,128)S(1)} %get-tuple-element.86.y_own), channel_id=1, source_target_pairs={{0,16},{1,17},{2,18},{3,19},{4,20},{5,21},{6,22},{7,23},{8,24},{9,... | collective-permute-start | bytes 12296 | tf_op jit(solution)/shard_map/ppermute | solution.py:643
  54.3 0.4 shard_map.85.part
  54.7 5.0 %collective-permute-done.14.y_other = f32[8,128]{1,0:T(8,128)S(1)} collective-permute-done((f32[8,128]{1,0:T(8,128)S(1)}, f32[8,128]{1,0:T(8,128)S(1)}, u32[]{:S(2)}, u32[]{:S(2)}) %collective-permute-start.14) | collective-permute-done | bytes 4128 | tf_op jit(solution)/shard_map/ppermute | solution.py:643
  59.7 1.7 %shard_map.86 = f32[5,4,32,256]{3,2,1,0:T(8,128)} custom-call(f32[8,128]{1,0:T(8,128)S(1)} %get-tuple-element.86.y_own, f32[8,128]{1,0:T(8,128)S(1)} %collective-permute-done.14.y_other, f32[50,128]{1,0:T(8,128)S(1)} %get-tuple-element.89.j_ref, f32[17,25,8,128]{3,2,1,0:T(8,128)S(1)} %get-tuple-element.77.q, f32[17,5,8,128]{3,2,1,0:T(8,128)S(1)} %shard_map.85.part, ...), custom_call_target="tpu_custom_call" | custom-call | flops 2000000000 | bytes 6000000 | tf_op jit(solution)/shard_map/pallas_call | solution.py:603
  (4 shorter events, 0.0 us)
Async XLA Ops:
  0.0 11.3 %copy-start = (f32[1,4,5,256]{3,1,2,0:T(4,128)S(1)}, f32[1,4,5,256]{3,1,2,0:T(4,128)}, u32[]{:S(2)}) copy-start(f32[1,4,5,256]{3,1,2,0:T(4,128)} %param.11) | copy-start | bytes 61444
  0.0 11.3 %collective-permute-start = (f32[5,4,256]{2,1,0:T(4,128)}, f32[5,4,256]{2,1,0:T(4,128)S(1)}, u32[]{:S(2)}, u32[]{:S(2)}) collective-permute-start(f32[5,4,256]{2,1,0:T(4,128)} %bitcast.3), channel_id=1, source_target_pairs={{0,24},{1,25},{2,26},{3,27},{4,28},{5,29},{6,30},{7,31},{8,16},{9,... | collective-permute-start | bytes 61448 | tf_op jit(solution)/shard_map/ppermute | solution.py:643
  7.6 14.7 %collective-permute-start.3 = (f32[5,32,256]{2,1,0:T(8,128)S(1)}, f32[5,32,256]{2,1,0:T(8,128)S(1)}, u32[]{:S(2)}, u32[]{:S(2)}) collective-permute-start(f32[5,32,256]{2,1,0:T(8,128)S(1)} %get-tuple-element.58), channel_id=1, source_target_pairs={{32,64},{64,32},{96,128},{128,96},{160,192},{192,160},{33,65},{65,... | collective-permute-start | bytes 491528 | tf_op jit(solution)/shard_map/ppermute | solution.py:623
  11.4 5.0 %collective-permute-start.1 = (f32[5,8,256]{2,1,0:T(8,128)S(1)}, f32[5,8,256]{2,1,0:T(8,128)S(1)}, u32[]{:S(2)}, u32[]{:S(2)}) collective-permute-start(f32[5,8,256]{2,1,0:T(8,128)S(1)} %shard_map.74.low), channel_id=1, source_target_pairs={{0,8},{1,9},{2,10},{3,11},{4,12},{5,13},{6,14},{7,15},{8,0},{9,1},... | collective-permute-start | bytes 122888 | tf_op jit(solution)/shard_map/ppermute | solution.py:643
  16.4 5.9 %collective-permute-start.4 = (f32[5,16,256]{2,1,0:T(8,128)S(1)}, f32[5,16,256]{2,1,0:T(8,128)S(1)}, u32[]{:S(2)}, u32[]{:S(2)}) collective-permute-start(f32[5,16,256]{2,1,0:T(8,128)S(1)} %shard_map.76.low), channel_id=1, source_target_pairs={{0,2},{1,3},{2,0},{3,1},{4,6},{5,7},{6,4},{7,5},{8,10},{9,11},{10,... | collective-permute-start | bytes 245768 | tf_op jit(solution)/shard_map/ppermute | solution.py:643
  19.3 6.9 %collective-permute-start.6 = (f32[5,4,256]{2,1,0:T(4,128)S(1)}, f32[5,4,256]{2,1,0:T(4,128)S(1)}, u32[]{:S(2)}, u32[]{:S(2)}) collective-permute-start(f32[5,4,256]{2,1,0:T(4,128)S(1)} %get-tuple-element.63), channel_id=1, source_target_pairs={{1,2},{2,1},{3,4},{4,3},{5,6},{6,5},{7,8},{8,7},{9,10},{10,9},{11,... | collective-permute-start | bytes 61448 | tf_op jit(solution)/shard_map/ppermute | solution.py:623
  19.3 6.9 %collective-permute-start.2 = (f32[5,32,256]{2,1,0:T(8,128)S(1)}, f32[5,32,256]{2,1,0:T(8,128)S(1)}, u32[]{:S(2)}, u32[]{:S(2)}) collective-permute-start(f32[5,32,256]{2,1,0:T(8,128)S(1)} %get-tuple-element.57), channel_id=1, source_target_pairs={{0,32},{32,0},{64,96},{96,64},{128,160},{160,128},{192,224},{224,1... | collective-permute-start | bytes 491528 | tf_op jit(solution)/shard_map/ppermute | solution.py:623
  22.3 5.4 %collective-permute-start.7 = (f32[5,32,256]{2,1,0:T(8,128)S(1)}, f32[5,32,256]{2,1,0:T(8,128)S(1)}, u32[]{:S(2)}, u32[]{:S(2)}) collective-permute-start(f32[5,32,256]{2,1,0:T(8,128)S(1)} %shard_map.77.low), channel_id=1, source_target_pairs={{0,4},{1,5},{2,6},{3,7},{4,0},{5,1},{6,2},{7,3},{8,12},{9,13},{10,... | collective-permute-start | bytes 491528 | tf_op jit(solution)/shard_map/ppermute | solution.py:643
  23.4 2.8 %collective-permute-start.5 = (f32[5,4,256]{2,1,0:T(4,128)S(1)}, f32[5,4,256]{2,1,0:T(4,128)S(1)}, u32[]{:S(2)}, u32[]{:S(2)}) collective-permute-start(f32[5,4,256]{2,1,0:T(4,128)S(1)} %get-tuple-element.61), channel_id=1, source_target_pairs={{0,1},{1,0},{2,3},{3,2},{4,5},{5,4},{6,7},{7,6},{8,9},{9,8},{10,11... | collective-permute-start | bytes 61448 | tf_op jit(solution)/shard_map/ppermute | solution.py:623
  27.8 1.7 %collective-permute-start.8 = (f32[5,64,256]{2,1,0:T(8,128)S(1)}, f32[5,64,256]{2,1,0:T(8,128)S(1)}, u32[]{:S(2)}, u32[]{:S(2)}) collective-permute-start(f32[5,64,256]{2,1,0:T(8,128)S(1)} %shard_map.79.low), channel_id=1, source_target_pairs={{0,1},{1,0},{2,3},{3,2},{4,5},{5,4},{6,7},{7,6},{8,9},{9,8},{10,11... | collective-permute-start | bytes 983048 | tf_op jit(solution)/shard_map/ppermute | solution.py:643
  30.9 7.7 %collective-permute-start.9 = (f32[32,128]{1,0:T(8,128)S(1)}, f32[32,128]{1,0:T(8,128)S(1)}, u32[]{:S(2)}, u32[]{:S(2)}) collective-permute-start(f32[32,128]{1,0:T(8,128)S(1)} %get-tuple-element.74.joint), channel_id=1, source_target_pairs={{0,16},{1,17},{2,18},{3,19},{4,20},{5,21},{6,22},{7,23},{8,24},{9,... | collective-permute-start | bytes 49160 | tf_op jit(solution)/shard_map/ppermute | solution.py:643
  39.7 11.0 %collective-permute-start.10 = (f32[5,32,256]{2,1,0:T(8,128)S(1)}, f32[5,32,256]{2,1,0:T(8,128)S(1)}, u32[]{:S(2)}, u32[]{:S(2)}) collective-permute-start(f32[5,32,256]{2,1,0:T(8,128)S(1)} %get-tuple-element.82), channel_id=1, source_target_pairs={{0,32},{32,0},{64,96},{96,64},{128,160},{160,128},{192,224},{224,1... | collective-permute-start | bytes 491528 | tf_op jit(solution)/shard_map/ppermute | solution.py:623
  40.0 10.7 %collective-permute-start.11 = (f32[5,32,256]{2,1,0:T(8,128)S(1)}, f32[5,32,256]{2,1,0:T(8,128)S(1)}, u32[]{:S(2)}, u32[]{:S(2)}) collective-permute-start(f32[5,32,256]{2,1,0:T(8,128)S(1)} %get-tuple-element.83), channel_id=1, source_target_pairs={{32,64},{64,32},{96,128},{128,96},{160,192},{192,160},{33,65},{65,... | collective-permute-start | bytes 491528 | tf_op jit(solution)/shard_map/ppermute | solution.py:623
  43.8 6.9 %collective-permute-start.12 = (f32[5,4,256]{2,1,0:T(4,128)S(1)}, f32[5,4,256]{2,1,0:T(4,128)S(1)}, u32[]{:S(2)}, u32[]{:S(2)}) collective-permute-start(f32[5,4,256]{2,1,0:T(4,128)S(1)} %get-tuple-element.84), channel_id=1, source_target_pairs={{1,2},{2,1},{3,4},{4,3},{5,6},{6,5},{7,8},{8,7},{9,10},{10,9},{11,... | collective-permute-start | bytes 61448 | tf_op jit(solution)/shard_map/ppermute | solution.py:623
  46.4 4.3 %collective-permute-start.13 = (f32[5,4,256]{2,1,0:T(4,128)S(1)}, f32[5,4,256]{2,1,0:T(4,128)S(1)}, u32[]{:S(2)}, u32[]{:S(2)}) collective-permute-start(f32[5,4,256]{2,1,0:T(4,128)S(1)} %get-tuple-element.85), channel_id=1, source_target_pairs={{0,1},{1,0},{2,3},{3,2},{4,5},{5,4},{6,7},{7,6},{8,9},{9,8},{10,11... | collective-permute-start | bytes 61448 | tf_op jit(solution)/shard_map/ppermute | solution.py:623
  52.1 7.6 %collective-permute-start.14 = (f32[8,128]{1,0:T(8,128)S(1)}, f32[8,128]{1,0:T(8,128)S(1)}, u32[]{:S(2)}, u32[]{:S(2)}) collective-permute-start(f32[8,128]{1,0:T(8,128)S(1)} %get-tuple-element.86.y_own), channel_id=1, source_target_pairs={{0,16},{1,17},{2,18},{3,19},{4,20},{5,21},{6,22},{7,23},{8,24},{9,... | collective-permute-start | bytes 12296 | tf_op jit(solution)/shard_map/ppermute | solution.py:643
